TPU v7x, 32 devices: a whole 2x2x4 slice. The times are simulated.
32 devices in a mesh: prow: 2 (over core), pcol: 16 (over z, y, x).
Axes of the slice: x: 2, y: 2, z: 4, core: 2. Of those that a mesh axis runs over, the one named last changes fastest.
Arguments:
- factor_rows: float32 [8, 256, 24, 2048], P(None, 'prow', None, 'pcol'), as said below
- sensitivity: float32 [1024, 24, 2048], P('prow', None, 'pcol'), may hold values from -6 to 6
- pivots: int32 [2048], replicated, may hold values from 0 to 2047, as said below
Outputs:
- adjoint: float32 [1024, 8, 256], P(None, None, 'prow')
- updated: float32 [1024, 24, 2048], P('prow', None, 'pcol')
Inputs may be any that keep to these rules, and one draw needn't show every extreme that they name: pivots is a permutation of the first 2048 columns. `factor_rows`: in M, the entries left of each block row's diagonal block are zero and each diagonal block is lower triangular.
All inputs are finite; a program needn't handle non-finite values.
Results may differ from a plain program's by a relative error of at most 0.0001.
Values sent between devices are 32-bit elements; how exact they have to be, the bound alone decides.
No kernel may reach another device: no remote copies, remote signals or barrier semaphores. Data moves between devices by JAX's collectives and lax.ppermute only.
A program may use at most 192 MiB of HBM per device.

v0:
```python
import jax
import jax.numpy as jnp
from jax import lax
from jax.sharding import PartitionSpec as P

NB = 1024


def shards(factor_rows, sensitivity, pivots):
    pcol_count = lax.axis_size("pcol")
    row_cycles = factor_rows.shape[0]
    half_cycles = row_cycles // 2
    tile_width = factor_rows.shape[1]
    col_tiles = factor_rows.shape[2]
    local_rhs = sensitivity.shape[0]
    per_block = NB // tile_width
    pcol_index = lax.axis_index("pcol")
    tile_ids = jnp.arange(col_tiles) * pcol_count + pcol_index
    stripe_cols = pcol_count * tile_width
    gathered = lax.all_gather(sensitivity[:, :1, :], "pcol", axis=2, tiled=True)
    flat_cols = gathered.reshape(local_rhs, stripe_cols)
    swapped = jnp.take(flat_cols, pivots, axis=1)
    merged = swapped.reshape(local_rhs, 1, pcol_count, tile_width)
    own_tiles = lax.dynamic_index_in_dim(merged, pcol_index, 2, keepdims=False)
    working = jnp.concatenate([own_tiles, sensitivity[:, 1:, :]], axis=1)

    def tile_range(section):
        return (
            section * per_block // pcol_count,
            ((section + 1) * per_block - 1) // pcol_count + 1,
        )

    def solve_block(working, section):
        low_tile, high_tile = tile_range(section)
        chosen = tile_ids[low_tile:high_tile]
        inside = ((chosen >= section * per_block) & (chosen < (section + 1) * per_block)).astype(
            jnp.float32
        )
        masked = working[:, low_tile:high_tile, :] * inside[None, :, None]
        all_rhs = lax.all_gather(masked, "prow", axis=0, tiled=True)
        inverse_tiles = factor_rows[
            section * half_cycles : (section + 1) * half_cycles, :, low_tile:high_tile, :
        ]
        partial_sum = jnp.einsum(
            "hbu,atbu->hat",
            all_rhs,
            inverse_tiles,
            precision=lax.Precision.HIGHEST,
            preferred_element_type=jnp.float32,
        )
        partial_sum = partial_sum.reshape(all_rhs.shape[0], half_cycles * tile_width)
        return lax.psum(partial_sum, "pcol")

    solved_first = solve_block(working, 0)
    low_tile, high_tile = tile_range(1)
    next_tiles = high_tile - low_tile
    first_rows = factor_rows[:half_cycles, :, low_tile:high_tile, :].reshape(
        half_cycles * tile_width, next_tiles * tile_width
    )
    picked = solved_first
    early = lax.psum_scatter(
        jnp.dot(
            picked, first_rows, precision=lax.Precision.HIGHEST, preferred_element_type=jnp.float32
        ),
        "prow",
        scatter_dimension=0,
        tiled=True,
    ).reshape(local_rhs, next_tiles, tile_width)
    chosen = tile_ids[low_tile:high_tile]
    inside = ((chosen >= per_block) & (chosen < 2 * per_block)).astype(jnp.float32)
    working = working.at[:, low_tile:high_tile, :].add(-early * inside[None, :, None])
    solved_second = solve_block(working, 1)
    both_solved = jnp.concatenate([solved_first, solved_second], axis=1)
    all_rows = factor_rows.reshape(row_cycles * tile_width, col_tiles * tile_width)
    picked = both_solved
    change = lax.psum_scatter(
        jnp.dot(
            picked, all_rows, precision=lax.Precision.HIGHEST, preferred_element_type=jnp.float32
        ),
        "prow",
        scatter_dimension=0,
        tiled=True,
    ).reshape(local_rhs, col_tiles, tile_width)
    keep_cols = (tile_ids >= 2 * per_block).astype(jnp.float32)
    working = working - change * keep_cols[None, :, None]
    adjoint = jnp.concatenate([solved_first, solved_second], axis=1).reshape(
        solved_first.shape[0], row_cycles, tile_width
    )
    return (adjoint, working)


def solution(mesh):
    return jax.shard_map(
        shards,
        mesh=mesh,
        in_specs=(P(None, "prow", None, "pcol"), P("prow", None, "pcol"), P()),
        out_specs=(P(None, None, "prow"), P("prow", None, "pcol")),
        check_vma=False,
    )
```

profile of v0, /device:TPU:0, one launch (start us, length us, event | category | flops | bytes accessed | tf_op | source)
XLA Modules:
  0.0 478.7 jit_solution(9994754397476234976)
XLA Ops:
  7.2 0.0 all-gather.3.cloned.1.call-start
  7.2 1.7 slice.41
  8.9 0.8 copy.11
  9.8 0.0 all-gather.3.cloned.1.call-update
  9.8 0.0 all-reduce.3.cloned.1.call-start
  9.9 0.7 and_bitcast_fusion
  10.7 0.7 fusion.4
  11.4 2.5 fusion.5
  13.9 76.2 %all-gather.3.cloned.1.call-done = f32[512,1,2048]{0,2,1:T(8,128)} async-done(((f32[512,1,128]{0,2,1:T(8,128)}), f32[512,1,2048]{0,2,1:T(8,128)}) %all-gather.3.cloned.1.call-update) | async-done | bytes 4194320 | tf_op jit(solution)/shard_map/all_gather | solution.py:20
  90.2 11.7 %gather_fusion = f32[2048,512]{1,0:T(8,128)} fusion(f32[512,2048]{0,1:T(8,128)} %bitcast.40, s32[2048]{0:T(1024)S(1)} %fusion.4), kind=kCustom, calls=%fused_computation | custom fusion | bytes 8396800 | tf_op jit(solution)/shard_map/jit(_take)/gather | solution.py:22
  101.8 1.0 constant_dynamic-slice_fusion.1
  102.8 0.1 copy.12
  103.0 2.2 all_gather.10
  105.2 3.1 fusion.6
  108.3 0.0 all-reduce.3.cloned.1.call-update
  108.3 0.0 reduce-scatter.3.cloned.1.call-start
  108.4 124.7 %all-reduce.3.cloned.1.call-done = f32[1024,512]{1,0:T(8,128)} async-done(((f32[1024,512]{1,0:T(8,128)}), f32[1024,512]{1,0:T(8,128)}) %all-reduce.3.cloned.1.call-update) | async-done | bytes 2097168 | tf_op jit(solution)/shard_map/psum | solution.py:52
  233.0 4.2 fusion.7
  237.2 0.0 copy-start
  237.2 0.0 reduce-scatter.3.cloned.1.call-update
  237.2 0.0 all-reduce.5.cloned.1.call-start
  237.4 7.3 %reduce-scatter.3.cloned.1.call-done = f32[512,128]{1,0:T(8,128)} async-done(((f32[1024,128]{1,0:T(8,128)}), f32[512,128]{1,0:T(8,128)}) %reduce-scatter.3.cloned.1.call-update) | async-done | bytes 262160 | tf_op jit(solution)/shard_map/reduce_scatter | solution.py:61
  244.7 1.0 broadcast_multiply_fusion
  245.7 2.2 all-gather
  247.9 3.1 fusion.8
  251.0 0.0 all-reduce.5.cloned.1.call-update
  251.0 0.2 reduce-scatter.5.cloned.1.call-start
  251.2 0.0 copy-done
  251.2 1.6 constant_dynamic-update-slice_fusion.1
  252.8 125.4 %all-reduce.5.cloned.1.call-done = f32[1024,512]{1,0:T(8,128)} async-done(((f32[1024,512]{1,0:T(8,128)}), f32[1024,512]{1,0:T(8,128)}) %all-reduce.5.cloned.1.call-update) | async-done | bytes 2097168 | tf_op jit(solution)/shard_map/psum | solution.py:52
  378.3 3.2 constant_dynamic-update-slice_fusion
  381.4 60.8 %fusion = f32[1024,3072]{1,0:T(8,128)} fusion(f32[1024,1024]{1,0:T(8,128)} %constant_dynamic-update-slice_fusion, f32[128,8,24,128]{3,2,1,0:T(8,128)} %bitcast.55), kind=kOutput, calls=%fused_computation.1 | convolution fusion | flops 38654705664 | bytes 29360128 | tf_op jit(solution)/shard_map/dot_general | solution.py:77
  442.2 0.0 reduce-scatter.5.cloned.1.call-update
  442.2 3.4 slice.45
  445.6 4.0 pad_maximum_fusion
  449.6 8.2 %scatter-add.4 = f32[512,24,128]{2,1,0:T(8,128)} dynamic-update-slice(f32[512,24,128]{2,1,0:T(8,128)} %pad_maximum_fusion, f32[512,1,128]{2,1,0:T(1,128)S(1)} %bitcast.52, s32[]{:T(128)} %constant.48.clone.1, s32[]{:T(128)} %constant.48.clone.1, s32[]{:T(128)} %constant.48.clone.1) | dynamic-update-slice | bytes 524292 | tf_op jit(solution)/shard_map/scatter-add | solution.py:71
  457.8 6.1 %copy.13 = f32[128,8,8,128]{3,2,1,0:T(8,128)} copy(f32[128,8,8,128]{3,1,2,0:T(8,128)} %bitcast.43) | data formatting | bytes 8388608
  464.0 0.0 reduce-scatter.5.cloned.1.call-done
  464.0 0.0 slice-start
  464.0 0.0 slice-start.1
  464.0 4.3 copy.15
  468.3 0.0 slice-done
  468.3 0.3 slice-done.1
  468.6 3.6 fusion.3
  (6 shorter events, 0.1 us)
Async XLA Ops:
  7.2 83.0 %all-gather.3.cloned.1.call-start = ((), (), s32[]{:S(2)}) async-start(), calls=%async_computation.2 | async-start | bytes 4456448 | tf_op jit(solution)/shard_map/all_gather | solution.py:20
  9.8 223.2 %all-reduce.3.cloned.1.call-start = ((), (), s32[]{:S(2)}) async-start(), calls=%async_computation.3 | async-start | bytes 4194304 | tf_op jit(solution)/shard_map/psum | solution.py:52
  108.3 136.4 %reduce-scatter.3.cloned.1.call-start = ((), (), s32[]{:S(2)}) async-start(), calls=%async_computation.4 | async-start | bytes 786432 | tf_op jit(solution)/shard_map/reduce_scatter | solution.py:61
  237.2 14.0 %copy-start = (f32[1024,512]{1,0:T(8,128)S(1)}, f32[1024,512]{1,0:T(8,128)}, u32[]{:S(2)}) copy-start(f32[1024,512]{1,0:T(8,128)} %all-reduce.3.cloned.1.call-done) | copy-start | bytes 6291460
  237.2 141.0 %all-reduce.5.cloned.1.call-start = ((), (), s32[]{:S(2)}) async-start(), calls=%async_computation.5 | async-start | bytes 4194304 | tf_op jit(solution)/shard_map/psum | solution.py:52
  251.0 213.0 %reduce-scatter.5.cloned.1.call-start = ((), (), s32[]{:S(2)}) async-start(), calls=%async_computation.6 | async-start | bytes 18874368 | tf_op jit(solution)/shard_map/reduce_scatter | solution.py:76
  464.0 4.4 slice-start
  464.0 4.7 slice-start.1
Sparse Core Ops, SparseCore 0:
  11.3 78.7 all-gather.2
  108.4 124.5 all-reduce.2
  237.4 7.2 reduce-scatter.2
  251.1 127.1 all-reduce.4
  442.4 20.8 reduce-scatter.4
where the time goes:
time: 479 us
  waiting for transfers between devices  334 us (70%)
  matrix products  71.2 us (15%)
  local copies, waits for them, and re-layouts  45.1 us (9%)
  between operations  14 us (3%)
  other arithmetic  9.97 us (2%)
    psum x2, waiting for transfers between devices, solve_block(): return lax.psum(partial_sum, 'pcol')  250 us
    all_gather x1, waiting for transfers between devices, shards(): gathered = lax.all_gather(sensitivity[:, :1, :], 'pcol', axis=2, tiled=True)  76.2 us
    dot_general x1, matrix products, shards(): jnp.dot(picked, all_rows, precision=lax.Precision.HIGHEST, preferred_elem...  60.8 us
    unnamed x11, local copies, waits for them, and re-layouts  13.4 us
    gather x1, local copies, waits for them, and re-layouts, shards(): swapped = jnp.take(flat_cols, pivots, axis=1)  11.7 us
  transfers between devices with their start and end apart: 5, of which 4 were waited for; matrix products, arithmetic and copies ran while one was open for 6% of the time, Pallas kernels for 0%

commit v1 on v0

v1 whole, which is shorter than its diff:
```python
import functools

import jax
import jax.numpy as jnp
from jax import lax
from jax.experimental import pallas as pl
from jax.experimental.pallas import tpu as pltpu
from jax.sharding import PartitionSpec as P

NB = 1024
F32 = jnp.float32
BF16 = jnp.bfloat16
VMEM_BYTES = 60 * 1024 * 1024


def grid_of(count):
    z_size = 4
    side = 1
    while side * side * z_size < count:
        side += 1
    return z_size, side, side


def split(value):
    high = value.astype(BF16)
    return high, (value - high.astype(F32)).astype(BF16)


def mul3(left, right, dims):
    dot = functools.partial(lax.dot_general, dimension_numbers=(dims, ((), ())), preferred_element_type=F32)
    return dot(left[0], right[0]) + (dot(left[0], right[1]) + dot(left[1], right[0]))


NN = ((1,), (0,))
NT = ((1,), (1,))


def shift(value, sizes, axis, step):
    z_size, y_size, x_size = sizes
    pairs = []
    for z in range(z_size):
        for y in range(y_size):
            for x in range(x_size):
                at = [z, y, x]
                to = list(at)
                to[axis] = (at[axis] + step) % sizes[axis]
                pairs.append(tuple((c[0] * y_size + c[1]) * x_size + c[2] for c in (at, to)))
    return lax.ppermute(value, "pcol", pairs)


def ring(value, sizes, axis):
    held = [value]
    for _ in range(sizes[axis] - 1):
        held.append(shift(held[-1], sizes, axis, 1))
    return held


def gather_pieces(block, sizes):
    half = block.shape[0] // 2
    pieces = []
    for dz, held in enumerate(ring(block, sizes, 0)):
        for dx, first in enumerate(ring(held[:half], sizes, 2)):
            for dy, second in enumerate(ring(first, sizes, 1)):
                pieces.append((0, (dz, dy, dx), second))
        for dy, first in enumerate(ring(held[half:], sizes, 1)):
            for dx, second in enumerate(ring(first, sizes, 2)):
                pieces.append((half, (dz, dy, dx), second))
    return pieces


def source_tiles(sizes, index):
    z_size, y_size, x_size = sizes
    z, y, x = index // (y_size * x_size), index // x_size % y_size, index % x_size
    places = jnp.arange(z_size * y_size * x_size)
    dz, dy, dx = places // (y_size * x_size), places // x_size % y_size, places % x_size
    return ((z - dz) % z_size * y_size + (y - dy) % y_size) * x_size + (x - dx) % x_size


def slot_of(place, sizes):
    return (place[0] * sizes[1] + place[1]) * sizes[2] + place[2]


def permute_columns(pieces, sizes, tiles, wanted, rows):
    count = sizes[0] * sizes[1] * sizes[2]
    width = wanted.shape[0]
    step = 256
    where = [(first, slot_of(place, sizes)) for first, place, _ in pieces]

    def kernel(tiles_ref, wanted_ref, *refs):
        parts, out_ref, high_ref, low_ref, hot_ref = refs[:-4], refs[-4], refs[-3], refs[-2], refs[-1]
        for (first, slot), part in zip(where, parts, strict=True):
            high, low = split(part[...])
            to = (pl.ds(first, part.shape[0]), pl.ds(slot * 128, 128))
            high_ref[to] = high
            low_ref[to] = low
        for start in range(0, width, step):
            size = min(step, width - start)
            columns = wanted_ref[:, pl.ds(start, size)]
            lane = lax.broadcasted_iota(jnp.int32, (128, size), 0)
            for slot in range(count):
                hot = (columns - tiles_ref[slot] * 128) == lane
                hot_ref[pl.ds(slot * 128, 128), pl.ds(0, size)] = hot.astype(F32).astype(BF16)
            hot = hot_ref[:, pl.ds(0, size)]
            dot = functools.partial(jnp.dot, preferred_element_type=F32)
            out_ref[:, pl.ds(start, size)] = dot(high_ref[...], hot) + dot(low_ref[...], hot)

    vmem = pl.BlockSpec(memory_space=pltpu.VMEM)
    return pl.pallas_call(
        kernel,
        out_shape=jax.ShapeDtypeStruct((rows, width), F32),
        in_specs=[pl.BlockSpec(memory_space=pltpu.SMEM), vmem] + [vmem] * len(pieces),
        out_specs=vmem,
        scratch_shapes=[
            pltpu.VMEM((rows, count * 128), BF16),
            pltpu.VMEM((rows, count * 128), BF16),
            pltpu.VMEM((count * 128, step), BF16),
        ],
        compiler_params=pltpu.CompilerParams(vmem_limit_bytes=VMEM_BYTES),
        name="permute_columns",
    )(tiles, wanted.reshape(1, width), *[p[2] for p in pieces])


def prepare(block, keep, name):
    cycles, depth, tiles, width = block.shape

    def kernel(keep_ref, in_ref, high_ref, low_ref):
        own = keep_ref[pl.program_id(0) // (cycles // 2)]
        for b in range(tiles):
            value = in_ref[0, pl.ds(b, depth, stride=tiles), :]
            if b == 0:
                value = jnp.where(own > 0, value, jnp.zeros_like(value))
            high, low = split(value)
            high_ref[:, pl.ds(b * width, width)] = high
            low_ref[:, pl.ds(b * width, width)] = low

    out = jax.ShapeDtypeStruct((cycles * depth, tiles * width), BF16)
    spec = pl.BlockSpec((depth, tiles * width), lambda a: (a, 0))
    return pl.pallas_call(
        kernel,
        grid=(cycles,),
        out_shape=(out, out),
        in_specs=[
            pl.BlockSpec(memory_space=pltpu.SMEM),
            pl.BlockSpec((1, depth * tiles, width), lambda a: (a, 0, 0)),
        ],
        out_specs=(spec, spec),
        compiler_params=pltpu.CompilerParams(vmem_limit_bytes=VMEM_BYTES),
        name=name,
    )(keep, block.reshape(cycles, depth * tiles, width))


def solve(rhs_offset, known, previous, stripe, coupling, diagonal):
    rows = stripe.shape[0]
    n_coupling = len(coupling)
    places = [(first, tile) for _, first, tile in coupling + diagonal]

    def kernel(*refs):
        refs = list(refs)
        stripe_ref = refs.pop(0)
        prev = (refs.pop(0), refs.pop(0)) if known else None
        parts = refs[: len(places)]
        out_ref, out_high, out_low, high_ref, low_ref, rhs_high, rhs_low = refs[len(places) :]

        def load(chosen):
            for (first, tile), part in chosen:
                high, low = split(part[...])
                to = (pl.ds(first, part.shape[0]), pl.ds(tile * 128, 128))
                high_ref[to] = high
                low_ref[to] = low

        pairs = list(zip(places, parts, strict=True))
        step = 256
        if known:
            load(pairs[:n_coupling])
            left = (prev[0][...], prev[1][...])
            for start in range(0, NB, step):
                to = (slice(None), pl.ds(start, step))
                value = stripe_ref[:, pl.ds(rhs_offset + start, step)] - mul3(left, (high_ref[to], low_ref[to]), NN)
                rhs_high[to], rhs_low[to] = split(value)
        else:
            for start in range(0, NB, step):
                to = (slice(None), pl.ds(start, step))
                rhs_high[to], rhs_low[to] = split(stripe_ref[:, pl.ds(rhs_offset + start, step)])
        load(pairs[n_coupling:])
        left = (rhs_high[...], rhs_low[...])
        for start in range(0, NB, step):
            to = (pl.ds(start, step), slice(None))
            value = mul3(left, (high_ref[to], low_ref[to]), NT)
            to = (slice(None), pl.ds(start, step))
            out_ref[to] = value
            out_high[to], out_low[to] = split(value)

    vmem = pl.BlockSpec(memory_space=pltpu.VMEM)
    operands = [stripe, *previous, *[c[0] for c in coupling + diagonal]]
    return pl.pallas_call(
        kernel,
        out_shape=(
            jax.ShapeDtypeStruct((rows, NB), F32),
            jax.ShapeDtypeStruct((rows, NB), BF16),
            jax.ShapeDtypeStruct((rows, NB), BF16),
        ),
        in_specs=[vmem] * len(operands),
        out_specs=(vmem, vmem, vmem),
        scratch_shapes=[pltpu.VMEM((NB, NB), BF16)] * 2 + [pltpu.VMEM((rows, NB), BF16)] * 2,
        compiler_params=pltpu.CompilerParams(vmem_limit_bytes=VMEM_BYTES),
        name="solve_second" if known else "solve_first",
    )(*operands)


def trail_first(sensitivity, own_tile, solved, halves):
    rows, tiles, width = sensitivity.shape
    group = 8

    def kernel(sens_ref, own_ref, yh_ref, yl_ref, ah_ref, al_ref, bh_ref, bl_ref, out_ref):
        half = NB // 2
        first = pl.program_id(0) == 0
        left_a = (yh_ref[:, pl.ds(0, half)], yl_ref[:, pl.ds(0, half)])
        left_b = (yh_ref[:, pl.ds(half, half)], yl_ref[:, pl.ds(half, half)])
        for b in range(0, group, 2):
            to = (slice(None), pl.ds(b * width, 2 * width))
            parts = []
            for c in (b, b + 1):
                part = sens_ref[pl.ds(c, rows, stride=group), :]
                if c == 0:
                    part = jnp.where(first, own_ref[...], part)
                parts.append(part)
            base = jnp.concatenate(parts, axis=1)
            change = mul3(left_a, (ah_ref[to], al_ref[to]), NN) + mul3(left_b, (bh_ref[to], bl_ref[to]), NN)
            out_ref[to] = base - change

    wide = group * width
    whole = pl.BlockSpec((rows, NB), lambda i: (0, 0))
    part = pl.BlockSpec((NB // 2, wide), lambda i: (0, i))

    def body(sens_ref, *refs):
        kernel(sens_ref.reshape(rows * group, width), *refs)

    return pl.pallas_call(
        body,
        grid=(tiles // group,),
        out_shape=jax.ShapeDtypeStruct((rows, tiles * width), F32),
        in_specs=[
            pl.BlockSpec((rows, group, width), lambda i: (0, i, 0)),
            pl.BlockSpec((rows, width), lambda i: (0, 0)),
            whole,
            whole,
            part,
            part,
            part,
            part,
        ],
        out_specs=pl.BlockSpec((rows, wide), lambda i: (0, i)),
        compiler_params=pltpu.CompilerParams(vmem_limit_bytes=VMEM_BYTES),
        name="trail_first",
    )(sensitivity, own_tile, *solved, *halves)


def trail_second(partial, solved, halves, tiles):
    rows = partial.shape[0]
    width = 128
    group = 8

    def kernel(in_ref, yh_ref, yl_ref, ah_ref, al_ref, bh_ref, bl_ref, out_ref):
        out_ref = out_ref.reshape(rows * group, width)
        half = NB // 2
        left_a = (yh_ref[:, pl.ds(0, half)], yl_ref[:, pl.ds(0, half)])
        left_b = (yh_ref[:, pl.ds(half, half)], yl_ref[:, pl.ds(half, half)])
        for b in range(0, group, 2):
            to = (slice(None), pl.ds(b * width, 2 * width))
            change = mul3(left_a, (ah_ref[to], al_ref[to]), NN) + mul3(left_b, (bh_ref[to], bl_ref[to]), NN)
            value = in_ref[to] - change
            out_ref[pl.ds(b, rows, stride=group), :] = value[:, :width]
            out_ref[pl.ds(b + 1, rows, stride=group), :] = value[:, width:]

    wide = group * width
    whole = pl.BlockSpec((rows, NB), lambda i: (0, 0))
    part = pl.BlockSpec((NB // 2, wide), lambda i: (1, i))
    return pl.pallas_call(
        kernel,
        grid=(tiles // group,),
        out_shape=jax.ShapeDtypeStruct((rows, tiles, width), F32),
        in_specs=[pl.BlockSpec((rows, wide), lambda i: (0, i)), whole, whole, part, part, part, part],
        out_specs=pl.BlockSpec((rows, group, width), lambda i: (0, i, 0)),
        compiler_params=pltpu.CompilerParams(vmem_limit_bytes=VMEM_BYTES),
        name="trail_second",
    )(partial, *solved, *halves)


def place_unknowns(core, parts):
    rows, half = parts[0].shape
    per_step = half // 128
    cycles = 2 * per_step

    def kernel(core_ref, *refs):
        out_ref = refs[-1].reshape(rows * cycles, 128)
        own = pl.program_id(0) == core_ref[0]
        for chosen, wanted in ((refs[0:2], own), (refs[2:4], jnp.logical_not(own))):

            @pl.when(wanted)
            def _(chosen=chosen):
                for step in range(2):
                    for a in range(per_step):
                        out_ref[pl.ds(step * per_step + a, rows, stride=cycles), :] = chosen[step][:, pl.ds(a * 128, 128)]

    spec = pl.BlockSpec((rows, half), lambda i, core_ref: (0, 0))
    return pl.pallas_call(
        kernel,
        out_shape=jax.ShapeDtypeStruct((2 * rows, cycles, 128), F32),
        grid_spec=pltpu.PrefetchScalarGridSpec(
            num_scalar_prefetch=1,
            grid=(2,),
            in_specs=[spec] * 4,
            out_specs=pl.BlockSpec((rows, cycles, 128), lambda i, core_ref: (i, 0, 0)),
        ),
        compiler_params=pltpu.CompilerParams(vmem_limit_bytes=VMEM_BYTES),
        name="place_unknowns",
    )(core, parts[0], parts[2], parts[1], parts[3])


def shards(factor_rows, sensitivity, pivots):
    count = lax.axis_size("pcol")
    sizes = grid_of(count)
    cycles, width, col_tiles = factor_rows.shape[:3]
    rows = sensitivity.shape[0]
    per_block = NB // width
    index = lax.axis_index("pcol")
    core = lax.axis_index("prow")
    tiles = source_tiles(sizes, index)
    swap = lambda value: lax.ppermute(value, "prow", [(0, 1), (1, 0)])

    own_pieces = gather_pieces(sensitivity[:, 0, :], sizes)
    other_rows = swap(factor_rows)
    corner = factor_rows[:, :, 0, :].reshape(cycles * width, width)
    gathered = lax.all_gather(corner, "pcol", axis=0)[: 2 * per_block]
    gathered_other = swap(gathered)

    keep = jnp.stack([index >= per_block, index >= 2 * per_block]).astype(jnp.int32)
    own_halves = prepare(factor_rows, keep, "prepare_own")
    other_halves = prepare(other_rows, keep, "prepare_other")
    halves = (*own_halves, *other_halves)

    wanted = jnp.concatenate([pivots[: 2 * NB], lax.dynamic_slice(pivots, (index * width,), (width,))])
    stripe = permute_columns(own_pieces, sizes, tiles, wanted, rows)
    own_tile = stripe[:, 2 * NB :]

    half = NB // 2
    first_diag, coupling, second_diag = [], [], []
    for side, block in enumerate((gathered, gathered_other)):
        for j in range(per_block):
            first_diag.append((block[j, :half], side * half, j))
            coupling.append((block[per_block + j, :half], side * half, j))
            second_diag.append((block[per_block + j, half:], side * half, j))
    y0, *y0_halves = solve(0, False, (), stripe, [], first_diag)
    partial = trail_first(sensitivity, own_tile, y0_halves, halves)
    y1, *y1_halves = solve(NB, True, y0_halves, stripe, coupling, second_diag)
    updated = trail_second(partial, y1_halves, halves, col_tiles)

    parts = []
    for y in (y0, y1):
        parts += [y[:, :half], swap(y[:, half:])]
    adjoint = place_unknowns(core.reshape(1).astype(jnp.int32), parts)
    return adjoint, updated


def solution(mesh):
    return jax.shard_map(
        shards,
        mesh=mesh,
        in_specs=(P(None, "prow", None, "pcol"), P("prow", None, "pcol"), P()),
        out_specs=(P(None, None, "prow"), P("prow", None, "pcol")),
        check_vma=False,
    )
```

time: 479 us -> 319 us (0.67)
  waiting for transfers between devices: 334 us -> 142 us
  Pallas kernels: 0 us -> 102 us
  matrix products: 71.2 us -> 0 us
  starting transfers between devices: 0.39 us -> 27.7 us
  local copies, waits for them, and re-layouts: 45.1 us -> 31.1 us
  other arithmetic: 9.97 us -> 1.84 us
    psum x2 -> x0, waiting for transfers between devices: 250 us -> none  [solve_block(): return lax.psum(partial_sum, 'pcol')]
    pallas_call x0 -> x8, Pallas kernels: none -> 102 us  [the longest x2 25.1 us: prepare(): pl.pallas_call(kernel, grid=(cycles,), out_shape=(out, out), in_specs=[pl...]
    dot_general x4 -> x0, matrix products: 71.2 us -> none  [the longest x1 60.8 us: shards(): jnp.dot(picked, all_rows, precision=lax.Precision.HIGHEST, preferred_elem...]
    all_gather x1, waiting for transfers between devices: 76.2 us -> 116 us  [shards(): gathered = lax.all_gather(corner, 'pcol', axis=0)[:2 * per_block]]
    ppermute x0 -> x31, starting transfers between devices: none -> 27.6 us  [the longest x27 26.6 us: shift(): return lax.ppermute(value, 'pcol', pairs)]
    ppermute x0 -> x31, waiting for transfers between devices: none -> 25.7 us  [the longest x27 25.7 us: shift(): return lax.ppermute(value, 'pcol', pairs)]
    squeeze x0 -> x4, local copies, waits for them, and re-layouts: none -> 14.1 us  [the longest x2 9.35 us: shards(): second_diag.append((block[per_block + j, half:], side * half, j))]
    unnamed x11 -> x58, local copies, waits for them, and re-layouts: 13.4 us -> 1.46 us
  transfers between devices with their start and end apart: 5 -> 32, of which waited for: 4 -> 18; matrix products, arithmetic and copies ran while one was open for 6% -> 9% of each run, Pallas kernels for 0% -> 30%
where the time goes in v1:
time: 319 us; the launch traced here: 318 us
  waiting for transfers between devices  142 us (45%)
  Pallas kernels  102 us (32%)
  local copies, waits for them, and re-layouts  31.1 us (10%)
  starting transfers between devices  27.7 us (9%)
  between operations  14.4 us (5%)
    all_gather x1, waiting for transfers between devices, shards(): gathered = lax.all_gather(corner, 'pcol', axis=0)[:2 * per_block]  116 us
    ppermute x27, starting transfers between devices, shift(): return lax.ppermute(value, 'pcol', pairs)  26.6 us
    ppermute x27, waiting for transfers between devices, shift(): return lax.ppermute(value, 'pcol', pairs)  25.7 us
    pallas_call x2, Pallas kernels, prepare(): pl.pallas_call(kernel, grid=(cycles,), out_shape=(out, out), in_specs=[pl...  25.1 us
    pallas_call x2, Pallas kernels, solve(): pl.pallas_call(kernel, out_shape=(jax.ShapeDtypeStruct((rows, NB), F32),...  24.3 us
    pallas_call x1, Pallas kernels, trail_second(): pl.pallas_call(kernel, grid=(tiles // group,), out_shape=jax.ShapeDtypeSt...  16.6 us
    pallas_call x1, Pallas kernels, trail_first(): pl.pallas_call(body, grid=(tiles // group,), out_shape=jax.ShapeDtypeStru...  16.1 us
    pallas_call x1, Pallas kernels, permute_columns(): pl.pallas_call(kernel, out_shape=jax.ShapeDtypeStruct((rows, width), F32)...  14.9 us
  transfers between devices with their start and end apart: 32, of which 18 were waited for; matrix products, arithmetic and copies ran while one was open for 9% of the time, Pallas kernels for 30%

profile of v1, /device:TPU:0, one launch (start us, length us, event | category | flops | bytes accessed | tf_op | source)
XLA Modules:
  0.0 318.5 jit_solution(17074356585005228604)
XLA Ops:
  7.2 3.3 %slice.208 = f32[8,128,1,128]{3,2,1,0:T(1,128)} slice(f32[8,128,24,128]{3,2,1,0:T(8,128)} %param.3), slice={[0:8], [0:128], [0:1], [0:128]} | slice | bytes 1048576 | tf_op jit(solution)/shard_map/slice | solution.py:333
  11.0 115.9 %all-gather.2.cloned.1.call-done = f32[16,1024,128]{2,1,0:T(8,128)} async-done(((f32[1,1024,128]{2,1,0:T(8,128)}), f32[16,1024,128]{2,1,0:T(8,128)}) %all-gather.2.cloned.1.call-update) | async-done | bytes 8388624 | tf_op jit(solution)/shard_map/all_gather | solution.py:334
  126.9 1.7 fusion.11
  128.6 1.3 collective-permute-start.1
  130.0 0.8 collective-permute-start
  130.7 1.7 slice.201
  132.8 1.8 collective-permute-done.1.refs_2_
  134.6 1.5 collective-permute-start.4
  136.1 0.6 collective-permute-start.3
  136.6 3.1 collective-permute-done.4.refs_6_
  139.7 1.5 collective-permute-start.2
  141.2 0.6 collective-permute-start.5
  141.8 0.7 collective-permute-done.6
  142.5 2.2 collective-permute-done.2.refs_3_
  144.7 1.5 collective-permute-start.11
  146.2 0.6 collective-permute-start.10
  146.7 2.9 collective-permute-done.11.refs_14_
  149.7 1.4 collective-permute-start.8
  151.1 0.7 collective-permute-done.10.refs_13_
  151.8 1.3 collective-permute-start.7
  153.1 0.7 collective-permute-start.12
  153.9 1.2 collective-permute-done.8.refs_10_
  155.1 1.4 collective-permute-start.9
  156.5 1.7 collective-permute-done.7.refs_9_
  158.2 1.3 collective-permute-start.18
  159.5 0.6 collective-permute-done.9.refs_11_
  160.1 1.5 collective-permute-start.17
  161.6 1.9 collective-permute-done.18.refs_22_
  163.5 0.9 collective-permute-start.15
  164.4 0.7 collective-permute-done.17.refs_21_
  165.1 1.4 collective-permute-start.14
  166.4 2.0 collective-permute-done.15.refs_18_
  168.5 0.9 collective-permute-start.19
  169.4 1.2 collective-permute-start.16
  170.7 0.9 collective-permute-start.25
  171.5 2.2 collective-permute-done.19.refs_23_
  173.7 1.4 collective-permute-start.24
  175.1 0.6 collective-permute-start.22
  175.7 0.8 dynamic_slice.3
  176.5 1.0 collective-permute-done.25.refs_30_
  177.9 0.9 collective-permute-done.24.refs_29_
  178.8 1.4 collective-permute-start.26
  180.2 1.4 collective-permute-start.23
  181.6 0.7 pad_add_fusion
  182.3 0.6 reshape.19.wanted_ref
  182.9 0.5 fusion.2.tiles_ref
  183.8 1.6 collective-permute-done.23.refs_27_
  185.7 14.9 %permute_columns.1.refs_0_ = f32[512,2176]{1,0:T(8,128)} custom-call(s32[16]{0:T(128)} %fusion.2.tiles_ref, s32[1,2176]{1,0:T(1,128)} %reshape.19.wanted_ref, f32[256,128]{1,0:T(8,128)} %bitcast.118, f32[256,128]{1,0:T(8,128)} %copy-done.11, f32[256,128]{1,0:T(8,128)} %copy-done.10, f32[256,128]{1,0:T(8,128)} %copy-done.14, f32[256,128]{1,0:T(8,128)} %bitcast.115, ...), custom_call_target="tpu_custom_call" | custom-call | tf_op jit(solution)/shard_map/permute_columns/pallas_call | solution.py:108
  200.7 2.4 slice_bitcast_fusion.43
  203.1 4.6 %slice_bitcast_fusion.8 = (f32[512,128]{1,0:T(8,128)}, f32[512,128]{1,0:T(8,128)}, f32[512,128]{1,0:T(8,128)}, f32[512,128]{1,0:T(8,128)}, f32[512,128]{1,0:T(8,...) fusion(f32[16,1024,128]{2,1,0:T(8,128)} %all-gather.2.cloned.1., ...), kind=kLoop, calls=%fused_computation.8 | loop fusion | bytes 9961472 | tf_op jit(solution)/shard_map/squeeze | solution.py:352
  207.7 2.4 slice_bitcast_fusion.35
  210.1 4.7 %slice_bitcast_fusion = (f32[512,128]{1,0:T(8,128)}, f32[512,128]{1,0:T(8,128)}, f32[512,128]{1,0:T(8,128)}, f32[512,128]{1,0:T(8,128)}, f32[512,128]{1,0:T(8,12...) fusion(f32[16,1024,128]{2,1,0:T(8,128)} %collective-permute-done.27), kind=kLoop, calls=%fused_computation | loop fusion | bytes 9961472 | tf_op jit(solution)/shard_map/squeeze | solution.py:352
  214.8 9.5 %solve_first.1 = (f32[512,1024]{1,0:T(8,128)}, bf16[512,1024]{1,0:T(8,128)(2,1)}, bf16[512,1024]{1,0:T(8,128)(2,1)}) custom-call(f32[512,2176]{1,0:T(8,128)} %permute_columns.1.refs_0_, f32[512,128]{1,0:T(8,128)} %get-tuple-element.69.refs_1_, f32[512,128]{1,0:T(8,128)} %get-tuple-element.68.refs_2_, f32[512,128]{1,0:T(8,128)} %get-tuple-element.67.refs_3_, ...), custom_call_target="tpu_custom_call" | custom-call | tf_op jit(solution)/shard_map/solve_first/pallas_call | solution.py:195
  224.3 2.7 fusion.13
  227.0 14.8 %solve_second.1 = (f32[512,1024]{1,0:T(8,128)}, bf16[512,1024]{1,0:T(8,128)(2,1)}, bf16[512,1024]{1,0:T(8,128)(2,1)}) custom-call(f32[512,2176]{1,0:T(8,128)} %permute_columns.1.refs_0_, bf16[512,1024]{1,0:T(8,128)(2,1)} %get-tuple-element.13.refs_1_, bf16[512,1024]{1,0:T(8,128)(2,1)} %get-tuple-element.14.refs_2_, f32[512,128]{1,0:T(8,128)} %get-tuple-element.56.refs_3_, ...), custom_call_target="tpu_custom_call" | custom-call | tf_op jit(solution)/shard_map/solve_second/pallas_call | solution.py:195
  241.8 3.0 fusion.12
  245.4 0.6 add_convert_fusion.keep_ref
  246.0 12.6 %prepare_own.1 = (bf16[1024,3072]{1,0:T(8,128)(2,1)}, bf16[1024,3072]{1,0:T(8,128)(2,1)}) custom-call(s32[2]{0:T(128)} %add_convert_fusion.keep_ref, f32[8,3072,128]{2,1,0:T(8,128)} %bitcast.111), custom_call_target="tpu_custom_call" | custom-call | tf_op jit(solution)/shard_map/prepare_own/pallas_call | solution.py:138
  258.6 1.7 slice.316.refs_0_
  260.3 12.5 %prepare_other.1 = (bf16[1024,3072]{1,0:T(8,128)(2,1)}, bf16[1024,3072]{1,0:T(8,128)(2,1)}) custom-call(s32[2]{0:T(128)} %add_convert_fusion.keep_ref, f32[8,3072,128]{2,1,0:T(8,128)} %bitcast.56.in_ref), custom_call_target="tpu_custom_call" | custom-call | tf_op jit(solution)/shard_map/prepare_other/pallas_call | solution.py:138
  272.8 16.1 %trail_first.1.in_ref = f32[512,3072]{1,0:T(8,128)} custom-call(f32[512,24,128]{2,1,0:T(8,128)} %sens_ref.1, f32[512,128]{1,0:T(8,128)} %slice.316.refs_0_, bf16[512,1024]{1,0:T(8,128)(2,1)} %get-tuple-element.13.refs_1_, bf16[512,1024]{1,0:T(8,128)(2,1)} %get-tuple-element.14.refs_2_, bf16[1024,3072]{1,0:T(8,128)(2,1)} %get-tuple-element.16.refs_3_.ah_ref, ...), custom_call_target="tpu_custom_call" | custom-call | tf_op jit(solution)/shard_map/trail_first/pallas_call | solution.py:238
  288.9 16.6 %trail_second.1 = f32[512,24,128]{2,1,0:T(8,128)} custom-call(f32[512,3072]{1,0:T(8,128)} %trail_first.1.in_ref, bf16[512,1024]{1,0:T(8,128)(2,1)} %get-tuple-element.20.yh_ref, bf16[512,1024]{1,0:T(8,128)(2,1)} %get-tuple-element.21.yl_ref, bf16[1024,3072]{1,0:T(8,128)(2,1)} %get-tuple-element.16.refs_3_.ah_ref, ...), custom_call_target="tpu_custom_call" | custom-call | tf_op jit(solution)/shard_map/trail_second/pallas_call | solution.py:278
  305.6 1.0 copy-done
  306.9 4.7 %place_unknowns.1 = f32[1024,8,128]{2,1,0:T(8,128)} custom-call(s32[1]{0:T(128)} %bitcast.core_ref, f32[512,512]{1,0:T(8,128)} %get-tuple-element.75.refs_0_, f32[512,512]{1,0:T(8,128)} %get-tuple-element.73.refs_1_, f32[512,512]{1,0:T(8,128)} %copy-done, f32[512,512]{1,0:T(8,128)} %copy-done.1), custom_call_target="tpu_custom_call" | custom-call | tf_op jit(solution)/shard_map/place_unknowns/pallas_call | solution.py:306
  (85 shorter events, 2.9 us)
Async XLA Ops:
  7.2 119.7 %all-gather.2.cloned.1.call-start = ((), (), s32[]{:S(2)}) async-start(), calls=%async_computation | async-start | bytes 8912896 | tf_op jit(solution)/shard_map/all_gather | solution.py:334
  10.5 249.7 %collective-permute-start.30 = (f32[8,128,24,128]{3,2,1,0:T(8,128)}, f32[8,128,24,128]{3,2,1,0:T(8,128)}, u32[]{:S(2)}, u32[]{:S(2)}) collective-permute-start(f32[8,128,24,128]{3,2,1,0:T(8,128)} %param.3), channel_id=1, source_target_pairs={{0,16},{16,0},{1,17},{17,1},{2,18},{18,2},{3,19},{19,3},{4,20},{20... | collective-permute-start | bytes 37748744 | tf_op jit(solution)/shard_map/ppermute | solution.py:329
  126.9 80.8 %collective-permute-start.27 = (f32[16,1024,128]{2,1,0:T(8,128)}, f32[16,1024,128]{2,1,0:T(8,128)}, u32[]{:S(2)}, u32[]{:S(2)}) collective-permute-start(f32[16,1024,128]{2,1,0:T(8,128)} %all-gather.2.cloned.1.call-done), channel_id=1, source_target_pairs={{0,16},{16,0},{1,17},{17,1},{2,18},{18,2},{3,19},{19,3},{4,20},{20... | collective-permute-start | bytes 25165832 | tf_op jit(solution)/shard_map/ppermute | solution.py:329
  128.6 56.9 %copy-start.2 = (f32[256,1,128]{2,1,0:T(1,128)}, f32[256,1,128]{2,1,0:T(1,128)S(1)}, u32[]{:S(2)}) copy-start(f32[256,1,128]{2,1,0:T(1,128)S(1)} %get-tuple-element.70) | copy-start | bytes 393220
  128.6 56.8 %copy-start.3 = (f32[256,1,128]{2,1,0:T(1,128)}, f32[256,1,128]{2,1,0:T(1,128)S(1)}, u32[]{:S(2)}) copy-start(f32[256,1,128]{2,1,0:T(1,128)S(1)} %get-tuple-element.71) | copy-start | bytes 393220
  128.6 6.0 %collective-permute-start.1 = (f32[256,128]{1,0:T(8,128)S(1)}, f32[256,128]{1,0:T(8,128)S(1)}, u32[]{:S(2)}, u32[]{:S(2)}) collective-permute-start(f32[256,128]{1,0:T(8,128)S(1)} %bitcast.116), channel_id=1, source_target_pairs={{0,1},{1,0},{2,3},{3,2},{4,5},{5,4},{6,7},{7,6},{8,9},{9,8},{10,11... | collective-permute-start | bytes 393224 | tf_op jit(solution)/shard_map/ppermute | solution.py:48
  130.0 6.1 %collective-permute-start = (f32[256,128]{1,0:T(8,128)S(1)}, f32[256,128]{1,0:T(8,128)S(1)}, u32[]{:S(2)}, u32[]{:S(2)}) collective-permute-start(f32[256,128]{1,0:T(8,128)S(1)} %bitcast.117), channel_id=1, source_target_pairs={{0,2},{1,3},{2,0},{3,1},{4,6},{5,7},{6,4},{7,5},{8,10},{9,11},{10,... | collective-permute-start | bytes 393224 | tf_op jit(solution)/shard_map/ppermute | solution.py:48
  132.5 10.0 %collective-permute-start.6 = (f32[512,128]{1,0:T(8,128)S(1)}, f32[512,128]{1,0:T(8,128)S(1)}, u32[]{:S(2)}, u32[]{:S(2)}) collective-permute-start(f32[512,128]{1,0:T(8,128)S(1)} %bitcast.119), channel_id=1, source_target_pairs={{0,4},{1,5},{2,6},{3,7},{4,8},{5,9},{6,10},{7,11},{8,12},{9,13},{1... | collective-permute-start | bytes 786440 | tf_op jit(solution)/shard_map/ppermute | solution.py:48
  134.6 50.9 %copy-start.10 = (f32[256,128]{1,0:T(8,128)}, f32[256,128]{1,0:T(8,128)S(1)}, u32[]{:S(2)}) copy-start(f32[256,128]{1,0:T(8,128)S(1)} %collective-permute-done.1.refs_2_) | copy-start | bytes 393220
  134.6 5.1 %collective-permute-start.4 = (f32[256,128]{1,0:T(8,128)S(1)}, f32[256,128]{1,0:T(8,128)S(1)}, u32[]{:S(2)}, u32[]{:S(2)}) collective-permute-start(f32[256,128]{1,0:T(8,128)S(1)} %bitcast.113), channel_id=1, source_target_pairs={{0,2},{1,3},{2,0},{3,1},{4,6},{5,7},{6,4},{7,5},{8,10},{9,11},{10,... | collective-permute-start | bytes 393224 | tf_op jit(solution)/shard_map/ppermute | solution.py:48
  136.1 49.4 %copy-start.11 = (f32[256,128]{1,0:T(8,128)}, f32[256,128]{1,0:T(8,128)S(1)}, u32[]{:S(2)}) copy-start(f32[256,128]{1,0:T(8,128)S(1)} %collective-permute-done.refs_1_) | copy-start | bytes 393220
  136.1 5.1 %collective-permute-start.3 = (f32[256,128]{1,0:T(8,128)S(1)}, f32[256,128]{1,0:T(8,128)S(1)}, u32[]{:S(2)}, u32[]{:S(2)}) collective-permute-start(f32[256,128]{1,0:T(8,128)S(1)} %bitcast.114), channel_id=1, source_target_pairs={{0,1},{1,0},{2,3},{3,2},{4,5},{5,4},{6,7},{7,6},{8,9},{9,8},{10,11... | collective-permute-start | bytes 393224 | tf_op jit(solution)/shard_map/ppermute | solution.py:48
  139.7 45.7 %copy-start.12 = (f32[256,128]{1,0:T(8,128)}, f32[256,128]{1,0:T(8,128)S(1)}, u32[]{:S(2)}) copy-start(f32[256,128]{1,0:T(8,128)S(1)} %collective-permute-done.4.refs_6_) | copy-start | bytes 393220
  139.7 5.0 %collective-permute-start.2 = (f32[256,128]{1,0:T(8,128)S(1)}, f32[256,128]{1,0:T(8,128)S(1)}, u32[]{:S(2)}, u32[]{:S(2)}) collective-permute-start(f32[256,128]{1,0:T(8,128)S(1)} %collective-permute-done.1.refs_2_), channel_id=1, source_target_pairs={{0,2},{1,3},{2,0},{3,1},{4,6},{5,7},{6,4},{7,5},{8,10},{9,11},{10,... | collective-permute-start | bytes 393224 | tf_op jit(solution)/shard_map/ppermute | solution.py:48
  141.2 44.3 %copy-start.13 = (f32[256,128]{1,0:T(8,128)}, f32[256,128]{1,0:T(8,128)S(1)}, u32[]{:S(2)}) copy-start(f32[256,128]{1,0:T(8,128)S(1)} %collective-permute-done.3.refs_5_) | copy-start | bytes 393220
  141.2 5.0 %collective-permute-start.5 = (f32[256,128]{1,0:T(8,128)S(1)}, f32[256,128]{1,0:T(8,128)S(1)}, u32[]{:S(2)}, u32[]{:S(2)}) collective-permute-start(f32[256,128]{1,0:T(8,128)S(1)} %collective-permute-done.4.refs_6_), channel_id=1, source_target_pairs={{0,1},{1,0},{2,3},{3,2},{4,5},{5,4},{6,7},{7,6},{8,9},{9,8},{10,11... | collective-permute-start | bytes 393224 | tf_op jit(solution)/shard_map/ppermute | solution.py:48
  142.5 10.6 %collective-permute-start.13 = (f32[512,128]{1,0:T(8,128)S(1)}, f32[512,128]{1,0:T(8,128)S(1)}, u32[]{:S(2)}, u32[]{:S(2)}) collective-permute-start(f32[512,128]{1,0:T(8,128)S(1)} %collective-permute-done.6), channel_id=1, source_target_pairs={{0,4},{1,5},{2,6},{3,7},{4,8},{5,9},{6,10},{7,11},{8,12},{9,13},{1... | collective-permute-start | bytes 786440 | tf_op jit(solution)/shard_map/ppermute | solution.py:48
  142.5 43.0 %copy-start.4 = (f32[256,128]{1,0:T(8,128)}, f32[256,128]{1,0:T(8,128)S(1)}, u32[]{:S(2)}) copy-start(f32[256,128]{1,0:T(8,128)S(1)} %get-tuple-element.80.refs_12_) | copy-start | bytes 393220
  142.5 43.0 %copy-start.5 = (f32[256,128]{1,0:T(8,128)}, f32[256,128]{1,0:T(8,128)S(1)}, u32[]{:S(2)}) copy-start(f32[256,128]{1,0:T(8,128)S(1)} %get-tuple-element.81.refs_8_) | copy-start | bytes 393220
  144.7 40.8 %copy-start.14 = (f32[256,128]{1,0:T(8,128)}, f32[256,128]{1,0:T(8,128)S(1)}, u32[]{:S(2)}) copy-start(f32[256,128]{1,0:T(8,128)S(1)} %collective-permute-done.2.refs_3_) | copy-start | bytes 393220
  144.7 5.0 %collective-permute-start.11 = (f32[256,128]{1,0:T(8,128)S(1)}, f32[256,128]{1,0:T(8,128)S(1)}, u32[]{:S(2)}, u32[]{:S(2)}) collective-permute-start(f32[256,128]{1,0:T(8,128)S(1)} %get-tuple-element.80.refs_12_), channel_id=1, source_target_pairs={{0,2},{1,3},{2,0},{3,1},{4,6},{5,7},{6,4},{7,5},{8,10},{9,11},{10,... | collective-permute-start | bytes 393224 | tf_op jit(solution)/shard_map/ppermute | solution.py:48
  146.2 39.3 %copy-start.15 = (f32[256,128]{1,0:T(8,128)}, f32[256,128]{1,0:T(8,128)S(1)}, u32[]{:S(2)}) copy-start(f32[256,128]{1,0:T(8,128)S(1)} %collective-permute-done.5.refs_7_) | copy-start | bytes 393220
  146.2 5.6 %collective-permute-start.10 = (f32[256,128]{1,0:T(8,128)S(1)}, f32[256,128]{1,0:T(8,128)S(1)}, u32[]{:S(2)}, u32[]{:S(2)}) collective-permute-start(f32[256,128]{1,0:T(8,128)S(1)} %get-tuple-element.80.refs_12_), channel_id=1, source_target_pairs={{0,1},{1,0},{2,3},{3,2},{4,5},{5,4},{6,7},{7,6},{8,9},{9,8},{10,11... | collective-permute-start | bytes 393224 | tf_op jit(solution)/shard_map/ppermute | solution.py:48
  149.7 35.9 %copy-start.16 = (f32[256,128]{1,0:T(8,128)}, f32[256,128]{1,0:T(8,128)S(1)}, u32[]{:S(2)}) copy-start(f32[256,128]{1,0:T(8,128)S(1)} %collective-permute-done.11.refs_14_) | copy-start | bytes 393220
  149.7 5.5 %collective-permute-start.8 = (f32[256,128]{1,0:T(8,128)S(1)}, f32[256,128]{1,0:T(8,128)S(1)}, u32[]{:S(2)}, u32[]{:S(2)}) collective-permute-start(f32[256,128]{1,0:T(8,128)S(1)} %get-tuple-element.81.refs_8_), channel_id=1, source_target_pairs={{0,1},{1,0},{2,3},{3,2},{4,5},{5,4},{6,7},{7,6},{8,9},{9,8},{10,11... | collective-permute-start | bytes 393224 | tf_op jit(solution)/shard_map/ppermute | solution.py:48
  151.8 33.7 %copy-start.17 = (f32[256,128]{1,0:T(8,128)}, f32[256,128]{1,0:T(8,128)S(1)}, u32[]{:S(2)}) copy-start(f32[256,128]{1,0:T(8,128)S(1)} %collective-permute-done.10.refs_13_) | copy-start | bytes 393220
  151.8 6.4 %collective-permute-start.7 = (f32[256,128]{1,0:T(8,128)S(1)}, f32[256,128]{1,0:T(8,128)S(1)}, u32[]{:S(2)}, u32[]{:S(2)}) collective-permute-start(f32[256,128]{1,0:T(8,128)S(1)} %get-tuple-element.81.refs_8_), channel_id=1, source_target_pairs={{0,2},{1,3},{2,0},{3,1},{4,6},{5,7},{6,4},{7,5},{8,10},{9,11},{10,... | collective-permute-start | bytes 393224 | tf_op jit(solution)/shard_map/ppermute | solution.py:48
  153.1 6.3 %collective-permute-start.12 = (f32[256,128]{1,0:T(8,128)S(1)}, f32[256,128]{1,0:T(8,128)S(1)}, u32[]{:S(2)}, u32[]{:S(2)}) collective-permute-start(f32[256,128]{1,0:T(8,128)S(1)} %collective-permute-done.11.refs_14_), channel_id=1, source_target_pairs={{0,1},{1,0},{2,3},{3,2},{4,5},{5,4},{6,7},{7,6},{8,9},{9,8},{10,11... | collective-permute-start | bytes 393224 | tf_op jit(solution)/shard_map/ppermute | solution.py:48
  153.9 31.7 %copy-start.6 = (f32[256,128]{1,0:T(8,128)}, f32[256,128]{1,0:T(8,128)S(1)}, u32[]{:S(2)}) copy-start(f32[256,128]{1,0:T(8,128)S(1)} %get-tuple-element.78.refs_20_) | copy-start | bytes 393220
  153.9 31.7 %copy-start.7 = (f32[256,128]{1,0:T(8,128)}, f32[256,128]{1,0:T(8,128)S(1)}, u32[]{:S(2)}) copy-start(f32[256,128]{1,0:T(8,128)S(1)} %get-tuple-element.79.refs_16_) | copy-start | bytes 393220
  155.1 30.4 %copy-start.18 = (f32[256,128]{1,0:T(8,128)}, f32[256,128]{1,0:T(8,128)S(1)}, u32[]{:S(2)}) copy-start(f32[256,128]{1,0:T(8,128)S(1)} %collective-permute-done.8.refs_10_) | copy-start | bytes 393220
  155.1 5.0 %collective-permute-start.9 = (f32[256,128]{1,0:T(8,128)S(1)}, f32[256,128]{1,0:T(8,128)S(1)}, u32[]{:S(2)}, u32[]{:S(2)}) collective-permute-start(f32[256,128]{1,0:T(8,128)S(1)} %collective-permute-done.8.refs_10_), channel_id=1, source_target_pairs={{0,2},{1,3},{2,0},{3,1},{4,6},{5,7},{6,4},{7,5},{8,10},{9,11},{10,... | collective-permute-start | bytes 393224 | tf_op jit(solution)/shard_map/ppermute | solution.py:48
  158.2 27.4 %copy-start.19 = (f32[256,128]{1,0:T(8,128)}, f32[256,128]{1,0:T(8,128)S(1)}, u32[]{:S(2)}) copy-start(f32[256,128]{1,0:T(8,128)S(1)} %collective-permute-done.7.refs_9_) | copy-start | bytes 393220
  158.2 5.3 %collective-permute-start.18 = (f32[256,128]{1,0:T(8,128)S(1)}, f32[256,128]{1,0:T(8,128)S(1)}, u32[]{:S(2)}, u32[]{:S(2)}) collective-permute-start(f32[256,128]{1,0:T(8,128)S(1)} %get-tuple-element.78.refs_20_), channel_id=1, source_target_pairs={{0,2},{1,3},{2,0},{3,1},{4,6},{5,7},{6,4},{7,5},{8,10},{9,11},{10,... | collective-permute-start | bytes 393224 | tf_op jit(solution)/shard_map/ppermute | solution.py:48
  159.4 26.2 %copy-start.20 = (f32[256,128]{1,0:T(8,128)}, f32[256,128]{1,0:T(8,128)S(1)}, u32[]{:S(2)}) copy-start(f32[256,128]{1,0:T(8,128)S(1)} %collective-permute-done.12.refs_15_) | copy-start | bytes 393220
  159.4 9.9 %collective-permute-start.20 = (f32[512,128]{1,0:T(8,128)S(1)}, f32[512,128]{1,0:T(8,128)S(1)}, u32[]{:S(2)}, u32[]{:S(2)}) collective-permute-start(f32[512,128]{1,0:T(8,128)S(1)} %collective-permute-done.13), channel_id=1, source_target_pairs={{0,4},{1,5},{2,6},{3,7},{4,8},{5,9},{6,10},{7,11},{8,12},{9,13},{1... | collective-permute-start | bytes 786440 | tf_op jit(solution)/shard_map/ppermute | solution.py:48
  160.1 25.5 %copy-start.21 = (f32[256,128]{1,0:T(8,128)}, f32[256,128]{1,0:T(8,128)S(1)}, u32[]{:S(2)}) copy-start(f32[256,128]{1,0:T(8,128)S(1)} %collective-permute-done.9.refs_11_) | copy-start | bytes 393220
  160.1 5.0 %collective-permute-start.17 = (f32[256,128]{1,0:T(8,128)S(1)}, f32[256,128]{1,0:T(8,128)S(1)}, u32[]{:S(2)}, u32[]{:S(2)}) collective-permute-start(f32[256,128]{1,0:T(8,128)S(1)} %get-tuple-element.78.refs_20_), channel_id=1, source_target_pairs={{0,1},{1,0},{2,3},{3,2},{4,5},{5,4},{6,7},{7,6},{8,9},{9,8},{10,11... | collective-permute-start | bytes 393224 | tf_op jit(solution)/shard_map/ppermute | solution.py:48
  163.5 22.1 %copy-start.22 = (f32[256,128]{1,0:T(8,128)}, f32[256,128]{1,0:T(8,128)S(1)}, u32[]{:S(2)}) copy-start(f32[256,128]{1,0:T(8,128)S(1)} %collective-permute-done.18.refs_22_) | copy-start | bytes 393220
  163.5 5.0 %collective-permute-start.15 = (f32[256,128]{1,0:T(8,128)S(1)}, f32[256,128]{1,0:T(8,128)S(1)}, u32[]{:S(2)}, u32[]{:S(2)}) collective-permute-start(f32[256,128]{1,0:T(8,128)S(1)} %get-tuple-element.79.refs_16_), channel_id=1, source_target_pairs={{0,1},{1,0},{2,3},{3,2},{4,5},{5,4},{6,7},{7,6},{8,9},{9,8},{10,11... | collective-permute-start | bytes 393224 | tf_op jit(solution)/shard_map/ppermute | solution.py:48
  165.1 20.5 %copy-start.23 = (f32[256,128]{1,0:T(8,128)}, f32[256,128]{1,0:T(8,128)S(1)}, u32[]{:S(2)}) copy-start(f32[256,128]{1,0:T(8,128)S(1)} %collective-permute-done.17.refs_21_) | copy-start | bytes 393220
  165.1 5.5 %collective-permute-start.14 = (f32[256,128]{1,0:T(8,128)S(1)}, f32[256,128]{1,0:T(8,128)S(1)}, u32[]{:S(2)}, u32[]{:S(2)}) collective-permute-start(f32[256,128]{1,0:T(8,128)S(1)} %get-tuple-element.79.refs_16_), channel_id=1, source_target_pairs={{0,2},{1,3},{2,0},{3,1},{4,6},{5,7},{6,4},{7,5},{8,10},{9,11},{10,... | collective-permute-start | bytes 393224 | tf_op jit(solution)/shard_map/ppermute | solution.py:48
  168.5 17.2 %copy-start.24 = (f32[256,128]{1,0:T(8,128)}, f32[256,128]{1,0:T(8,128)S(1)}, u32[]{:S(2)}) copy-start(f32[256,128]{1,0:T(8,128)S(1)} %collective-permute-done.15.refs_18_) | copy-start | bytes 393220
  168.5 5.2 %collective-permute-start.19 = (f32[256,128]{1,0:T(8,128)S(1)}, f32[256,128]{1,0:T(8,128)S(1)}, u32[]{:S(2)}, u32[]{:S(2)}) collective-permute-start(f32[256,128]{1,0:T(8,128)S(1)} %collective-permute-done.18.refs_22_), channel_id=1, source_target_pairs={{0,1},{1,0},{2,3},{3,2},{4,5},{5,4},{6,7},{7,6},{8,9},{9,8},{10,11... | collective-permute-start | bytes 393224 | tf_op jit(solution)/shard_map/ppermute | solution.py:48
  169.4 5.7 %collective-permute-start.16 = (f32[256,128]{1,0:T(8,128)S(1)}, f32[256,128]{1,0:T(8,128)S(1)}, u32[]{:S(2)}, u32[]{:S(2)}) collective-permute-start(f32[256,128]{1,0:T(8,128)S(1)} %collective-permute-done.15.refs_18_), channel_id=1, source_target_pairs={{0,2},{1,3},{2,0},{3,1},{4,6},{5,7},{6,4},{7,5},{8,10},{9,11},{10,... | collective-permute-start | bytes 393224 | tf_op jit(solution)/shard_map/ppermute | solution.py:48
  170.6 15.0 %copy-start.8 = (f32[256,128]{1,0:T(8,128)}, f32[256,128]{1,0:T(8,128)S(1)}, u32[]{:S(2)}) copy-start(f32[256,128]{1,0:T(8,128)S(1)} %get-tuple-element.76.refs_28_) | copy-start | bytes 393220
  170.6 15.0 %copy-start.9 = (f32[256,128]{1,0:T(8,128)}, f32[256,128]{1,0:T(8,128)S(1)}, u32[]{:S(2)}) copy-start(f32[256,128]{1,0:T(8,128)S(1)} %get-tuple-element.77.refs_24_) | copy-start | bytes 393220
  170.6 15.0 %copy-start.25 = (f32[256,128]{1,0:T(8,128)}, f32[256,128]{1,0:T(8,128)S(1)}, u32[]{:S(2)}) copy-start(f32[256,128]{1,0:T(8,128)S(1)} %collective-permute-done.14.refs_17_) | copy-start | bytes 393220
  170.7 6.9 %collective-permute-start.25 = (f32[256,128]{1,0:T(8,128)S(1)}, f32[256,128]{1,0:T(8,128)S(1)}, u32[]{:S(2)}, u32[]{:S(2)}) collective-permute-start(f32[256,128]{1,0:T(8,128)S(1)} %get-tuple-element.76.refs_28_), channel_id=1, source_target_pairs={{0,2},{1,3},{2,0},{3,1},{4,6},{5,7},{6,4},{7,5},{8,10},{9,11},{10,... | collective-permute-start | bytes 393224 | tf_op jit(solution)/shard_map/ppermute | solution.py:48
  173.7 12.0 %copy-start.26 = (f32[256,128]{1,0:T(8,128)}, f32[256,128]{1,0:T(8,128)S(1)}, u32[]{:S(2)}) copy-start(f32[256,128]{1,0:T(8,128)S(1)} %collective-permute-done.19.refs_23_) | copy-start | bytes 393220
  173.7 5.1 %collective-permute-start.24 = (f32[256,128]{1,0:T(8,128)S(1)}, f32[256,128]{1,0:T(8,128)}, u32[]{:S(2)}, u32[]{:S(2)}) collective-permute-start(f32[256,128]{1,0:T(8,128)S(1)} %get-tuple-element.76.refs_28_), channel_id=1, source_target_pairs={{0,1},{1,0},{2,3},{3,2},{4,5},{5,4},{6,7},{7,6},{8,9},{9,8},{10,11... | collective-permute-start | bytes 393224 | tf_op jit(solution)/shard_map/ppermute | solution.py:48
  175.1 10.6 %copy-start.27 = (f32[256,128]{1,0:T(8,128)}, f32[256,128]{1,0:T(8,128)S(1)}, u32[]{:S(2)}) copy-start(f32[256,128]{1,0:T(8,128)S(1)} %collective-permute-done.16.refs_19_) | copy-start | bytes 393220
  175.1 5.1 %collective-permute-start.22 = (f32[256,128]{1,0:T(8,128)S(1)}, f32[256,128]{1,0:T(8,128)}, u32[]{:S(2)}, u32[]{:S(2)}) collective-permute-start(f32[256,128]{1,0:T(8,128)S(1)} %get-tuple-element.77.refs_24_), channel_id=1, source_target_pairs={{0,1},{1,0},{2,3},{3,2},{4,5},{5,4},{6,7},{7,6},{8,9},{9,8},{10,11... | collective-permute-start | bytes 393224 | tf_op jit(solution)/shard_map/ppermute | solution.py:48
  177.5 8.2 %copy-start.28 = (f32[256,128]{1,0:T(8,128)}, f32[256,128]{1,0:T(8,128)S(1)}, u32[]{:S(2)}) copy-start(f32[256,128]{1,0:T(8,128)S(1)} %collective-permute-done.25.refs_30_) | copy-start | bytes 393220
  177.5 5.9 %collective-permute-start.21 = (f32[256,128]{1,0:T(8,128)S(1)}, f32[256,128]{1,0:T(8,128)}, u32[]{:S(2)}, u32[]{:S(2)}) collective-permute-start(f32[256,128]{1,0:T(8,128)S(1)} %get-tuple-element.77.refs_24_), channel_id=1, source_target_pairs={{0,2},{1,3},{2,0},{3,1},{4,6},{5,7},{6,4},{7,5},{8,10},{9,11},{10,... | collective-permute-start | bytes 393224 | tf_op jit(solution)/shard_map/ppermute | solution.py:48
  178.8 5.1 %collective-permute-start.26 = (f32[256,128]{1,0:T(8,128)S(1)}, f32[256,128]{1,0:T(8,128)}, u32[]{:S(2)}, u32[]{:S(2)}) collective-permute-start(f32[256,128]{1,0:T(8,128)S(1)} %collective-permute-done.25.refs_30_), channel_id=1, source_target_pairs={{0,1},{1,0},{2,3},{3,2},{4,5},{5,4},{6,7},{7,6},{8,9},{9,8},{10,11... | collective-permute-start | bytes 393224 | tf_op jit(solution)/shard_map/ppermute | solution.py:48
  180.2 5.3 %collective-permute-start.23 = (f32[256,128]{1,0:T(8,128)}, f32[256,128]{1,0:T(8,128)}, u32[]{:S(2)}, u32[]{:S(2)}) collective-permute-start(f32[256,128]{1,0:T(8,128)} %collective-permute-done.22.refs_26_), channel_id=1, source_target_pairs={{0,2},{1,3},{2,0},{3,1},{4,6},{5,7},{6,4},{7,5},{8,10},{9,11},{10,... | collective-permute-start | bytes 393224 | tf_op jit(solution)/shard_map/ppermute | solution.py:48
  227.0 78.5 %collective-permute-start.28 = (f32[512,512]{1,0:T(8,128)S(1)}, f32[512,512]{1,0:T(8,128)S(1)}, u32[]{:S(2)}, u32[]{:S(2)}) collective-permute-start(f32[512,512]{1,0:T(8,128)S(1)} %get-tuple-element.74), channel_id=1, source_target_pairs={{0,16},{16,0},{1,17},{17,1},{2,18},{18,2},{3,19},{19,3},{4,20},{20... | collective-permute-start | bytes 3145736 | tf_op jit(solution)/shard_map/ppermute | solution.py:329
  244.8 60.7 %collective-permute-start.29 = (f32[512,512]{1,0:T(8,128)}, f32[512,512]{1,0:T(8,128)S(1)}, u32[]{:S(2)}, u32[]{:S(2)}) collective-permute-start(f32[512,512]{1,0:T(8,128)} %get-tuple-element.72), channel_id=1, source_target_pairs={{0,16},{16,0},{1,17},{17,1},{2,18},{18,2},{3,19},{19,3},{4,20},{20... | collective-permute-start | bytes 3145736 | tf_op jit(solution)/shard_map/ppermute | solution.py:329
  305.5 1.0 copy-start
  305.6 1.4 copy-start.1
Sparse Core Ops, SparseCore 0:
  11.3 115.5 all-gather.1

commit v2 on v1

v2 whole, which is shorter than its diff:
```python
import functools

import jax
import jax.numpy as jnp
from jax import lax
from jax.experimental import pallas as pl
from jax.experimental.pallas import tpu as pltpu
from jax.sharding import PartitionSpec as P

NB = 1024
F32 = jnp.float32
BF16 = jnp.bfloat16
MIB = 1024 * 1024


def grid_of(count):
    z_size = 4
    side = 1
    while side * side * z_size < count:
        side += 1
    return z_size, side, side


def split(value):
    high = value.astype(BF16)
    return high, (value - high.astype(F32)).astype(BF16)


NN = ((1,), (0,))
NT = ((1,), (1,))


def mul3(left, right, dims):
    left = jnp.concatenate([left[0], left[0], left[1]], axis=1)
    right = jnp.concatenate([right[0], right[1], right[0]], axis=dims[1][0])
    return lax.dot_general(left, right, (dims, ((), ())), preferred_element_type=F32)


def gate(wanted, *others):
    return lax.optimization_barrier((wanted, others))[0]


def shift(value, sizes, axis, step):
    z_size, y_size, x_size = sizes
    pairs = []
    for z in range(z_size):
        for y in range(y_size):
            for x in range(x_size):
                at = [z, y, x]
                to = list(at)
                to[axis] = (at[axis] + step) % sizes[axis]
                pairs.append(tuple((c[0] * y_size + c[1]) * x_size + c[2] for c in (at, to)))
    return lax.ppermute(value, "pcol", pairs)


def ring(value, sizes, axis):
    held = [value]
    for _ in range(sizes[axis] - 1):
        held.append(shift(held[-1], sizes, axis, 1))
    return held


def gather_across(layers, sizes):
    half = layers[0].shape[0] // 2
    upper = jnp.concatenate([held[:half] for held in layers], axis=0)
    lower = jnp.concatenate([held[half:] for held in layers], axis=0)
    return jnp.concatenate(ring(upper, sizes, 2), axis=0), jnp.concatenate(ring(lower, sizes, 1), axis=0)


def gather_along(across, sizes):
    return ring(across[0], sizes, 1) + ring(across[1], sizes, 2)


def gathered_places(first_layer, layers, half, sizes):
    places = []
    for dy in range(sizes[1]):
        inner = [((dx * layers + d) * half, 0, (first_layer + d, dy, dx)) for dx in range(sizes[2]) for d in range(layers)]
        places.append(inner)
    for dx in range(sizes[2]):
        inner = [((dy * layers + d) * half, half, (first_layer + d, dy, dx)) for dy in range(sizes[1]) for d in range(layers)]
        places.append(inner)
    return places


def source_tiles(sizes, index):
    z_size, y_size, x_size = sizes
    z, y, x = index // (y_size * x_size), index // x_size % y_size, index % x_size
    places = jnp.arange(z_size * y_size * x_size)
    dz, dy, dx = places // (y_size * x_size), places // x_size % y_size, places % x_size
    return ((z - dz) % z_size * y_size + (y - dy) % y_size) * x_size + (x - dx) % x_size


def slot_of(place, sizes):
    return (place[0] * sizes[1] + place[1]) * sizes[2] + place[2]


def permute_columns(arrays, places, half, sizes, tiles, wanted, rows):
    count = sizes[0] * sizes[1] * sizes[2]
    width = wanted.shape[0]
    step = 256
    depth = count * 128

    def kernel(tiles_ref, wanted_ref, *refs):
        parts, outs, (both_ref, hot_ref) = refs[:-5], refs[-5:-2], refs[-2:]
        for part, inner in zip(parts, places, strict=True):
            for start, first, place in inner:
                high, low = split(part[pl.ds(start, half), :])
                lanes = pl.ds(slot_of(place, sizes) * 128, 128)
                both_ref[pl.ds(first, half), lanes] = high
                both_ref[pl.ds(rows + first, half), lanes] = low
        for start in range(0, width, step):
            size = min(step, width - start)
            columns = wanted_ref[:, pl.ds(start, size)]
            lane = lax.broadcasted_iota(jnp.int32, (128, size), 0)
            for slot in range(count):
                hot = (columns - tiles_ref[slot] * 128) == lane
                hot_ref[pl.ds(slot * 128, 128), pl.ds(0, size)] = hot.astype(F32).astype(BF16)
            got = jnp.dot(both_ref[...], hot_ref[:, pl.ds(0, size)], preferred_element_type=F32)
            outs[start // NB][:, pl.ds(start % NB, size)] = got[:rows] + got[rows:]

    vmem = pl.BlockSpec(memory_space=pltpu.VMEM)
    return pl.pallas_call(
        kernel,
        out_shape=[jax.ShapeDtypeStruct((rows, size), F32) for size in (NB, NB, width - 2 * NB)],
        in_specs=[pl.BlockSpec(memory_space=pltpu.SMEM), vmem] + [vmem] * len(arrays),
        out_specs=[vmem] * 3,
        scratch_shapes=[pltpu.VMEM((2 * rows, depth), BF16), pltpu.VMEM((depth, step), BF16)],
        compiler_params=pltpu.CompilerParams(vmem_limit_bytes=22 * MIB),
        cost_estimate=pl.CostEstimate(flops=4 * rows * depth * width, transcendentals=0, bytes_accessed=8 * rows * depth),
        name="permute_columns",
    )(tiles, wanted.reshape(1, width), *arrays)


def prepare(block, keep, step, name):
    cycles, depth, tiles, width = block.shape
    cycles //= 2

    def kernel(keep_ref, in_ref, high_ref, low_ref):
        own = keep_ref[step]
        for b in range(tiles):
            value = in_ref[0, pl.ds(b, depth, stride=tiles), :]
            if b == 0:
                value = jnp.where(own > 0, value, jnp.zeros_like(value))
            high, low = split(value)
            high_ref[:, pl.ds(b * width, width)] = high
            low_ref[:, pl.ds(b * width, width)] = low

    out = pltpu.HBM((cycles * depth, tiles * width), BF16)
    spec = pl.BlockSpec((depth, tiles * width), lambda a: (a, 0))
    return pl.pallas_call(
        kernel,
        grid=(cycles,),
        out_shape=(out, out),
        in_specs=[
            pl.BlockSpec(memory_space=pltpu.SMEM),
            pl.BlockSpec((1, depth * tiles, width), lambda a: (a + step * cycles, 0, 0)),
        ],
        out_specs=(spec, spec),
        compiler_params=pltpu.CompilerParams(vmem_limit_bytes=12 * MIB),
        cost_estimate=pl.CostEstimate(flops=0, transcendentals=0, bytes_accessed=12 * cycles * depth * tiles * width),
        name=name,
    )(keep, block.reshape(2 * cycles, depth * tiles, width))


def load_blocks(group, tiles_ref, parts, sizes, high_ref, low_ref):
    arrays, places, size, where = group
    half = NB // 2
    at = 0
    for pair, inner in zip(arrays, places, strict=True):
        for side in range(len(pair)):
            part = parts[at]
            if len(part.shape) == 3:
                part = part.reshape(part.shape[0] * part.shape[1], 128)
            at += 1
            for start, first, place in inner:
                belongs, tile, row = where(tiles_ref[slot_of(place, sizes)], first)

                def put(part=part, start=start, tile=tile, row=row, side=side):
                    high, low = split(part[pl.ds(start, size), :])
                    rows_to = pl.ds(pl.multiple_of(row + side * half, 128), size)
                    high_ref[tile, rows_to, :] = high
                    low_ref[tile, rows_to, :] = low

                if sizes[0] * sizes[1] * sizes[2] * 128 <= 2 * NB:
                    put()
                else:
                    pl.when(belongs)(put)


def block_specs(operands, chosen):
    if chosen is None:
        return [pl.BlockSpec(memory_space=pltpu.VMEM)] * len(operands)
    chips, depth, width = operands[0].shape
    spec = pl.BlockSpec((chips, depth // 2, width), lambda i: (0, chosen, 0), pipeline_mode=pl.Buffered(1))
    return [spec] * len(operands)


def solve(tiles, rhs, sizes, diagonal, name, chosen=None):
    rows = rhs.shape[0]
    per_block = NB // 128
    half = NB // 2
    step = 256
    operands = [array for pair in diagonal[0] for array in pair]

    def kernel(tiles_ref, rhs_ref, *refs):
        parts = refs[: len(operands)]
        own_ref, other_ref, out_high, out_low, high_ref, low_ref = refs[len(operands) :]
        load_blocks(diagonal, tiles_ref, parts, sizes, high_ref, low_ref)
        left = split(rhs_ref[...])
        for start in range(0, NB, step):
            wanted = pl.ds(start, step)
            right = tuple(jnp.concatenate([r[t, wanted, :] for t in range(per_block)], axis=1) for r in (high_ref, low_ref))
            value = mul3(left, right, NT)
            out_high[:, wanted], out_low[:, wanted] = split(value)
            to = own_ref if start < half else other_ref
            to[:, pl.ds(start % half, step)] = value

    vmem = pl.BlockSpec(memory_space=pltpu.VMEM)
    f32 = jax.ShapeDtypeStruct((rows, half), F32)
    b16 = jax.ShapeDtypeStruct((rows, NB), BF16)
    return pl.pallas_call(
        kernel,
        out_shape=(f32, f32, b16, b16),
        grid=(1,),
        in_specs=[pl.BlockSpec(memory_space=pltpu.SMEM), vmem, *block_specs(operands, chosen)],
        out_specs=(vmem,) * 4,
        scratch_shapes=[pltpu.VMEM((per_block, NB, 128), BF16)] * 2,
        compiler_params=pltpu.CompilerParams(vmem_limit_bytes=24 * MIB),
        cost_estimate=pl.CostEstimate(flops=6 * rows * NB * NB, transcendentals=0, bytes_accessed=8 * NB * NB),
        name=name,
    )(tiles, rhs, *operands)


def couple(tiles, rhs, sizes, solved, coupling, chosen):
    rows = rhs.shape[0]
    per_block = NB // 128
    operands = [array for pair in coupling[0] for array in pair]

    def kernel(tiles_ref, rhs_ref, yh_ref, yl_ref, *refs):
        parts, (out_ref, high_ref, low_ref) = refs[: len(operands)], refs[len(operands) :]
        load_blocks(coupling, tiles_ref, parts, sizes, high_ref, low_ref)
        left = (yh_ref[...], yl_ref[...])
        for t in range(0, per_block, 2):
            to = (slice(None), pl.ds(t * 128, 256))
            right = tuple(jnp.concatenate([r[t], r[t + 1]], axis=1) for r in (high_ref, low_ref))
            out_ref[to] = rhs_ref[to] - mul3(left, right, NN)

    vmem = pl.BlockSpec(memory_space=pltpu.VMEM)
    return pl.pallas_call(
        kernel,
        out_shape=jax.ShapeDtypeStruct((rows, NB), F32),
        grid=(1,),
        in_specs=[pl.BlockSpec(memory_space=pltpu.SMEM), vmem, vmem, vmem, *block_specs(operands, chosen)],
        out_specs=vmem,
        scratch_shapes=[pltpu.VMEM((per_block, NB, 128), BF16)] * 2,
        compiler_params=pltpu.CompilerParams(vmem_limit_bytes=22 * MIB),
        cost_estimate=pl.CostEstimate(flops=6 * rows * NB * NB, transcendentals=0, bytes_accessed=8 * NB * NB),
        name="couple",
    )(tiles, rhs, *solved, *operands)


def in_hbm(arrays):
    return [pltpu.with_memory_space_constraint(array, pltpu.HBM) for array in arrays]


def trail_specs(rows, wide):
    whole = pl.BlockSpec((rows, NB), lambda i: (0, 0))
    part = pl.BlockSpec((NB // 2, wide), lambda i: (0, i))
    return [whole, whole, part, part, part, part]


def trail_change(refs, to):
    yh_ref, yl_ref, ah_ref, al_ref, bh_ref, bl_ref = refs
    high = jnp.concatenate([ah_ref[to], bh_ref[to]], axis=0)
    low = jnp.concatenate([al_ref[to], bl_ref[to]], axis=0)
    return mul3((yh_ref[...], yl_ref[...]), (high, low), NN)


def trail_cost(rows, tiles):
    return pl.CostEstimate(flops=6 * rows * NB * tiles * 128, transcendentals=0, bytes_accessed=(8 * rows + 4 * NB) * tiles * 128)


def trail_first(sensitivity, own_tile, solved, halves):
    rows, tiles, width = sensitivity.shape
    group = 8

    def kernel(sens_ref, own_ref, *refs):
        refs, out_ref = refs[:-1], refs[-1]
        sens_ref = sens_ref.reshape(rows * group, width)
        first = pl.program_id(0) == 0
        for b in range(0, group, 2):
            to = (slice(None), pl.ds(b * width, 2 * width))
            parts = []
            for c in (b, b + 1):
                part = sens_ref[pl.ds(c, rows, stride=group), :]
                if c == 0:
                    part = jnp.where(first, own_ref[...], part)
                parts.append(part)
            out_ref[to] = jnp.concatenate(parts, axis=1) - trail_change(refs, to)

    wide = group * width
    return pl.pallas_call(
        kernel,
        grid=(tiles // group,),
        out_shape=pltpu.HBM((rows, tiles * width), F32),
        in_specs=[
            pl.BlockSpec((rows, group, width), lambda i: (0, i, 0)),
            pl.BlockSpec((rows, width), lambda i: (0, 0)),
            *trail_specs(rows, wide),
        ],
        out_specs=pl.BlockSpec((rows, wide), lambda i: (0, i)),
        compiler_params=pltpu.CompilerParams(vmem_limit_bytes=24 * MIB),
        cost_estimate=trail_cost(rows, tiles),
        name="trail_first",
    )(*in_hbm([sensitivity]), own_tile, *solved, *in_hbm(halves))


def trail_second(partial, solved, halves, tiles):
    rows = partial.shape[0]
    width = 128
    group = 8

    def kernel(in_ref, *refs):
        refs, out_ref = refs[:-1], refs[-1].reshape(rows * group, width)
        for b in range(0, group, 2):
            to = (slice(None), pl.ds(b * width, 2 * width))
            value = in_ref[to] - trail_change(refs, to)
            out_ref[pl.ds(b, rows, stride=group), :] = value[:, :width]
            out_ref[pl.ds(b + 1, rows, stride=group), :] = value[:, width:]

    wide = group * width
    return pl.pallas_call(
        kernel,
        grid=(tiles // group,),
        out_shape=jax.ShapeDtypeStruct((rows, tiles, width), F32),
        in_specs=[pl.BlockSpec((rows, wide), lambda i: (0, i)), *trail_specs(rows, wide)],
        out_specs=pl.BlockSpec((rows, group, width), lambda i: (0, i, 0)),
        compiler_params=pltpu.CompilerParams(vmem_limit_bytes=24 * MIB),
        cost_estimate=trail_cost(rows, tiles),
        name="trail_second",
    )(*in_hbm([partial]), *solved, *in_hbm(halves))


def place_unknowns(core, parts):
    rows, half = parts[0].shape
    per_step = half // 128
    cycles = 2 * per_step

    def kernel(core_ref, *refs):
        out_ref = refs[-1].reshape(rows * cycles, 128)
        own = pl.program_id(0) == core_ref[0]
        for chosen, wanted in ((refs[0:2], own), (refs[2:4], jnp.logical_not(own))):

            @pl.when(wanted)
            def _(chosen=chosen):
                for step in range(2):
                    for a in range(per_step):
                        out_ref[pl.ds(step * per_step + a, rows, stride=cycles), :] = chosen[step][:, pl.ds(a * 128, 128)]

    spec = pl.BlockSpec((rows, half), lambda i, core_ref: (0, 0))
    return pl.pallas_call(
        kernel,
        out_shape=jax.ShapeDtypeStruct((2 * rows, cycles, 128), F32),
        grid_spec=pltpu.PrefetchScalarGridSpec(
            num_scalar_prefetch=1,
            grid=(2,),
            in_specs=[spec] * 4,
            out_specs=pl.BlockSpec((rows, cycles, 128), lambda i, core_ref: (i, 0, 0)),
        ),
        compiler_params=pltpu.CompilerParams(vmem_limit_bytes=18 * MIB),
        name="place_unknowns",
    )(core, parts[0], parts[2], parts[1], parts[3])


def shards(factor_rows, sensitivity, pivots):
    count = lax.axis_size("pcol")
    sizes = grid_of(count)
    cycles, width, col_tiles = factor_rows.shape[:3]
    rows = sensitivity.shape[0]
    per_block = NB // width
    half = NB // 2
    quarter = half // 2
    index = lax.axis_index("pcol")
    core = lax.axis_index("prow")
    tiles = source_tiles(sizes, index)
    swap = lambda value: lax.ppermute(value, "prow", [(0, 1), (1, 0)])
    step_z = lambda value: shift(value, sizes, 0, 1)
    keep = jnp.stack([index >= per_block, index >= 2 * per_block]).astype(jnp.int32)
    own_columns = lax.dynamic_slice(pivots, (index * width,), (width,))

    stripe_layers = [sensitivity[:, 0, :]]
    corner = factor_rows[:, :, 0, :].reshape(cycles * width, width)
    partners = [(j, j + per_block) for j in range(per_block)] + [(j + per_block, j) for j in range(per_block)]
    shared = jnp.concatenate([corner[quarter:half], corner[half + quarter :]], axis=0)
    received = lax.ppermute(shared, "pcol", partners)
    stripe_layers.append(step_z(stripe_layers[0]))
    other_rows = swap(factor_rows)
    stripe_layers, received, keep = gate((stripe_layers, received, keep))
    first = index < per_block
    diag0 = [jnp.where(first, corner[:quarter], received[:quarter])]
    late = jnp.concatenate(
        [
            jnp.where(first, received[:quarter], corner[:quarter]),
            jnp.where(first, received[quarter:], corner[half : half + quarter]),
        ],
        axis=0,
    )
    late = lax.all_gather(late, "pcol", axis=0)[: 2 * per_block]

    across = gather_across(stripe_layers[:1], sizes)
    stripe_layers.append(step_z(stripe_layers[1]))
    diag0.append(step_z(diag0[0]))
    own0 = prepare(factor_rows, keep, 0, "prepare_own_first")
    stripe_layers, across, keep, diag0 = gate((stripe_layers, across, keep, diag0), own0)

    arrays = [gather_along(across, sizes)]
    across = gather_across(stripe_layers[1:2], sizes)
    stripe_layers.append(step_z(stripe_layers[2]))
    diag0.append(step_z(diag0[1]))
    stripe_layers, across, diag0 = gate((stripe_layers, across, diag0))

    arrays.append(gather_along(across, sizes))
    across = gather_across(stripe_layers[2:3], sizes)
    diag0.append(step_z(diag0[2]))
    across, diag0, keep = gate((across, diag0, keep), arrays[0])

    arrays.append(gather_along(across, sizes))
    across = gather_across(stripe_layers[3:4], sizes)
    across, diag0 = gate((across, diag0), arrays[1])

    arrays.append(gather_along(across, sizes))
    diag_across = gather_across(diag0, sizes)
    other0 = prepare(other_rows, keep, 0, "prepare_other_first")
    diag_across, pivots, keep = gate((diag_across, pivots, keep), arrays, other0)

    diag_arrays = gather_along(diag_across, sizes)
    stripe_places = [p for d in range(sizes[0]) for p in gathered_places(d, 1, rows // 2, sizes)]
    stripe_arrays = [array for layer in arrays for array in layer]
    wanted = jnp.concatenate([pivots[: 2 * NB], own_columns])
    stripe = permute_columns(stripe_arrays, stripe_places, rows // 2, sizes, tiles, wanted, rows)
    rhs0, rhs1, own_tile = stripe
    diag_arrays, keep = gate((diag_arrays, keep), rhs0)
    diag_pairs = [(array, swap(array)) for array in diag_arrays]

    block_places = gathered_places(0, sizes[0], quarter // 2, sizes)
    own1 = prepare(factor_rows, keep, 1, "prepare_own_second")
    other1 = prepare(other_rows, keep, 1, "prepare_other_second")

    def first_rows(tile, row):
        return tile < 2 * per_block, tile % per_block, row + jnp.where(tile < per_block, 0, quarter)

    def second_rows(tile, row):
        return tile < 2 * per_block, tile % per_block, row + jnp.where(tile < per_block, quarter, 0)

    own_y0, other_y0, *y0 = solve(
        tiles, rhs0, sizes, (diag_pairs, block_places, quarter // 2, first_rows), "solve_first"
    )

    late = gate(late, y0, own1, other1)
    late_pairs = [(late, swap(late))]
    late_places = [[(j * quarter, 0, (0, 0, j)) for j in range(2 * per_block)]]
    late_group = (late_pairs, late_places, quarter, second_rows)
    in_order = jnp.arange(2 * per_block)
    partial = trail_first(sensitivity, own_tile, y0, (*own0, *other0))
    rhs1 = couple(in_order, rhs1, sizes, y0, late_group, 0)
    own_y1, other_y1, *y1 = solve(in_order, gate(rhs1, partial), sizes, late_group, "solve_second", 1)
    updated = trail_second(partial, y1, (*own1, *other1), col_tiles)

    parts = [own_y0, swap(other_y0), own_y1, swap(other_y1)]
    adjoint = place_unknowns(core.reshape(1).astype(jnp.int32), parts)
    return adjoint, updated


def solution(mesh):
    return jax.shard_map(
        shards,
        mesh=mesh,
        in_specs=(P(None, "prow", None, "pcol"), P("prow", None, "pcol"), P()),
        out_specs=(P(None, None, "prow"), P("prow", None, "pcol")),
        check_vma=False,
    )
```

time: 319 us -> 224 us (0.70)
  waiting for transfers between devices: 142 us -> 53 us
  Pallas kernels: 102 us -> 82.6 us
  starting transfers between devices: 27.7 us -> 35.9 us
  local copies, waits for them, and re-layouts: 31.1 us -> 35.7 us
    all_gather x1, waiting for transfers between devices: 116 us -> 0.01 us  [shards(): late = lax.all_gather(late, 'pcol', axis=0)[:2 * per_block]]
    unnamed x58 -> x78, local copies, waits for them, and re-layouts: 1.46 us -> 25.2 us
    ppermute x0 -> x1, waiting for transfers between devices: none -> 14.8 us  [shards(): received = lax.ppermute(shared, 'pcol', partners)]
    squeeze x4 -> x0, local copies, waits for them, and re-layouts: 14.1 us -> none  [the longest x2 9.35 us: shards(): second_diag.append((block[per_block + j, half:], side * half, j))]
    pallas_call x4 -> x5, Pallas kernels: 55.3 us -> 41.9 us  [the longest x1 15.1 us: trail_first(): pl.pallas_call(kernel, grid=(tiles // group,), out_shape=pltpu.HBM((rows,...]
    ppermute x27 -> x26, waiting for transfers between devices: 25.7 us -> 38.2 us  [shift(): return lax.ppermute(value, 'pcol', pairs)]
    slice x9 -> x10, local copies, waits for them, and re-layouts: 14.2 us -> 7 us  [the longest x8 2.78 us: gather_across(): lower = jnp.concatenate([held[half:] for held in layers], axis=0)]
    ppermute x0 -> x1, starting transfers between devices: none -> 3.67 us  [shards(): received = lax.ppermute(shared, 'pcol', partners)]
  transfers between devices with their start and end apart: 32 -> 36, of which waited for: 18 -> 14; matrix products, arithmetic and copies ran while one was open for 9% -> 5% of each run, Pallas kernels for 30% -> 35%
where the time goes in v2:
time: 224 us; the launch traced here: 223 us
  Pallas kernels  82.6 us (37%)
  waiting for transfers between devices  53 us (24%)
  starting transfers between devices  35.9 us (16%)
  local copies, waits for them, and re-layouts  35.7 us (16%)
  between operations  14.5 us (6%)
    ppermute x26, waiting for transfers between devices, shift(): return lax.ppermute(value, 'pcol', pairs)  38.2 us
    ppermute x26, starting transfers between devices, shift(): return lax.ppermute(value, 'pcol', pairs)  30.1 us
    unnamed x78, local copies, waits for them, and re-layouts  25.2 us
    pallas_call x4, Pallas kernels, prepare(): pl.pallas_call(kernel, grid=(cycles,), out_shape=(out, out), in_specs=[pl...  22.1 us
    pallas_call x1, Pallas kernels, trail_first(): pl.pallas_call(kernel, grid=(tiles // group,), out_shape=pltpu.HBM((rows,...  15.1 us
    pallas_call x1, Pallas kernels, trail_second(): pl.pallas_call(kernel, grid=(tiles // group,), out_shape=jax.ShapeDtypeSt...  14.8 us
    ppermute x1, waiting for transfers between devices, shards(): received = lax.ppermute(shared, 'pcol', partners)  14.8 us
    pallas_call x1, Pallas kernels, permute_columns(): pl.pallas_call(kernel, out_shape=[jax.ShapeDtypeStruct((rows, size), F32)...  11.4 us
  transfers between devices with their start and end apart: 36, of which 14 were waited for; matrix products, arithmetic and copies ran while one was open for 5% of the time, Pallas kernels for 35%

profile of v2, /device:TPU:0, one launch (start us, length us, event | category | flops | bytes accessed | tf_op | source)
XLA Modules:
  0.0 223.4 jit_solution(4165057633131120111)
XLA Ops:
  7.7 2.5 %fusion.11 = (f32[2,128,1,128]{3,2,1,0:T(1,128)S(1)}, f32[2,128,1,128]{3,2,1,0:T(1,128)S(1)}, f32[2,128,1,128]{3,2,1,0:T(1,128)S(1)}, f32[2,128,1,128]{3,2,1,0:T(1,128)S(1)}) fusion(f32[8,128,24,128]{3,2,1,0:T(8,128)} %param.3), kind=kLoop, calls=%fused_computation.58 | loop fusion | bytes 1048576 | tf_op jit(solution)/shard_map/slice | solution.py:404
  10.2 3.7 %collective-permute-start.1 = (f32[512,128]{1,0:T(8,128)S(1)}, f32[512,128]{1,0:T(8,128)S(1)}, u32[]{:S(2)}, u32[]{:S(2)}) collective-permute-start(f32[512,128]{1,0:T(8,128)S(1)} %pad_maximum_fusion), channel_id=1, source_target_pairs={{0,8},{1,9},{2,10},{3,11},{4,12},{5,13},{6,14},{7,15},{8,0},{9,1},... | collective-permute-start | bytes 786440 | tf_op jit(solution)/shard_map/ppermute | solution.py:395
  13.9 1.7 slice.88
  15.6 1.6 collective-permute-start
  17.4 14.8 %collective-permute-done.1 = f32[512,128]{1,0:T(8,128)S(1)} collective-permute-done((f32[512,128]{1,0:T(8,128)S(1)}, f32[512,128]{1,0:T(8,128)S(1)}, u32[]{:S(2)}, u32[]{:S(2)}) %collective-permute-start.1) | collective-permute-done | bytes 262176 | tf_op jit(solution)/shard_map/ppermute | solution.py:395
  32.9 1.6 collective-permute-start.4
  35.3 1.5 collective-permute-start.3
  36.8 2.5 %collective-permute-start.5 = (f32[256,128]{1,0:T(8,128)S(1)}, f32[256,128]{1,0:T(8,128)S(1)}, u32[]{:S(2)}, u32[]{:S(2)}) collective-permute-start(f32[256,128]{1,0:T(8,128)S(1)} %get-tuple-element.87), channel_id=1, source_target_pairs={{0,4},{1,5},{2,6},{3,7},{4,8},{5,9},{6,10},{7,11},{8,12},{9,13},{1... | collective-permute-start | bytes 393224 | tf_op jit(solution)/shard_map/ppermute | solution.py:53
  39.3 4.9 %copy-done = f32[8,128,24,128]{3,2,1,0:T(8,128)S(1)} copy-done((f32[8,128,24,128]{3,2,1,0:T(8,128)S(1)}, f32[8,128,24,128]{3,2,1,0:T(8,128)}, u32[]{:S(2)}) %copy-start) | copy-done | bytes 12582936
  44.1 4.2 %prepare_own_first.1 = (bf16[512,3072]{1,0:T(8,128)(2,1)}, bf16[512,3072]{1,0:T(8,128)(2,1)}) custom-call(s32[2]{0:T(128)S(1)} %add_convert_fusion.keep_ref, f32[8,3072,128]{2,1,0:T(8,128)S(1)} %bitcast.13), custom_call_target="tpu_custom_call" | custom-call | bytes 18874368 | tf_op jit(solution)/shard_map/prepare_own_first/pallas_call | solution.py:150
  48.9 1.1 collective-permute-start.7
  50.1 2.5 %collective-permute-start.9 = (f32[256,128]{1,0:T(8,128)S(1)}, f32[256,128]{1,0:T(8,128)S(1)}, u32[]{:S(2)}, u32[]{:S(2)}) collective-permute-start(f32[256,128]{1,0:T(8,128)S(1)} %collective-permute-done.5), channel_id=1, source_target_pairs={{0,4},{1,5},{2,6},{3,7},{4,8},{5,9},{6,10},{7,11},{8,12},{9,13},{1... | collective-permute-start | bytes 393224 | tf_op jit(solution)/shard_map/ppermute | solution.py:53
  52.5 0.9 collective-permute-done.8
  54.1 1.2 collective-permute-start.16
  55.3 7.0 %collective-permute-done.9 = f32[256,128]{1,0:T(8,128)S(1)} collective-permute-done((f32[256,128]{1,0:T(8,128)S(1)}, f32[256,128]{1,0:T(8,128)S(1)}, u32[]{:S(2)}, u32[]{:S(2)}) %collective-permute-start.9) | collective-permute-done | bytes 131104 | tf_op jit(solution)/shard_map/ppermute | solution.py:53
  62.4 1.5 collective-permute-start.13
  63.9 1.0 collective-permute-start.12
  65.0 2.6 %collective-permute-done.13 = f32[256,128]{1,0:T(8,128)S(1)} collective-permute-done((f32[256,128]{1,0:T(8,128)S(1)}, f32[256,128]{1,0:T(8,128)S(1)}, u32[]{:S(2)}, u32[]{:S(2)}) %collective-permute-start.13) | collective-permute-done | bytes 131104 | tf_op jit(solution)/shard_map/ppermute | solution.py:53
  67.6 2.5 %collective-permute-start.11 = (f32[256,128]{1,0:T(8,128)S(1)}, f32[256,128]{1,0:T(8,128)S(1)}, u32[]{:S(2)}, u32[]{:S(2)}) collective-permute-start(f32[256,128]{1,0:T(8,128)S(1)} %get-tuple-element.133), channel_id=1, source_target_pairs={{0,2},{1,3},{2,0},{3,1},{4,6},{5,7},{6,4},{7,5},{8,10},{9,11},{10,... | collective-permute-start | bytes 393224 | tf_op jit(solution)/shard_map/ppermute | solution.py:53
  70.2 1.0 collective-permute-done.12
  71.1 3.1 %collective-permute-done.14 = f32[256,128]{1,0:T(8,128)S(1)} collective-permute-done((f32[256,128]{1,0:T(8,128)S(1)}, f32[256,128]{1,0:T(8,128)S(1)}, u32[]{:S(2)}, u32[]{:S(2)}) %collective-permute-start.14) | collective-permute-done | bytes 131104 | tf_op jit(solution)/shard_map/ppermute | solution.py:53
  74.3 0.8 collective-permute-start.18
  75.9 3.4 %collective-permute-done.10 = f32[256,128]{1,0:T(8,128)S(1)} collective-permute-done((f32[256,128]{1,0:T(8,128)S(1)}, f32[256,128]{1,0:T(8,128)S(1)}, u32[]{:S(2)}, u32[]{:S(2)}) %collective-permute-start.10) | collective-permute-done | bytes 131104 | tf_op jit(solution)/shard_map/ppermute | solution.py:53
  80.0 4.8 %collective-permute-done.18.refs_7_ = f32[512,128]{1,0:T(8,128)S(1)} collective-permute-done((f32[512,128]{1,0:T(8,128)S(1)}, f32[512,128]{1,0:T(8,128)S(1)}, u32[]{:S(2)}, u32[]{:S(2)}) %collective-permute-start.18) | collective-permute-done | bytes 262176 | tf_op jit(solution)/shard_map/ppermute | solution.py:53
  89.0 1.2 collective-permute-start.19
  90.3 1.1 collective-permute-start.21
  91.3 1.0 collective-permute-start.22
  92.3 5.8 %collective-permute-done.20 = f32[512,128]{1,0:T(8,128)} collective-permute-done((f32[512,128]{1,0:T(8,128)S(1)}, f32[512,128]{1,0:T(8,128)}, u32[]{:S(2)}, u32[]{:S(2)}) %collective-permute-start.20) | collective-permute-done | bytes 262176 | tf_op jit(solution)/shard_map/ppermute | solution.py:53
  98.1 1.2 collective-permute-start.23
  99.3 2.2 collective-permute-done.19
  101.6 2.1 collective-permute-start.24
  103.8 1.7 constant_dynamic-update-slice_fusion.5.refs_4_
  105.5 1.7 constant_dynamic-update-slice_fusion.refs_0_
  107.2 7.0 %prepare_other_first.1 = (bf16[512,3072]{1,0:T(8,128)(2,1)}, bf16[512,3072]{1,0:T(8,128)(2,1)}) custom-call(s32[2]{0:T(128)S(1)} %add_convert_fusion.keep_ref, f32[8,3072,128]{2,1,0:T(8,128)} %bitcast.8.in_ref), custom_call_target="tpu_custom_call" | custom-call | bytes 18874368 | tf_op jit(solution)/shard_map/prepare_other_first/pallas_call | solution.py:150
  115.7 2.7 %collective-permute-done.23.refs_13_ = f32[512,128]{1,0:T(8,128)S(1)} collective-permute-done((f32[512,128]{1,0:T(8,128)S(1)}, f32[512,128]{1,0:T(8,128)S(1)}, u32[]{:S(2)}, u32[]{:S(2)}) %collective-permute-start.23) | collective-permute-done | bytes 262176 | tf_op jit(solution)/shard_map/ppermute | solution.py:53
  119.1 3.3 %collective-permute-done.24.refs_15_ = f32[512,128]{1,0:T(8,128)} collective-permute-done((f32[512,128]{1,0:T(8,128)S(1)}, f32[512,128]{1,0:T(8,128)}, u32[]{:S(2)}, u32[]{:S(2)}) %collective-permute-start.24) | collective-permute-done | bytes 262176 | tf_op jit(solution)/shard_map/ppermute | solution.py:53
  122.3 0.9 collective-permute-start.26
  123.3 2.0 collective-permute-start.27
  125.3 0.9 copy-done.9
  126.2 0.9 copy-done.11
  127.2 0.9 copy-done.13
  128.1 0.9 copy-done.20
  129.1 0.9 copy-done.22
  130.0 0.9 copy-done.24
  131.0 0.9 copy-done.26
  131.9 0.9 copy-done.28
  132.9 11.4 %permute_columns.1 = (f32[512,1024]{1,0:T(8,128)S(1)}, f32[512,1024]{1,0:T(8,128)S(1)}, f32[512,128]{1,0:T(8,128)S(1)}) custom-call(s32[16]{0:T(128)S(1)} %fusion.2.tiles_ref, s32[1,2176]{1,0:T(1,128)S(1)} %reshape.25.wanted_ref, f32[512,128]{1,0:T(8,128)S(1)} %pad_maximum_fusion.1.refs_0_, f32[512,128]{1,0:T(8,128)S(1)} %copy-done.16, ...), custom_call_target="tpu_custom_call" | custom-call | flops 9126805504 | bytes 8388608 | tf_op jit(solution)/shard_map/permute_columns/pallas_call | solution.py:122
  146.0 6.6 %prepare_other_second.1 = (bf16[512,3072]{1,0:T(8,128)(2,1)}, bf16[512,3072]{1,0:T(8,128)(2,1)}) custom-call(s32[2]{0:T(128)S(1)} %add_convert_fusion.keep_ref, f32[8,3072,128]{2,1,0:T(8,128)} %bitcast.8.in_ref), custom_call_target="tpu_custom_call" | custom-call | bytes 18874368 | tf_op jit(solution)/shard_map/prepare_other_second/pallas_call | solution.py:150
  152.6 4.3 %prepare_own_second.1 = (bf16[512,3072]{1,0:T(8,128)(2,1)}, bf16[512,3072]{1,0:T(8,128)(2,1)}) custom-call(s32[2]{0:T(128)S(1)} %add_convert_fusion.keep_ref, f32[8,3072,128]{2,1,0:T(8,128)S(1)} %bitcast.16), custom_call_target="tpu_custom_call" | custom-call | bytes 18874368 | tf_op jit(solution)/shard_map/prepare_own_second/pallas_call | solution.py:150
  157.0 5.3 %solve_first.1 = (f32[512,512]{1,0:T(8,128)S(1)}, f32[512,512]{1,0:T(8,128)S(1)}, bf16[512,1024]{1,0:T(8,128)(2,1)S(1)}, bf16[512,1024]{1,0:T(8,128)(2,1)S(1)}) custom-call(s32[16]{0:T(128)S(1)} %fusion.2.tiles_ref, f32[512,1024]{1,0:T(8,128)S(1)} %get-tuple-element.99.rhs_ref, f32[1024,128]{1,0:T(8,128)} %constant_dynamic-update-slice_fusion.refs_0_, ...), custom_call_target="tpu_custom_call" | custom-call | flops 3221225472 | bytes 8388608 | tf_op jit(solution)/shard_map/solve_first/pallas_call | solution.py:221
  162.3 1.0 copy-done.2
  163.3 1.0 copy-done.5
  164.3 1.0 copy-done.14
  165.8 1.2 copy-done.3
  167.0 1.2 copy-done.6
  168.3 15.1 %trail_first.1.in_ref = f32[512,3072]{1,0:T(8,128)} custom-call(f32[512,24,128]{2,1,0:T(8,128)} %sens_ref.1, f32[512,128]{1,0:T(8,128)S(1)} %copy-done.34, bf16[512,1024]{1,0:T(8,128)(2,1)S(1)} %copy-done.3, bf16[512,1024]{1,0:T(8,128)(2,1)S(1)} %copy-done.6, bf16[512,3072]{1,0:T(8,128)(2,1)} %get-tuple-element.67.refs_2_, ...), custom_call_target="tpu_custom_call" | custom-call | flops 9663676416 | bytes 25165824 | tf_op jit(solution)/shard_map/trail_first/pallas_call | solution.py:302
  183.4 4.5 %couple.1.rhs_ref = f32[512,1024]{1,0:T(8,128)S(1)} custom-call(s32[16]{0:T(128)S(1)} %iota.15.tiles_ref, f32[512,1024]{1,0:T(8,128)S(1)} %get-tuple-element.108.rhs_ref, bf16[512,1024]{1,0:T(8,128)(2,1)S(1)} %copy-done.4, bf16[512,1024]{1,0:T(8,128)(2,1)S(1)} %copy-done.7, f32[16,512,128]{2,1,0:T(8,128)S(1)} %bitcast.18, ...), custom_call_target="tpu_custom_call" | custom-call | flops 3221225472 | bytes 8388608 | tf_op jit(solution)/shard_map/couple/pallas_call | solution.py:249
  187.9 5.5 %solve_second.1 = (f32[512,512]{1,0:T(8,128)S(1)}, f32[512,512]{1,0:T(8,128)}, bf16[512,1024]{1,0:T(8,128)(2,1)S(1)}, bf16[512,1024]{1,0:T(8,128)(2,1)S(1)}) custom-call(s32[16]{0:T(128)S(1)} %iota.14.tiles_ref, f32[512,1024]{1,0:T(8,128)S(1)} %couple.1.rhs_ref, f32[16,512,128]{2,1,0:T(8,128)S(1)} %bitcast.19, ...), custom_call_target="tpu_custom_call" | custom-call | flops 3221225472 | bytes 8388608 | tf_op jit(solution)/shard_map/solve_second/pallas_call | solution.py:221
  193.5 1.0 copy-done.29
  194.4 1.0 copy-done.31
  195.5 1.2 copy-done.30
  196.7 1.2 copy-done.32
  197.9 14.8 %trail_second.1 = f32[512,24,128]{2,1,0:T(8,128)} custom-call(f32[512,3072]{1,0:T(8,128)} %trail_first.1.in_ref, bf16[512,1024]{1,0:T(8,128)(2,1)S(1)} %copy-done.30, bf16[512,1024]{1,0:T(8,128)(2,1)S(1)} %copy-done.32, bf16[512,3072]{1,0:T(8,128)(2,1)} %get-tuple-element.112.refs_2_, bf16[512,3072]{1,0:T(8,128)(2,1)} %get-tuple-element.113.refs_3_, ...), custom_call_target="tpu_custom_call" | custom-call | flops 9663676416 | bytes 25165824 | tf_op jit(solution)/shard_map/trail_second/pallas_call | solution.py:332
  212.8 3.8 %place_unknowns.1 = f32[1024,8,128]{2,1,0:T(8,128)} custom-call(s32[1]{0:T(128)} %bitcast.core_ref, f32[512,512]{1,0:T(8,128)S(1)} %get-tuple-element.107.refs_0_, f32[512,512]{1,0:T(8,128)S(1)} %get-tuple-element.119.refs_1_, f32[512,512]{1,0:T(8,128)} %collective-permute-done.33.refs_2_, f32[512,512]{1,0:T(8,128)S(1)} %collective-permute-done.34.refs_3_), custom_call_target="tpu_custom_call" | custom-call | tf_op jit(solution)/shard_map/place_unknowns/pallas_call | solution.py:361
  (131 shorter events, 13.9 us)
Async XLA Ops:
  7.2 158.1 %all-gather.3.cloned.1.call-start = ((), (), s32[]{:S(2)}) async-start(), calls=%async_computation | async-start | bytes 4456448 | tf_op jit(solution)/shard_map/all_gather | solution.py:408
  7.2 100.0 %collective-permute-start.25 = (f32[8,128,24,128]{3,2,1,0:T(8,128)}, f32[8,128,24,128]{3,2,1,0:T(8,128)}, u32[]{:S(2)}, u32[]{:S(2)}) collective-permute-start(f32[8,128,24,128]{3,2,1,0:T(8,128)} %param.3), channel_id=1, source_target_pairs={{0,16},{16,0},{1,17},{17,1},{2,18},{18,2},{3,19},{19,3},{4,20},{20... | collective-permute-start | bytes 37748744 | tf_op jit(solution)/shard_map/ppermute | solution.py:386
  10.2 21.9 %collective-permute-start.1 = (f32[512,128]{1,0:T(8,128)S(1)}, f32[512,128]{1,0:T(8,128)S(1)}, u32[]{:S(2)}, u32[]{:S(2)}) collective-permute-start(f32[512,128]{1,0:T(8,128)S(1)} %pad_maximum_fusion), channel_id=1, source_target_pairs={{0,8},{1,9},{2,10},{3,11},{4,12},{5,13},{6,14},{7,15},{8,0},{9,1},... | collective-permute-start | bytes 786440 | tf_op jit(solution)/shard_map/ppermute | solution.py:395
  15.6 16.5 %collective-permute-start = (f32[512,128]{1,0:T(8,128)S(1)}, f32[512,128]{1,0:T(8,128)S(1)}, u32[]{:S(2)}, u32[]{:S(2)}) collective-permute-start(f32[512,128]{1,0:T(8,128)S(1)} %bitcast.20), channel_id=1, source_target_pairs={{0,4},{1,5},{2,6},{3,7},{4,8},{5,9},{6,10},{7,11},{8,12},{9,13},{1... | collective-permute-start | bytes 786440 | tf_op jit(solution)/shard_map/ppermute | solution.py:53
  32.9 15.4 %collective-permute-start.4 = (f32[256,128]{1,0:T(8,128)S(1)}, f32[256,128]{1,0:T(8,128)S(1)}, u32[]{:S(2)}, u32[]{:S(2)}) collective-permute-start(f32[256,128]{1,0:T(8,128)S(1)} %get-tuple-element.137), channel_id=1, source_target_pairs={{0,2},{1,3},{2,0},{3,1},{4,6},{5,7},{6,4},{7,5},{8,10},{9,11},{10,... | collective-permute-start | bytes 393224 | tf_op jit(solution)/shard_map/ppermute | solution.py:53
  34.6 13.8 %collective-permute-start.2 = (f32[512,128]{1,0:T(8,128)S(1)}, f32[512,128]{1,0:T(8,128)S(1)}, u32[]{:S(2)}, u32[]{:S(2)}) collective-permute-start(f32[512,128]{1,0:T(8,128)S(1)} %collective-permute-done), channel_id=1, source_target_pairs={{0,4},{1,5},{2,6},{3,7},{4,8},{5,9},{6,10},{7,11},{8,12},{9,13},{1... | collective-permute-start | bytes 786440 | tf_op jit(solution)/shard_map/ppermute | solution.py:53
  35.3 13.1 %collective-permute-start.3 = (f32[256,128]{1,0:T(8,128)S(1)}, f32[256,128]{1,0:T(8,128)S(1)}, u32[]{:S(2)}, u32[]{:S(2)}) collective-permute-start(f32[256,128]{1,0:T(8,128)S(1)} %get-tuple-element.138), channel_id=1, source_target_pairs={{0,1},{1,0},{2,3},{3,2},{4,5},{5,4},{6,7},{7,6},{8,9},{9,8},{10,11... | collective-permute-start | bytes 393224 | tf_op jit(solution)/shard_map/ppermute | solution.py:53
  36.8 11.6 %collective-permute-start.5 = (f32[256,128]{1,0:T(8,128)S(1)}, f32[256,128]{1,0:T(8,128)S(1)}, u32[]{:S(2)}, u32[]{:S(2)}) collective-permute-start(f32[256,128]{1,0:T(8,128)S(1)} %get-tuple-element.87), channel_id=1, source_target_pairs={{0,4},{1,5},{2,6},{3,7},{4,8},{5,9},{6,10},{7,11},{8,12},{9,13},{1... | collective-permute-start | bytes 393224 | tf_op jit(solution)/shard_map/ppermute | solution.py:53
  39.3 4.9 %copy-start = (f32[8,128,24,128]{3,2,1,0:T(8,128)S(1)}, f32[8,128,24,128]{3,2,1,0:T(8,128)}, u32[]{:S(2)}) copy-start(f32[8,128,24,128]{3,2,1,0:T(8,128)} %param.3) | copy-start | bytes 37748740
  48.4 5.0 %collective-permute-start.8 = (f32[256,128]{1,0:T(8,128)S(1)}, f32[256,128]{1,0:T(8,128)S(1)}, u32[]{:S(2)}, u32[]{:S(2)}) collective-permute-start(f32[256,128]{1,0:T(8,128)S(1)} %get-tuple-element.135), channel_id=1, source_target_pairs={{0,2},{1,3},{2,0},{3,1},{4,6},{5,7},{6,4},{7,5},{8,10},{9,11},{10,... | collective-permute-start | bytes 393224 | tf_op jit(solution)/shard_map/ppermute | solution.py:53
  48.9 13.4 %collective-permute-start.6 = (f32[512,128]{1,0:T(8,128)S(1)}, f32[512,128]{1,0:T(8,128)S(1)}, u32[]{:S(2)}, u32[]{:S(2)}) collective-permute-start(f32[512,128]{1,0:T(8,128)S(1)} %collective-permute-done.2), channel_id=1, source_target_pairs={{0,4},{1,5},{2,6},{3,7},{4,8},{5,9},{6,10},{7,11},{8,12},{9,13},{1... | collective-permute-start | bytes 786440 | tf_op jit(solution)/shard_map/ppermute | solution.py:53
  48.9 5.2 %collective-permute-start.7 = (f32[256,128]{1,0:T(8,128)S(1)}, f32[256,128]{1,0:T(8,128)S(1)}, u32[]{:S(2)}, u32[]{:S(2)}) collective-permute-start(f32[256,128]{1,0:T(8,128)S(1)} %get-tuple-element.136), channel_id=1, source_target_pairs={{0,1},{1,0},{2,3},{3,2},{4,5},{5,4},{6,7},{7,6},{8,9},{9,8},{10,11... | collective-permute-start | bytes 393224 | tf_op jit(solution)/shard_map/ppermute | solution.py:53
  50.1 12.3 %collective-permute-start.9 = (f32[256,128]{1,0:T(8,128)S(1)}, f32[256,128]{1,0:T(8,128)S(1)}, u32[]{:S(2)}, u32[]{:S(2)}) collective-permute-start(f32[256,128]{1,0:T(8,128)S(1)} %collective-permute-done.5), channel_id=1, source_target_pairs={{0,4},{1,5},{2,6},{3,7},{4,8},{5,9},{6,10},{7,11},{8,12},{9,13},{1... | collective-permute-start | bytes 393224 | tf_op jit(solution)/shard_map/ppermute | solution.py:53
  53.5 11.4 %collective-permute-start.15 = (f32[512,128]{1,0:T(8,128)S(1)}, f32[512,128]{1,0:T(8,128)S(1)}, u32[]{:S(2)}, u32[]{:S(2)}) collective-permute-start(f32[512,128]{1,0:T(8,128)S(1)} %pad_maximum_fusion.1.refs_0_), channel_id=1, source_target_pairs={{0,2},{1,3},{2,0},{3,1},{4,6},{5,7},{6,4},{7,5},{8,10},{9,11},{10,... | collective-permute-start | bytes 786440 | tf_op jit(solution)/shard_map/ppermute | solution.py:53
  54.1 49.6 %copy-start.35 = (s32[2048]{0:T(1024)S(1)}, s32[2048]{0:T(1024)}, u32[]{:S(2)}) copy-start(s32[2048]{0:T(1024)} %param.5) | copy-start | bytes 24580
  54.1 16.0 %collective-permute-start.16 = (f32[512,128]{1,0:T(8,128)S(1)}, f32[512,128]{1,0:T(8,128)S(1)}, u32[]{:S(2)}, u32[]{:S(2)}) collective-permute-start(f32[512,128]{1,0:T(8,128)S(1)} %pad_maximum_fusion.2.refs_2_), channel_id=1, source_target_pairs={{0,1},{1,0},{2,3},{3,2},{4,5},{5,4},{6,7},{7,6},{8,9},{9,8},{10,11... | collective-permute-start | bytes 786440 | tf_op jit(solution)/shard_map/ppermute | solution.py:53
  62.4 5.2 %collective-permute-start.13 = (f32[256,128]{1,0:T(8,128)S(1)}, f32[256,128]{1,0:T(8,128)S(1)}, u32[]{:S(2)}, u32[]{:S(2)}) collective-permute-start(f32[256,128]{1,0:T(8,128)S(1)} %get-tuple-element.131), channel_id=1, source_target_pairs={{0,2},{1,3},{2,0},{3,1},{4,6},{5,7},{6,4},{7,5},{8,10},{9,11},{10,... | collective-permute-start | bytes 393224 | tf_op jit(solution)/shard_map/ppermute | solution.py:53
  63.9 7.2 %collective-permute-start.12 = (f32[256,128]{1,0:T(8,128)S(1)}, f32[256,128]{1,0:T(8,128)S(1)}, u32[]{:S(2)}, u32[]{:S(2)}) collective-permute-start(f32[256,128]{1,0:T(8,128)S(1)} %get-tuple-element.132), channel_id=1, source_target_pairs={{0,1},{1,0},{2,3},{3,2},{4,5},{5,4},{6,7},{7,6},{8,9},{9,8},{10,11... | collective-permute-start | bytes 393224 | tf_op jit(solution)/shard_map/ppermute | solution.py:53
  64.9 2.7 %copy-start.15 = (f32[512,128]{1,0:T(8,128)}, f32[512,128]{1,0:T(8,128)S(1)}, u32[]{:S(2)}) copy-start(f32[512,128]{1,0:T(8,128)S(1)} %collective-permute-done.15.refs_1_) | copy-start | bytes 786436
  64.9 9.3 %collective-permute-start.14 = (f32[256,128]{1,0:T(8,128)S(1)}, f32[256,128]{1,0:T(8,128)S(1)}, u32[]{:S(2)}, u32[]{:S(2)}) collective-permute-start(f32[256,128]{1,0:T(8,128)S(1)} %collective-permute-done.9), channel_id=1, source_target_pairs={{0,4},{1,5},{2,6},{3,7},{4,8},{5,9},{6,10},{7,11},{8,12},{9,13},{1... | collective-permute-start | bytes 393224 | tf_op jit(solution)/shard_map/ppermute | solution.py:53
  67.6 8.3 %collective-permute-start.11 = (f32[256,128]{1,0:T(8,128)S(1)}, f32[256,128]{1,0:T(8,128)S(1)}, u32[]{:S(2)}, u32[]{:S(2)}) collective-permute-start(f32[256,128]{1,0:T(8,128)S(1)} %get-tuple-element.133), channel_id=1, source_target_pairs={{0,2},{1,3},{2,0},{3,1},{4,6},{5,7},{6,4},{7,5},{8,10},{9,11},{10,... | collective-permute-start | bytes 393224 | tf_op jit(solution)/shard_map/ppermute | solution.py:53
  70.1 14.7 %copy-start.17 = (f32[512,128]{1,0:T(8,128)}, f32[512,128]{1,0:T(8,128)S(1)}, u32[]{:S(2)}) copy-start(f32[512,128]{1,0:T(8,128)S(1)} %collective-permute-done.16.refs_3_) | copy-start | bytes 786436
  70.1 9.2 %collective-permute-start.10 = (f32[256,128]{1,0:T(8,128)S(1)}, f32[256,128]{1,0:T(8,128)S(1)}, u32[]{:S(2)}, u32[]{:S(2)}) collective-permute-start(f32[256,128]{1,0:T(8,128)S(1)} %get-tuple-element.134), channel_id=1, source_target_pairs={{0,1},{1,0},{2,3},{3,2},{4,5},{5,4},{6,7},{7,6},{8,9},{9,8},{10,11... | collective-permute-start | bytes 393224 | tf_op jit(solution)/shard_map/ppermute | solution.py:53
  71.1 8.8 %collective-permute-start.17 = (f32[512,128]{1,0:T(8,128)S(1)}, f32[512,128]{1,0:T(8,128)S(1)}, u32[]{:S(2)}, u32[]{:S(2)}) collective-permute-start(f32[512,128]{1,0:T(8,128)S(1)} %pad_maximum_fusion.3.refs_4_), channel_id=1, source_target_pairs={{0,2},{1,3},{2,0},{3,1},{4,6},{5,7},{6,4},{7,5},{8,10},{9,11},{10,... | collective-permute-start | bytes 786440 | tf_op jit(solution)/shard_map/ppermute | solution.py:53
  74.3 10.5 %collective-permute-start.18 = (f32[512,128]{1,0:T(8,128)S(1)}, f32[512,128]{1,0:T(8,128)S(1)}, u32[]{:S(2)}, u32[]{:S(2)}) collective-permute-start(f32[512,128]{1,0:T(8,128)S(1)} %pad_maximum_fusion.4.refs_6_), channel_id=1, source_target_pairs={{0,1},{1,0},{2,3},{3,2},{4,5},{5,4},{6,7},{7,6},{8,9},{9,8},{10,11... | collective-permute-start | bytes 786440 | tf_op jit(solution)/shard_map/ppermute | solution.py:53
  75.1 39.1 %copy-start.8 = (f32[512,128]{1,0:T(8,128)}, f32[512,128]{1,0:T(8,128)S(1)}, u32[]{:S(2)}) copy-start(f32[512,128]{1,0:T(8,128)S(1)} %pad_maximum_fusion.7.refs_8_) | copy-start | bytes 786436
  75.9 38.3 %copy-start.10 = (f32[512,128]{1,0:T(8,128)}, f32[512,128]{1,0:T(8,128)S(1)}, u32[]{:S(2)}) copy-start(f32[512,128]{1,0:T(8,128)S(1)} %pad_maximum_fusion.6.refs_14_) | copy-start | bytes 786436
  79.3 34.9 %copy-start.12 = (f32[512,128]{1,0:T(8,128)}, f32[512,128]{1,0:T(8,128)S(1)}, u32[]{:S(2)}) copy-start(f32[512,128]{1,0:T(8,128)S(1)} %pad_maximum_fusion.5.refs_12_) | copy-start | bytes 786436
  80.0 34.2 %copy-start.19 = (f32[512,128]{1,0:T(8,128)}, f32[512,128]{1,0:T(8,128)S(1)}, u32[]{:S(2)}) copy-start(f32[512,128]{1,0:T(8,128)S(1)} %collective-permute-done.17.refs_5_) | copy-start | bytes 786436
  84.8 29.5 %copy-start.21 = (f32[512,128]{1,0:T(8,128)}, f32[512,128]{1,0:T(8,128)S(1)}, u32[]{:S(2)}) copy-start(f32[512,128]{1,0:T(8,128)S(1)} %collective-permute-done.18.refs_7_) | copy-start | bytes 786436
  87.5 10.6 %collective-permute-start.20 = (f32[512,128]{1,0:T(8,128)S(1)}, f32[512,128]{1,0:T(8,128)}, u32[]{:S(2)}, u32[]{:S(2)}) collective-permute-start(f32[512,128]{1,0:T(8,128)S(1)} %pad_maximum_fusion.10), channel_id=1, source_target_pairs={{0,2},{1,3},{2,0},{3,1},{4,6},{5,7},{6,4},{7,5},{8,10},{9,11},{10,... | collective-permute-start | bytes 786440 | tf_op jit(solution)/shard_map/ppermute | solution.py:53
  89.0 12.5 %collective-permute-start.19 = (f32[512,128]{1,0:T(8,128)}, f32[512,128]{1,0:T(8,128)}, u32[]{:S(2)}, u32[]{:S(2)}) collective-permute-start(f32[512,128]{1,0:T(8,128)} %pad_maximum_fusion.9), channel_id=1, source_target_pairs={{0,1},{1,0},{2,3},{3,2},{4,5},{5,4},{6,7},{7,6},{8,9},{9,8},{10,11... | collective-permute-start | bytes 786440 | tf_op jit(solution)/shard_map/ppermute | solution.py:53
  90.3 24.0 %collective-permute-start.21 = (f32[512,128]{1,0:T(8,128)S(1)}, f32[512,128]{1,0:T(8,128)S(1)}, u32[]{:S(2)}, u32[]{:S(2)}) collective-permute-start(f32[512,128]{1,0:T(8,128)S(1)} %pad_maximum_fusion.7.refs_8_), channel_id=1, source_target_pairs={{0,2},{1,3},{2,0},{3,1},{4,6},{5,7},{6,4},{7,5},{8,10},{9,11},{10,... | collective-permute-start | bytes 786440 | tf_op jit(solution)/shard_map/ppermute | solution.py:53
  91.3 23.6 %collective-permute-start.22 = (f32[512,128]{1,0:T(8,128)S(1)}, f32[512,128]{1,0:T(8,128)S(1)}, u32[]{:S(2)}, u32[]{:S(2)}) collective-permute-start(f32[512,128]{1,0:T(8,128)S(1)} %pad_maximum_fusion.8.refs_10_), channel_id=1, source_target_pairs={{0,1},{1,0},{2,3},{3,2},{4,5},{5,4},{6,7},{7,6},{8,9},{9,8},{10,11... | collective-permute-start | bytes 786440 | tf_op jit(solution)/shard_map/ppermute | solution.py:53
  98.1 20.2 %collective-permute-start.23 = (f32[512,128]{1,0:T(8,128)S(1)}, f32[512,128]{1,0:T(8,128)S(1)}, u32[]{:S(2)}, u32[]{:S(2)}) collective-permute-start(f32[512,128]{1,0:T(8,128)S(1)} %pad_maximum_fusion.5.refs_12_), channel_id=1, source_target_pairs={{0,2},{1,3},{2,0},{3,1},{4,6},{5,7},{6,4},{7,5},{8,10},{9,11},{10,... | collective-permute-start | bytes 786440 | tf_op jit(solution)/shard_map/ppermute | solution.py:53
  101.6 20.8 %collective-permute-start.24 = (f32[512,128]{1,0:T(8,128)S(1)}, f32[512,128]{1,0:T(8,128)}, u32[]{:S(2)}, u32[]{:S(2)}) collective-permute-start(f32[512,128]{1,0:T(8,128)S(1)} %pad_maximum_fusion.6.refs_14_), channel_id=1, source_target_pairs={{0,1},{1,0},{2,3},{3,2},{4,5},{5,4},{6,7},{7,6},{8,9},{9,8},{10,11... | collective-permute-start | bytes 786440 | tf_op jit(solution)/shard_map/ppermute | solution.py:53
  107.2 18.1 %copy-start.16 = (f32[512,128]{1,0:T(8,128)S(1)}, f32[512,128]{1,0:T(8,128)}, u32[]{:S(2)}) copy-start(f32[512,128]{1,0:T(8,128)} %copy-done.15) | copy-start | bytes 786436
  107.2 18.1 %copy-start.18 = (f32[512,128]{1,0:T(8,128)S(1)}, f32[512,128]{1,0:T(8,128)}, u32[]{:S(2)}) copy-start(f32[512,128]{1,0:T(8,128)} %copy-done.17) | copy-start | bytes 786436
  107.2 45.4 %slice-start = ((s8[12582912]{0:T(1024)(128)(4,1)}), s8[4194304]{0:T(1024)(128)(4,1)S(1)}, s32[]{:S(2)}) async-start(s8[12582912]{0:T(1024)(128)(4,1)} %bitcast.14), calls=%async_computation.1 | async-start | bytes 8388608
  122.3 30.3 %slice-start.1 = ((s8[12582912]{0:T(1024)(128)(4,1)}), s8[4194304]{0:T(1024)(128)(4,1)S(1)}, s32[]{:S(2)}) async-start(s8[12582912]{0:T(1024)(128)(4,1)} %bitcast.14), calls=%async_computation.2 | async-start | bytes 8388608
  122.3 30.3 %slice-start.2 = ((s8[12582912]{0:T(1024)(128)(4,1)}), s8[4194304]{0:T(1024)(128)(4,1)S(1)}, s32[]{:S(2)}) async-start(s8[12582912]{0:T(1024)(128)(4,1)} %bitcast.14), calls=%async_computation.3 | async-start | bytes 8388608
  122.3 22.6 %collective-permute-start.26 = (f32[1024,128]{1,0:T(8,128)}, f32[1024,128]{1,0:T(8,128)S(1)}, u32[]{:S(2)}, u32[]{:S(2)}) collective-permute-start(f32[1024,128]{1,0:T(8,128)} %constant_dynamic-update-slice_fusion.refs_0_), channel_id=1, source_target_pairs={{0,2},{1,3},{2,0},{3,1},{4,6},{5,7},{6,4},{7,5},{8,10},{9,11},{10,... | collective-permute-start | bytes 1572872 | tf_op jit(solution)/shard_map/ppermute | solution.py:53
  123.3 21.7 %collective-permute-start.27 = (f32[1024,128]{1,0:T(8,128)}, f32[1024,128]{1,0:T(8,128)S(1)}, u32[]{:S(2)}, u32[]{:S(2)}) collective-permute-start(f32[1024,128]{1,0:T(8,128)} %constant_dynamic-update-slice_fusion.5.refs_4_), channel_id=1, source_target_pairs={{0,1},{1,0},{2,3},{3,2},{4,5},{5,4},{6,7},{7,6},{8,9},{9,8},{10,11... | collective-permute-start | bytes 1572872 | tf_op jit(solution)/shard_map/ppermute | solution.py:53
  125.3 1.0 copy-start.9
  145.0 11.9 %collective-permute-start.28 = (f32[1024,128]{1,0:T(8,128)}, f32[1024,128]{1,0:T(8,128)S(1)}, u32[]{:S(2)}, u32[]{:S(2)}) collective-permute-start(f32[1024,128]{1,0:T(8,128)} %constant_dynamic-update-slice_fusion.refs_0_), channel_id=1, source_target_pairs={{0,16},{16,0},{1,17},{17,1},{2,18},{18,2},{3,19},{19,3},{4,20},{20... | collective-permute-start | bytes 1572872 | tf_op jit(solution)/shard_map/ppermute | solution.py:386
  145.0 11.9 %collective-permute-start.29 = (f32[1024,128]{1,0:T(8,128)S(1)}, f32[1024,128]{1,0:T(8,128)S(1)}, u32[]{:S(2)}, u32[]{:S(2)}) collective-permute-start(f32[1024,128]{1,0:T(8,128)S(1)} %collective-permute-done.26.refs_2_), channel_id=1, source_target_pairs={{0,16},{16,0},{1,17},{17,1},{2,18},{18,2},{3,19},{19,3},{4,20},{20... | collective-permute-start | bytes 1572872 | tf_op jit(solution)/shard_map/ppermute | solution.py:386
  145.5 11.4 %collective-permute-start.30 = (f32[1024,128]{1,0:T(8,128)}, f32[1024,128]{1,0:T(8,128)S(1)}, u32[]{:S(2)}, u32[]{:S(2)}) collective-permute-start(f32[1024,128]{1,0:T(8,128)} %constant_dynamic-update-slice_fusion.5.refs_4_), channel_id=1, source_target_pairs={{0,16},{16,0},{1,17},{17,1},{2,18},{18,2},{3,19},{19,3},{4,20},{20... | collective-permute-start | bytes 1572872 | tf_op jit(solution)/shard_map/ppermute | solution.py:386
  145.6 11.4 %collective-permute-start.31 = (f32[1024,128]{1,0:T(8,128)S(1)}, f32[1024,128]{1,0:T(8,128)S(1)}, u32[]{:S(2)}, u32[]{:S(2)}) collective-permute-start(f32[1024,128]{1,0:T(8,128)S(1)} %collective-permute-done.27.refs_6_), channel_id=1, source_target_pairs={{0,16},{16,0},{1,17},{17,1},{2,18},{18,2},{3,19},{19,3},{4,20},{20... | collective-permute-start | bytes 1572872 | tf_op jit(solution)/shard_map/ppermute | solution.py:386
  156.9 8.9 %copy-start.34 = (f32[512,128]{1,0:T(8,128)S(1)}, f32[512,128]{1,0:T(8,128)}, u32[]{:S(2)}) copy-start(f32[512,128]{1,0:T(8,128)} %copy-done.33) | copy-start | bytes 786436
  162.3 1.0 copy-start.2
  163.3 1.0 copy-start.5
  164.3 1.0 copy-start.14
  165.3 18.1 %collective-permute-start.32 = (f32[16,512,128]{2,1,0:T(8,128)}, f32[16,512,128]{2,1,0:T(8,128)S(1)}, u32[]{:S(2)}, u32[]{:S(2)}) collective-permute-start(f32[16,512,128]{2,1,0:T(8,128)} %bitcast.17), channel_id=1, source_target_pairs={{0,16},{16,0},{1,17},{17,1},{2,18},{18,2},{3,19},{19,3},{4,20},{20... | collective-permute-start | bytes 12582920 | tf_op jit(solution)/shard_map/ppermute | solution.py:386
  165.4 47.4 %collective-permute-start.33 = (f32[512,512]{1,0:T(8,128)}, f32[512,512]{1,0:T(8,128)}, u32[]{:S(2)}, u32[]{:S(2)}) collective-permute-start(f32[512,512]{1,0:T(8,128)} %copy-done.14), channel_id=1, source_target_pairs={{0,16},{16,0},{1,17},{17,1},{2,18},{18,2},{3,19},{19,3},{4,20},{20... | collective-permute-start | bytes 3145736 | tf_op jit(solution)/shard_map/ppermute | solution.py:386
  165.8 1.2 copy-start.3
  167.0 1.2 copy-start.6
  168.2 15.1 %copy-start.1 = (f32[8192,128]{1,0:T(8,128)S(1)}, f32[8192,128]{1,0:T(8,128)}, u32[]{:S(2)}) copy-start(f32[8192,128]{1,0:T(8,128)} %all-gather.3.cloned.1.call-done) | copy-start | bytes 12582916
  168.3 15.1 %copy-start.4 = (bf16[512,1024]{1,0:T(8,128)(2,1)S(1)}, bf16[512,1024]{1,0:T(8,128)(2,1)}, u32[]{:S(2)}) copy-start(bf16[512,1024]{1,0:T(8,128)(2,1)} %copy-done.2) | copy-start | bytes 3145732
  168.3 15.1 %copy-start.7 = (bf16[512,1024]{1,0:T(8,128)(2,1)S(1)}, bf16[512,1024]{1,0:T(8,128)(2,1)}, u32[]{:S(2)}) copy-start(bf16[512,1024]{1,0:T(8,128)(2,1)} %copy-done.5) | copy-start | bytes 3145732
  193.5 1.0 copy-start.29
  194.4 1.0 copy-start.31
  195.4 17.3 %collective-permute-start.34 = (f32[512,512]{1,0:T(8,128)}, f32[512,512]{1,0:T(8,128)S(1)}, u32[]{:S(2)}, u32[]{:S(2)}) collective-permute-start(f32[512,512]{1,0:T(8,128)} %get-tuple-element.121), channel_id=1, source_target_pairs={{0,16},{16,0},{1,17},{17,1},{2,18},{18,2},{3,19},{19,3},{4,20},{20... | collective-permute-start | bytes 3145736 | tf_op jit(solution)/shard_map/ppermute | solution.py:386
  195.5 1.2 copy-start.30
  196.7 1.2 copy-start.32
  (11 other events, 9.5 us)
Sparse Core Ops, SparseCore 0:
  33.0 100.4 all-gather.2

commit v3 on v2

--- a/solution.py
+++ b/solution.py
@@ -82,6 +82,14 @@
     return places
 
 
+def end_to_end(arrays, places):
+    inner, base = [], 0
+    for array, own in zip(arrays, places, strict=True):
+        inner += [(base + start, first, place) for start, first, place in own]
+        base += array.shape[0]
+    return jnp.concatenate(arrays, axis=0), inner
+
+
 def source_tiles(sizes, index):
     z_size, y_size, x_size = sizes
     z, y, x = index // (y_size * x_size), index // x_size % y_size, index % x_size
@@ -108,15 +116,23 @@
                 lanes = pl.ds(slot_of(place, sizes) * 128, 128)
                 both_ref[pl.ds(first, half), lanes] = high
                 both_ref[pl.ds(rows + first, half), lanes] = low
-        for start in range(0, width, step):
-            size = min(step, width - start)
+        def pick(start, size, out_ref, to):
             columns = wanted_ref[:, pl.ds(start, size)]
             lane = lax.broadcasted_iota(jnp.int32, (128, size), 0)
             for slot in range(count):
                 hot = (columns - tiles_ref[slot] * 128) == lane
                 hot_ref[pl.ds(slot * 128, 128), pl.ds(0, size)] = hot.astype(F32).astype(BF16)
             got = jnp.dot(both_ref[...], hot_ref[:, pl.ds(0, size)], preferred_element_type=F32)
-            outs[start // NB][:, pl.ds(start % NB, size)] = got[:rows] + got[rows:]
+            out_ref[:, pl.ds(to, size)] = got[:rows] + got[rows:]
+
+        for k in range(2):
+
+            @pl.loop(0, NB // step, unroll=NB // step if depth <= 2 * NB else 1)
+            def _(i, k=k):
+                to = pl.multiple_of(i * step, step)
+                pick(k * NB + to, step, outs[k], to)
+
+        pick(2 * NB, width - 2 * NB, outs[2], 0)
 
     vmem = pl.BlockSpec(memory_space=pltpu.VMEM)
     return pl.pallas_call(
@@ -129,6 +145,10 @@
         cost_estimate=pl.CostEstimate(flops=4 * rows * depth * width, transcendentals=0, bytes_accessed=8 * rows * depth),
         name="permute_columns",
     )(tiles, wanted.reshape(1, width), *arrays)
+
+
+def in_hbm(arrays):
+    return [pltpu.with_memory_space_constraint(array, pltpu.HBM) for array in arrays]
 
 
 def prepare(block, keep, step, name):
@@ -159,7 +179,7 @@
         compiler_params=pltpu.CompilerParams(vmem_limit_bytes=12 * MIB),
         cost_estimate=pl.CostEstimate(flops=0, transcendentals=0, bytes_accessed=12 * cycles * depth * tiles * width),
         name=name,
-    )(keep, block.reshape(2 * cycles, depth * tiles, width))
+    )(keep, *in_hbm([block.reshape(2 * cycles, depth * tiles, width)]))
 
 
 def load_blocks(group, tiles_ref, parts, sizes, high_ref, low_ref):
@@ -217,13 +237,14 @@
 
     vmem = pl.BlockSpec(memory_space=pltpu.VMEM)
     f32 = jax.ShapeDtypeStruct((rows, half), F32)
-    b16 = jax.ShapeDtypeStruct((rows, NB), BF16)
+    b16 = pltpu.HBM((rows, NB), BF16)
+    whole = pl.BlockSpec((rows, NB), lambda i: (0, 0), pipeline_mode=pl.Buffered(1))
     return pl.pallas_call(
         kernel,
         out_shape=(f32, f32, b16, b16),
         grid=(1,),
         in_specs=[pl.BlockSpec(memory_space=pltpu.SMEM), vmem, *block_specs(operands, chosen)],
-        out_specs=(vmem,) * 4,
+        out_specs=(vmem, vmem, whole, whole),
         scratch_shapes=[pltpu.VMEM((per_block, NB, 128), BF16)] * 2,
         compiler_params=pltpu.CompilerParams(vmem_limit_bytes=24 * MIB),
         cost_estimate=pl.CostEstimate(flops=6 * rows * NB * NB, transcendentals=0, bytes_accessed=8 * NB * NB),
@@ -246,25 +267,22 @@
             out_ref[to] = rhs_ref[to] - mul3(left, right, NN)
 
     vmem = pl.BlockSpec(memory_space=pltpu.VMEM)
+    whole = pl.BlockSpec((rows, NB), lambda i: (0, 0), pipeline_mode=pl.Buffered(1))
     return pl.pallas_call(
         kernel,
         out_shape=jax.ShapeDtypeStruct((rows, NB), F32),
         grid=(1,),
-        in_specs=[pl.BlockSpec(memory_space=pltpu.SMEM), vmem, vmem, vmem, *block_specs(operands, chosen)],
+        in_specs=[pl.BlockSpec(memory_space=pltpu.SMEM), vmem, whole, whole, *block_specs(operands, chosen)],
         out_specs=vmem,
         scratch_shapes=[pltpu.VMEM((per_block, NB, 128), BF16)] * 2,
         compiler_params=pltpu.CompilerParams(vmem_limit_bytes=22 * MIB),
         cost_estimate=pl.CostEstimate(flops=6 * rows * NB * NB, transcendentals=0, bytes_accessed=8 * NB * NB),
         name="couple",
-    )(tiles, rhs, *solved, *operands)
-
-
-def in_hbm(arrays):
-    return [pltpu.with_memory_space_constraint(array, pltpu.HBM) for array in arrays]
+    )(tiles, rhs, *in_hbm(solved), *operands)
 
 
 def trail_specs(rows, wide):
-    whole = pl.BlockSpec((rows, NB), lambda i: (0, 0))
+    whole = pl.BlockSpec((rows, NB), lambda i: (0, 0), pipeline_mode=pl.Buffered(1))
     part = pl.BlockSpec((NB // 2, wide), lambda i: (0, i))
     return [whole, whole, part, part, part, part]
 
@@ -312,7 +330,7 @@
         compiler_params=pltpu.CompilerParams(vmem_limit_bytes=24 * MIB),
         cost_estimate=trail_cost(rows, tiles),
         name="trail_first",
-    )(*in_hbm([sensitivity]), own_tile, *solved, *in_hbm(halves))
+    )(*in_hbm([sensitivity]), own_tile, *in_hbm([*solved, *halves]))
 
 
 def trail_second(partial, solved, halves, tiles):
@@ -338,7 +356,7 @@
         compiler_params=pltpu.CompilerParams(vmem_limit_bytes=24 * MIB),
         cost_estimate=trail_cost(rows, tiles),
         name="trail_second",
-    )(*in_hbm([partial]), *solved, *in_hbm(halves))
+    )(*in_hbm([partial, *solved, *halves]))
 
 
 def place_unknowns(core, parts):
@@ -388,63 +406,67 @@
     keep = jnp.stack([index >= per_block, index >= 2 * per_block]).astype(jnp.int32)
     own_columns = lax.dynamic_slice(pivots, (index * width,), (width,))
 
-    stripe_layers = [sensitivity[:, 0, :]]
+    stripe_layers = [lax.optimization_barrier(sensitivity[:, 0, :])]
+    stripe_layers.append(step_z(stripe_layers[0]))
     corner = factor_rows[:, :, 0, :].reshape(cycles * width, width)
     partners = [(j, j + per_block) for j in range(per_block)] + [(j + per_block, j) for j in range(per_block)]
     shared = jnp.concatenate([corner[quarter:half], corner[half + quarter :]], axis=0)
     received = lax.ppermute(shared, "pcol", partners)
-    stripe_layers.append(step_z(stripe_layers[0]))
     other_rows = swap(factor_rows)
-    stripe_layers, received, keep = gate((stripe_layers, received, keep))
+    across = gather_across(stripe_layers[:1], sizes)
+    own0 = prepare(factor_rows, keep, 0, "prepare_own_first")
     first = index < per_block
     diag0 = [jnp.where(first, corner[:quarter], received[:quarter])]
-    late = jnp.concatenate(
-        [
-            jnp.where(first, received[:quarter], corner[:quarter]),
-            jnp.where(first, received[quarter:], corner[half : half + quarter]),
-        ],
-        axis=0,
+    late = [
+        jnp.concatenate(
+            [
+                jnp.where(first, received[:quarter], corner[:quarter]),
+                jnp.where(first, received[quarter:], corner[half : half + quarter]),
+            ],
+            axis=0,
+        )
+    ]
+    stripe_layers[1], across, keep, diag0[0], late[0] = gate((stripe_layers[1], across, keep, diag0[0], late[0]), own0)
+
+    stripe_layers.append(step_z(stripe_layers[1]))
+    arrays = [gather_along(across, sizes)]
+    diag0.append(step_z(diag0[0]))
+    across = gather_across(stripe_layers[1:2], sizes)
+    own1 = prepare(factor_rows, keep, 1, "prepare_own_second")
+    stripe_layers[2], across, keep, diag0[1], late[0] = gate((stripe_layers[2], across, keep, diag0[1], late[0]), own1)
+
+    stripe_layers.append(step_z(stripe_layers[2]))
+    arrays.append(gather_along(across, sizes))
+    diag0.append(step_z(diag0[1]))
+    across = gather_across(stripe_layers[2:3], sizes)
+    late.append(step_z(late[0]))
+    stripe_layers[3], across, keep, diag0[2], late[1] = gate(
+        (stripe_layers[3], across, keep, diag0[2], late[1]), arrays[0]
     )
-    late = lax.all_gather(late, "pcol", axis=0)[: 2 * per_block]
-
-    across = gather_across(stripe_layers[:1], sizes)
-    stripe_layers.append(step_z(stripe_layers[1]))
-    diag0.append(step_z(diag0[0]))
-    own0 = prepare(factor_rows, keep, 0, "prepare_own_first")
-    stripe_layers, across, keep, diag0 = gate((stripe_layers, across, keep, diag0), own0)
-
-    arrays = [gather_along(across, sizes)]
-    across = gather_across(stripe_layers[1:2], sizes)
-    stripe_layers.append(step_z(stripe_layers[2]))
-    diag0.append(step_z(diag0[1]))
-    stripe_layers, across, diag0 = gate((stripe_layers, across, diag0))
-
-    arrays.append(gather_along(across, sizes))
-    across = gather_across(stripe_layers[2:3], sizes)
-    diag0.append(step_z(diag0[2]))
-    across, diag0, keep = gate((across, diag0, keep), arrays[0])
 
     arrays.append(gather_along(across, sizes))
     across = gather_across(stripe_layers[3:4], sizes)
-    across, diag0 = gate((across, diag0), arrays[1])
+    diag0.append(step_z(diag0[2]))
+    late.append(step_z(late[1]))
+    other0 = prepare(other_rows, keep, 0, "prepare_other_first")
+    across, keep, diag0[3], late[2] = gate((across, keep, diag0[3], late[2]), arrays[1], other0)
 
     arrays.append(gather_along(across, sizes))
+    late.append(step_z(late[2]))
     diag_across = gather_across(diag0, sizes)
-    other0 = prepare(other_rows, keep, 0, "prepare_other_first")
-    diag_across, pivots, keep = gate((diag_across, pivots, keep), arrays, other0)
+    other1 = prepare(other_rows, keep, 1, "prepare_other_second")
+    diag_across, late[3], pivots = gate((diag_across, late[3], pivots), arrays, other1)
 
     diag_arrays = gather_along(diag_across, sizes)
+    late_across = gather_across(late, sizes)
     stripe_places = [p for d in range(sizes[0]) for p in gathered_places(d, 1, rows // 2, sizes)]
     stripe_arrays = [array for layer in arrays for array in layer]
     wanted = jnp.concatenate([pivots[: 2 * NB], own_columns])
-    stripe = permute_columns(stripe_arrays, stripe_places, rows // 2, sizes, tiles, wanted, rows)
-    rhs0, rhs1, own_tile = stripe
-    diag_arrays, keep = gate((diag_arrays, keep), rhs0)
-    diag_pairs = [(array, swap(array)) for array in diag_arrays]
-
-    block_places = gathered_places(0, sizes[0], quarter // 2, sizes)
-    own1 = prepare(factor_rows, keep, 1, "prepare_own_second")
-    other1 = prepare(other_rows, keep, 1, "prepare_other_second")
+    rhs0, rhs1, own_tile = permute_columns(stripe_arrays, stripe_places, rows // 2, sizes, tiles, wanted, rows)
+    late_across, diag_arrays = gate((late_across, diag_arrays), rhs0)
+
+    late_arrays = gather_along(late_across, sizes)
+    own_diag, diag_places = end_to_end(diag_arrays, gathered_places(0, sizes[0], quarter // 2, sizes))
 
     def first_rows(tile, row):
         return tile < 2 * per_block, tile % per_block, row + jnp.where(tile < per_block, 0, quarter)
@@ -453,21 +475,29 @@
         return tile < 2 * per_block, tile % per_block, row + jnp.where(tile < per_block, quarter, 0)
 
     own_y0, other_y0, *y0 = solve(
-        tiles, rhs0, sizes, (diag_pairs, block_places, quarter // 2, first_rows), "solve_first"
+        tiles, rhs0, sizes, ([(own_diag, swap(own_diag))], [diag_places], quarter // 2, first_rows), "solve_first"
     )
-
-    late = gate(late, y0, own1, other1)
-    late_pairs = [(late, swap(late))]
-    late_places = [[(j * quarter, 0, (0, 0, j)) for j in range(2 * per_block)]]
-    late_group = (late_pairs, late_places, quarter, second_rows)
-    in_order = jnp.arange(2 * per_block)
     partial = trail_first(sensitivity, own_tile, y0, (*own0, *other0))
-    rhs1 = couple(in_order, rhs1, sizes, y0, late_group, 0)
-    own_y1, other_y1, *y1 = solve(in_order, gate(rhs1, partial), sizes, late_group, "solve_second", 1)
+    swapped_y0 = swap(other_y0)
+
+    ups = sizes[1]
+    held = (0, ups)
+    early = {k: swap(late_arrays[k]) for k in held}
+    late_arrays, early, rhs1, swapped_y0 = gate((late_arrays, early, rhs1, swapped_y0), partial)
+    pairs = [(array, early[k] if k in held else swap(array)) for k, array in enumerate(late_arrays)]
+    late_places = gathered_places(0, sizes[0], quarter, sizes)
+    couple_group = (pairs[:ups], late_places[:ups], quarter, second_rows)
+    second_group = (
+        pairs[ups:],
+        [[(start, row - quarter, place) for start, row, place in inner] for inner in late_places[ups:]],
+        quarter,
+        second_rows,
+    )
+    rhs1 = couple(tiles, rhs1, sizes, y0, couple_group, None)
+    own_y1, other_y1, *y1 = solve(tiles, rhs1, sizes, second_group, "solve_second")
     updated = trail_second(partial, y1, (*own1, *other1), col_tiles)
 
-    parts = [own_y0, swap(other_y0), own_y1, swap(other_y1)]
-    adjoint = place_unknowns(core.reshape(1).astype(jnp.int32), parts)
+    adjoint = place_unknowns(core.reshape(1).astype(jnp.int32), [own_y0, swapped_y0, own_y1, swap(other_y1)])
     return adjoint, updated
 
 

time: 224 us -> 179 us (0.80)
  local copies, waits for them, and re-layouts: 35.7 us -> 4.85 us
  between operations: 14.5 us -> 1.05 us
  waiting for transfers between devices: 53 us -> 42 us
  Pallas kernels: 82.6 us -> 92.7 us
    unnamed x78 -> x5, local copies, waits for them, and re-layouts: 25.2 us -> 0.11 us
    ppermute x1, waiting for transfers between devices: 14.8 us -> 5.3 us  [shards(): received = lax.ppermute(shared, 'pcol', partners)]
    ppermute x26 -> x33, waiting for transfers between devices: 38.2 us -> 33.2 us  [shift(): return lax.ppermute(value, 'pcol', pairs)]
    pallas_call x4, Pallas kernels: 22.1 us -> 26.2 us  [prepare(): pl.pallas_call(kernel, grid=(cycles,), out_shape=(out, out), in_specs=[pl...]
    ppermute x8, waiting for transfers between devices: 0.02 us -> 3.54 us  [shards(): swap = lambda value: lax.ppermute(value, 'prow', [(0, 1), (1, 0)])]
    ppermute x26 -> x33, starting transfers between devices: 30.1 us -> 32.7 us  [shift(): return lax.ppermute(value, 'pcol', pairs)]
    slice x8 -> x12, local copies, waits for them, and re-layouts: 2.78 us -> 0.29 us  [gather_across(): lower = jnp.concatenate([held[half:] for held in layers], axis=0)]
  transfers between devices with their start and end apart: 36 -> 42, of which waited for: 14 -> 14; matrix products, arithmetic and copies ran while one was open for 5% -> 3% of each run, Pallas kernels for 35% -> 46%
where the time goes in v3:
time: 179 us; the launch traced here: 178 us
  Pallas kernels  92.7 us (52%)
  waiting for transfers between devices  42 us (23%)
  starting transfers between devices  37.3 us (21%)
  local copies, waits for them, and re-layouts  4.85 us (3%)
    ppermute x33, waiting for transfers between devices, shift(): return lax.ppermute(value, 'pcol', pairs)  33.2 us
    ppermute x33, starting transfers between devices, shift(): return lax.ppermute(value, 'pcol', pairs)  32.7 us
    pallas_call x4, Pallas kernels, prepare(): pl.pallas_call(kernel, grid=(cycles,), out_shape=(out, out), in_specs=[pl...  26.2 us
    pallas_call x1, Pallas kernels, trail_second(): pl.pallas_call(kernel, grid=(tiles // group,), out_shape=jax.ShapeDtypeSt...  16.8 us
    pallas_call x1, Pallas kernels, trail_first(): pl.pallas_call(kernel, grid=(tiles // group,), out_shape=pltpu.HBM((rows,...  16.6 us
    pallas_call x2, Pallas kernels, solve(): pl.pallas_call(kernel, out_shape=(f32, f32, b16, b16), grid=(1,), in_spec...  12.7 us
    pallas_call x1, Pallas kernels, permute_columns(): pl.pallas_call(kernel, out_shape=[jax.ShapeDtypeStruct((rows, size), F32)...  11 us
    pallas_call x1, Pallas kernels, couple(): pl.pallas_call(kernel, out_shape=jax.ShapeDtypeStruct((rows, NB), F32), g...  5.6 us
  transfers between devices with their start and end apart: 42, of which 14 were waited for; matrix products, arithmetic and copies ran while one was open for 3% of the time, Pallas kernels for 46%

profile of v3, /device:TPU:0, one launch (start us, length us, event | category | flops | bytes accessed | tf_op | source)
XLA Modules:
  0.0 178.3 jit_solution(17493209276521900687)
XLA Ops:
  0.6 0.5 collective-permute-start.21
  1.1 1.7 slice.112
  2.9 2.6 %collective-permute-start = (f32[512,128]{1,0:T(8,128)S(1)}, f32[512,128]{1,0:T(8,128)S(1)}, u32[]{:S(2)}, u32[]{:S(2)}) collective-permute-start(f32[512,128]{1,0:T(8,128)S(1)} %bitcast.14), channel_id=1, source_target_pairs={{0,4},{1,5},{2,6},{3,7},{4,8},{5,9},{6,10},{7,11},{8,12},{9,13},{1... | collective-permute-start | bytes 786440 | tf_op jit(solution)/shard_map/ppermute | solution.py:53
  5.5 1.6 collective-permute-start.1
  7.1 1.5 collective-permute-start.2
  8.6 2.5 %fusion.11 = (f32[2,128,1,128]{3,2,1,0:T(1,128)S(1)}, f32[2,128,1,128]{3,2,1,0:T(1,128)S(1)}, f32[2,128,1,128]{3,2,1,0:T(1,128)S(1)}, f32[2,128,1,128]{3,2,1,0:T(1,128)S(1)}) fusion(f32[8,128,24,128]{3,2,1,0:T(8,128)} %param.3), kind=kLoop, calls=%fused_computation.74 | loop fusion | bytes 1048576 | tf_op jit(solution)/shard_map/slice | solution.py:424
  11.1 2.7 %collective-permute-start.3 = (f32[512,128]{1,0:T(8,128)S(1)}, f32[512,128]{1,0:T(8,128)S(1)}, u32[]{:S(2)}, u32[]{:S(2)}) collective-permute-start(f32[512,128]{1,0:T(8,128)S(1)} %pad_maximum_fusion.4), channel_id=1, source_target_pairs={{0,8},{1,9},{2,10},{3,11},{4,12},{5,13},{6,14},{7,15},{8,0},{9,1},... | collective-permute-start | bytes 786440 | tf_op jit(solution)/shard_map/ppermute | solution.py:414
  13.8 0.1 add_convert_fusion.keep_ref
  13.9 6.5 %prepare_own_first.1 = (bf16[512,3072]{1,0:T(8,128)(2,1)}, bf16[512,3072]{1,0:T(8,128)(2,1)}) custom-call(s32[2]{0:T(128)S(1)} %add_convert_fusion.keep_ref, f32[8,3072,128]{2,1,0:T(8,128)} %bitcast.12), custom_call_target="tpu_custom_call" | custom-call | bytes 18874368 | tf_op jit(solution)/shard_map/prepare_own_first/pallas_call | solution.py:170
  20.4 5.3 %collective-permute-done.3 = f32[512,128]{1,0:T(8,128)S(1)} collective-permute-done((f32[512,128]{1,0:T(8,128)S(1)}, f32[512,128]{1,0:T(8,128)S(1)}, u32[]{:S(2)}, u32[]{:S(2)}) %collective-permute-start.3) | collective-permute-done | bytes 262176 | tf_op jit(solution)/shard_map/ppermute | solution.py:414
  25.8 1.6 collective-permute-start.5
  27.4 1.5 collective-permute-start.6
  28.9 0.1 collective-permute-start.7
  29.0 6.5 %prepare_own_second.1 = (bf16[512,3072]{1,0:T(8,128)(2,1)}, bf16[512,3072]{1,0:T(8,128)(2,1)}) custom-call(s32[2]{0:T(128)S(1)} %add_convert_fusion.keep_ref, f32[8,3072,128]{2,1,0:T(8,128)} %bitcast.13), custom_call_target="tpu_custom_call" | custom-call | bytes 18874368 | tf_op jit(solution)/shard_map/prepare_own_second/pallas_call | solution.py:170
  35.6 0.5 collective-permute-start.13
  36.1 3.8 %collective-permute-done.7 = f32[256,128]{1,0:T(8,128)S(1)} collective-permute-done((f32[256,128]{1,0:T(8,128)S(1)}, f32[256,128]{1,0:T(8,128)S(1)}, u32[]{:S(2)}, u32[]{:S(2)}) %collective-permute-start.7) | collective-permute-done | bytes 131104 | tf_op jit(solution)/shard_map/ppermute | solution.py:53
  40.0 0.4 collective-permute-start.9
  40.4 0.1 dynamic_slice.3
  40.5 1.7 collective-permute-start.14
  42.2 0.9 collective-permute-done.13.refs_1_
  43.1 0.6 collective-permute-start.10
  43.8 2.7 %collective-permute-done.9 = f32[256,128]{1,0:T(8,128)S(1)} collective-permute-done((f32[256,128]{1,0:T(8,128)S(1)}, f32[256,128]{1,0:T(8,128)S(1)}, u32[]{:S(2)}, u32[]{:S(2)}) %collective-permute-start.9) | collective-permute-done | bytes 131104 | tf_op jit(solution)/shard_map/ppermute | solution.py:53
  46.5 1.6 collective-permute-done.10
  48.1 1.9 %collective-permute-start.11 = (f32[256,128]{1,0:T(8,128)S(1)}, f32[256,128]{1,0:T(8,128)S(1)}, u32[]{:S(2)}, u32[]{:S(2)}) collective-permute-start(f32[256,128]{1,0:T(8,128)S(1)} %collective-permute-done.7), channel_id=1, source_target_pairs={{0,4},{1,5},{2,6},{3,7},{4,8},{5,9},{6,10},{7,11},{8,12},{9,13},{1... | collective-permute-start | bytes 393224 | tf_op jit(solution)/shard_map/ppermute | solution.py:53
  50.0 1.4 collective-permute-start.19
  51.4 7.5 %collective-permute-done.11 = f32[256,128]{1,0:T(8,128)S(1)} collective-permute-done((f32[256,128]{1,0:T(8,128)S(1)}, f32[256,128]{1,0:T(8,128)S(1)}, u32[]{:S(2)}, u32[]{:S(2)}) %collective-permute-start.11) | collective-permute-done | bytes 131104 | tf_op jit(solution)/shard_map/ppermute | solution.py:53
  59.0 0.3 collective-permute-start.20
  59.3 1.8 collective-permute-start.15
  61.1 1.6 collective-permute-start.16
  62.7 4.7 %collective-permute-done.15 = f32[256,128]{1,0:T(8,128)S(1)} collective-permute-done((f32[256,128]{1,0:T(8,128)S(1)}, f32[256,128]{1,0:T(8,128)S(1)}, u32[]{:S(2)}, u32[]{:S(2)}) %collective-permute-start.15) | collective-permute-done | bytes 131104 | tf_op jit(solution)/shard_map/ppermute | solution.py:53
  67.6 6.5 %prepare_other_first.1 = (bf16[512,3072]{1,0:T(8,128)(2,1)}, bf16[512,3072]{1,0:T(8,128)(2,1)}) custom-call(s32[2]{0:T(128)S(1)} %add_convert_fusion.keep_ref, f32[8,3072,128]{2,1,0:T(8,128)} %bitcast.9.in_ref), custom_call_target="tpu_custom_call" | custom-call | bytes 18874368 | tf_op jit(solution)/shard_map/prepare_other_first/pallas_call | solution.py:170
  74.1 2.9 %collective-permute-done.17 = f32[256,128]{1,0:T(8,128)S(1)} collective-permute-done((f32[256,128]{1,0:T(8,128)S(1)}, f32[256,128]{1,0:T(8,128)S(1)}, u32[]{:S(2)}, u32[]{:S(2)}) %collective-permute-start.17) | collective-permute-done | bytes 131104 | tf_op jit(solution)/shard_map/ppermute | solution.py:53
  77.0 0.4 collective-permute-start.22
  77.4 1.8 collective-permute-start.23
  79.2 0.4 collective-permute-start.25
  79.6 1.7 collective-permute-start.26
  81.4 4.1 %collective-permute-done.22 = f32[512,128]{1,0:T(8,128)S(1)} collective-permute-done((f32[512,128]{1,0:T(8,128)S(1)}, f32[512,128]{1,0:T(8,128)S(1)}, u32[]{:S(2)}, u32[]{:S(2)}) %collective-permute-start.22) | collective-permute-done | bytes 262176 | tf_op jit(solution)/shard_map/ppermute | solution.py:53
  85.6 2.1 %collective-permute-start.27 = (f32[512,128]{1,0:T(8,128)S(1)}, f32[512,128]{1,0:T(8,128)S(1)}, u32[]{:S(2)}, u32[]{:S(2)}) collective-permute-start(f32[512,128]{1,0:T(8,128)S(1)} %pad_maximum_fusion.10.refs_12_), channel_id=1, source_target_pairs={{0,2},{1,3},{2,0},{3,1},{4,6},{5,7},{6,4},{7,5},{8,10},{9,11},{10,... | collective-permute-start | bytes 786440 | tf_op jit(solution)/shard_map/ppermute | solution.py:53
  87.7 0.4 collective-permute-start.28
  88.1 6.7 %prepare_other_second.1 = (bf16[512,3072]{1,0:T(8,128)(2,1)}, bf16[512,3072]{1,0:T(8,128)(2,1)}) custom-call(s32[2]{0:T(128)S(1)} %add_convert_fusion.keep_ref, f32[8,3072,128]{2,1,0:T(8,128)} %bitcast.9.in_ref), custom_call_target="tpu_custom_call" | custom-call | bytes 18874368 | tf_op jit(solution)/shard_map/prepare_other_second/pallas_call | solution.py:170
  94.9 2.1 %collective-permute-done.28.refs_15_ = f32[512,128]{1,0:T(8,128)S(1)} collective-permute-done((f32[512,128]{1,0:T(8,128)S(1)}, f32[512,128]{1,0:T(8,128)S(1)}, u32[]{:S(2)}, u32[]{:S(2)}) %collective-permute-start.28) | collective-permute-done | bytes 262176 | tf_op jit(solution)/shard_map/ppermute | solution.py:53
  97.0 0.4 collective-permute-start.29
  97.5 1.5 collective-permute-start.30
  99.0 0.6 collective-permute-start.31
  99.6 1.7 collective-permute-start.32
  101.3 11.0 %permute_columns.1 = (f32[512,1024]{1,0:T(8,128)S(1)}, f32[512,1024]{1,0:T(8,128)S(1)}, f32[512,128]{1,0:T(8,128)S(1)}) custom-call(s32[16]{0:T(128)S(1)} %fusion.2.tiles_ref, s32[1,2176]{1,0:T(1,128)S(1)} %reshape.25.wanted_ref, f32[512,128]{1,0:T(8,128)S(1)} %pad_maximum_fusion.2.refs_0_, f32[512,128]{1,0:T(8,128)S(1)} %collective-permute-done.13.refs_1_, ...), custom_call_target="tpu_custom_call" | custom-call | flops 9126805504 | bytes 8388608 | tf_op jit(solution)/shard_map/permute_columns/pallas_call | solution.py:138
  112.4 2.1 %collective-permute-done.31 = f32[1024,128]{1,0:T(8,128)S(1)} collective-permute-done((f32[1024,128]{1,0:T(8,128)S(1)}, f32[1024,128]{1,0:T(8,128)S(1)}, u32[]{:S(2)}, u32[]{:S(2)}) %collective-permute-start.31) | collective-permute-done | bytes 524320 | tf_op jit(solution)/shard_map/ppermute | solution.py:53
  114.5 0.6 collective-permute-done.32
  115.3 0.1 collective-permute-start.33
  115.4 1.5 collective-permute-start.34
  116.8 0.2 collective-permute-start.36
  117.0 1.1 collective-permute-start.35
  118.2 1.4 collective-permute-done.33.refs_1_
  119.5 6.3 %solve_first.1 = (f32[512,512]{1,0:T(8,128)S(1)}, f32[512,512]{1,0:T(8,128)S(1)}, bf16[512,1024]{1,0:T(8,128)(2,1)}, bf16[512,1024]{1,0:T(8,128)(2,1)}) custom-call(s32[16]{0:T(128)S(1)} %fusion.2.tiles_ref, f32[512,1024]{1,0:T(8,128)S(1)} %get-tuple-element.94.rhs_ref, f32[4096,128]{1,0:T(8,128)S(1)} %constant_dynamic-update-slice_fusion.20.refs_0_, ...), custom_call_target="tpu_custom_call" | custom-call | flops 3221225472 | bytes 8388608 | tf_op jit(solution)/shard_map/solve_first/pallas_call | solution.py:242
  125.8 0.1 collective-permute-start.38
  125.9 16.6 %trail_first.1.in_ref = f32[512,3072]{1,0:T(8,128)} custom-call(f32[512,24,128]{2,1,0:T(8,128)} %sens_ref.1, f32[512,128]{1,0:T(8,128)S(1)} %get-tuple-element.107.own_ref, bf16[512,1024]{1,0:T(8,128)(2,1)} %get-tuple-element.108.refs_0_.yh_ref, bf16[512,1024]{1,0:T(8,128)(2,1)} %get-tuple-element.109.refs_1_.yl_ref, ...), custom_call_target="tpu_custom_call" | custom-call | flops 9663676416 | bytes 25165824 | tf_op jit(solution)/shard_map/trail_first/pallas_call | solution.py:320
  142.6 0.4 collective-permute-start.39
  143.0 0.1 collective-permute-start.40
  143.2 2.2 %collective-permute-done.39.refs_3_ = f32[2048,128]{1,0:T(8,128)S(1)} collective-permute-done((f32[2048,128]{1,0:T(8,128)S(1)}, f32[2048,128]{1,0:T(8,128)S(1)}, u32[]{:S(2)}, u32[]{:S(2)}) %collective-permute-start.39) | collective-permute-done | bytes 1048608 | tf_op jit(solution)/shard_map/ppermute | solution.py:404
  145.3 5.6 %couple.1.rhs_ref = f32[512,1024]{1,0:T(8,128)S(1)} custom-call(s32[16]{0:T(128)S(1)} %fusion.2.tiles_ref, f32[512,1024]{1,0:T(8,128)S(1)} %get-tuple-element.110.rhs_ref, bf16[512,1024]{1,0:T(8,128)(2,1)} %get-tuple-element.108.refs_0_.yh_ref, bf16[512,1024]{1,0:T(8,128)(2,1)} %get-tuple-element.109.refs_1_.yl_ref, ...), custom_call_target="tpu_custom_call" | custom-call | flops 3221225472 | bytes 8388608 | tf_op jit(solution)/shard_map/couple/pallas_call | solution.py:271
  150.9 6.4 %solve_second.1 = (f32[512,512]{1,0:T(8,128)S(1)}, f32[512,512]{1,0:T(8,128)}, bf16[512,1024]{1,0:T(8,128)(2,1)}, bf16[512,1024]{1,0:T(8,128)(2,1)}) custom-call(s32[16]{0:T(128)S(1)} %fusion.2.tiles_ref, f32[512,1024]{1,0:T(8,128)S(1)} %couple.1.rhs_ref, f32[2048,128]{1,0:T(8,128)S(1)} %constant_dynamic-update-slice_fusion.15.refs_0_, ...), custom_call_target="tpu_custom_call" | custom-call | flops 3221225472 | bytes 8388608 | tf_op jit(solution)/shard_map/solve_second/pallas_call | solution.py:242
  157.4 0.4 collective-permute-start.41
  157.8 16.8 %trail_second.1 = f32[512,24,128]{2,1,0:T(8,128)} custom-call(f32[512,3072]{1,0:T(8,128)} %trail_first.1.in_ref, bf16[512,1024]{1,0:T(8,128)(2,1)} %get-tuple-element.120.refs_0_, bf16[512,1024]{1,0:T(8,128)(2,1)} %get-tuple-element.121.refs_1_, bf16[512,3072]{1,0:T(8,128)(2,1)} %get-tuple-element.68.refs_2_, bf16[512,3072]{1,0:T(8,128)(2,1)} %get-tuple-element.69.refs_3_, ...), custom_call_target="tpu_custom_call" | custom-call | flops 9663676416 | bytes 25165824 | tf_op jit(solution)/shard_map/trail_second/pallas_call | solution.py:350
  174.6 3.8 %place_unknowns.1 = f32[1024,8,128]{2,1,0:T(8,128)} custom-call(s32[1]{0:T(128)} %bitcast.core_ref, f32[512,512]{1,0:T(8,128)S(1)} %get-tuple-element.102.refs_0_, f32[512,512]{1,0:T(8,128)S(1)} %get-tuple-element.117.refs_1_, f32[512,512]{1,0:T(8,128)S(1)} %collective-permute-done.38.refs_2_, f32[512,512]{1,0:T(8,128)} %collective-permute-done.41.refs_3_), custom_call_target="tpu_custom_call" | custom-call | tf_op jit(solution)/shard_map/place_unknowns/pallas_call | solution.py:379
  (75 shorter events, 1.2 us)
Async XLA Ops:
  0.6 66.9 %collective-permute-start.21 = (f32[8,128,24,128]{3,2,1,0:T(8,128)}, f32[8,128,24,128]{3,2,1,0:T(8,128)}, u32[]{:S(2)}, u32[]{:S(2)}) collective-permute-start(f32[8,128,24,128]{3,2,1,0:T(8,128)} %param.3), channel_id=1, source_target_pairs={{0,16},{16,0},{1,17},{17,1},{2,18},{18,2},{3,19},{19,3},{4,20},{20... | collective-permute-start | bytes 37748744 | tf_op jit(solution)/shard_map/ppermute | solution.py:404
  2.9 22.9 %collective-permute-start = (f32[512,128]{1,0:T(8,128)S(1)}, f32[512,128]{1,0:T(8,128)S(1)}, u32[]{:S(2)}, u32[]{:S(2)}) collective-permute-start(f32[512,128]{1,0:T(8,128)S(1)} %bitcast.14), channel_id=1, source_target_pairs={{0,4},{1,5},{2,6},{3,7},{4,8},{5,9},{6,10},{7,11},{8,12},{9,13},{1... | collective-permute-start | bytes 786440 | tf_op jit(solution)/shard_map/ppermute | solution.py:53
  5.5 14.8 %collective-permute-start.1 = (f32[256,128]{1,0:T(8,128)S(1)}, f32[256,128]{1,0:T(8,128)S(1)}, u32[]{:S(2)}, u32[]{:S(2)}) collective-permute-start(f32[256,128]{1,0:T(8,128)S(1)} %get-tuple-element.152), channel_id=1, source_target_pairs={{0,1},{1,0},{2,3},{3,2},{4,5},{5,4},{6,7},{7,6},{8,9},{9,8},{10,11... | collective-permute-start | bytes 393224 | tf_op jit(solution)/shard_map/ppermute | solution.py:53
  7.1 13.3 %collective-permute-start.2 = (f32[256,128]{1,0:T(8,128)S(1)}, f32[256,128]{1,0:T(8,128)S(1)}, u32[]{:S(2)}, u32[]{:S(2)}) collective-permute-start(f32[256,128]{1,0:T(8,128)S(1)} %get-tuple-element.151), channel_id=1, source_target_pairs={{0,2},{1,3},{2,0},{3,1},{4,6},{5,7},{6,4},{7,5},{8,10},{9,11},{10,... | collective-permute-start | bytes 393224 | tf_op jit(solution)/shard_map/ppermute | solution.py:53
  11.1 14.6 %collective-permute-start.3 = (f32[512,128]{1,0:T(8,128)S(1)}, f32[512,128]{1,0:T(8,128)S(1)}, u32[]{:S(2)}, u32[]{:S(2)}) collective-permute-start(f32[512,128]{1,0:T(8,128)S(1)} %pad_maximum_fusion.4), channel_id=1, source_target_pairs={{0,8},{1,9},{2,10},{3,11},{4,12},{5,13},{6,14},{7,15},{8,0},{9,1},... | collective-permute-start | bytes 786440 | tf_op jit(solution)/shard_map/ppermute | solution.py:414
  25.8 9.7 %collective-permute-start.5 = (f32[256,128]{1,0:T(8,128)S(1)}, f32[256,128]{1,0:T(8,128)S(1)}, u32[]{:S(2)}, u32[]{:S(2)}) collective-permute-start(f32[256,128]{1,0:T(8,128)S(1)} %get-tuple-element.149), channel_id=1, source_target_pairs={{0,1},{1,0},{2,3},{3,2},{4,5},{5,4},{6,7},{7,6},{8,9},{9,8},{10,11... | collective-permute-start | bytes 393224 | tf_op jit(solution)/shard_map/ppermute | solution.py:53
  27.4 12.6 %collective-permute-start.4 = (f32[512,128]{1,0:T(8,128)S(1)}, f32[512,128]{1,0:T(8,128)S(1)}, u32[]{:S(2)}, u32[]{:S(2)}) collective-permute-start(f32[512,128]{1,0:T(8,128)S(1)} %collective-permute-done), channel_id=1, source_target_pairs={{0,4},{1,5},{2,6},{3,7},{4,8},{5,9},{6,10},{7,11},{8,12},{9,13},{1... | collective-permute-start | bytes 786440 | tf_op jit(solution)/shard_map/ppermute | solution.py:53
  27.4 13.0 %copy-start = (s32[2048]{0:T(1024)S(1)}, s32[2048]{0:T(1024)}, u32[]{:S(2)}) copy-start(s32[2048]{0:T(1024)} %param.5) | copy-start | bytes 24580
  27.4 8.7 %collective-permute-start.6 = (f32[256,128]{1,0:T(8,128)S(1)}, f32[256,128]{1,0:T(8,128)S(1)}, u32[]{:S(2)}, u32[]{:S(2)}) collective-permute-start(f32[256,128]{1,0:T(8,128)S(1)} %get-tuple-element.148), channel_id=1, source_target_pairs={{0,2},{1,3},{2,0},{3,1},{4,6},{5,7},{6,4},{7,5},{8,10},{9,11},{10,... | collective-permute-start | bytes 393224 | tf_op jit(solution)/shard_map/ppermute | solution.py:53
  28.9 11.0 %collective-permute-start.7 = (f32[256,128]{1,0:T(8,128)S(1)}, f32[256,128]{1,0:T(8,128)S(1)}, u32[]{:S(2)}, u32[]{:S(2)}) collective-permute-start(f32[256,128]{1,0:T(8,128)S(1)} %get-tuple-element.64), channel_id=1, source_target_pairs={{0,4},{1,5},{2,6},{3,7},{4,8},{5,9},{6,10},{7,11},{8,12},{9,13},{1... | collective-permute-start | bytes 393224 | tf_op jit(solution)/shard_map/ppermute | solution.py:53
  35.6 7.6 %collective-permute-start.13 = (f32[512,128]{1,0:T(8,128)S(1)}, f32[512,128]{1,0:T(8,128)S(1)}, u32[]{:S(2)}, u32[]{:S(2)}) collective-permute-start(f32[512,128]{1,0:T(8,128)S(1)} %pad_maximum_fusion.2.refs_0_), channel_id=1, source_target_pairs={{0,2},{1,3},{2,0},{3,1},{4,6},{5,7},{6,4},{7,5},{8,10},{9,11},{10,... | collective-permute-start | bytes 786440 | tf_op jit(solution)/shard_map/ppermute | solution.py:53
  40.0 6.5 %collective-permute-start.9 = (f32[256,128]{1,0:T(8,128)S(1)}, f32[256,128]{1,0:T(8,128)S(1)}, u32[]{:S(2)}, u32[]{:S(2)}) collective-permute-start(f32[256,128]{1,0:T(8,128)S(1)} %get-tuple-element.147), channel_id=1, source_target_pairs={{0,1},{1,0},{2,3},{3,2},{4,5},{5,4},{6,7},{7,6},{8,9},{9,8},{10,11... | collective-permute-start | bytes 393224 | tf_op jit(solution)/shard_map/ppermute | solution.py:53
  40.5 9.5 %collective-permute-start.14 = (f32[512,128]{1,0:T(8,128)S(1)}, f32[512,128]{1,0:T(8,128)S(1)}, u32[]{:S(2)}, u32[]{:S(2)}) collective-permute-start(f32[512,128]{1,0:T(8,128)S(1)} %pad_maximum_fusion.3.refs_2_), channel_id=1, source_target_pairs={{0,1},{1,0},{2,3},{3,2},{4,5},{5,4},{6,7},{7,6},{8,9},{9,8},{10,11... | collective-permute-start | bytes 786440 | tf_op jit(solution)/shard_map/ppermute | solution.py:53
  42.2 17.1 %collective-permute-start.8 = (f32[512,128]{1,0:T(8,128)S(1)}, f32[512,128]{1,0:T(8,128)S(1)}, u32[]{:S(2)}, u32[]{:S(2)}) collective-permute-start(f32[512,128]{1,0:T(8,128)S(1)} %collective-permute-done.4), channel_id=1, source_target_pairs={{0,4},{1,5},{2,6},{3,7},{4,8},{5,9},{6,10},{7,11},{8,12},{9,13},{1... | collective-permute-start | bytes 786440 | tf_op jit(solution)/shard_map/ppermute | solution.py:53
  43.1 5.0 %collective-permute-start.10 = (f32[256,128]{1,0:T(8,128)S(1)}, f32[256,128]{1,0:T(8,128)S(1)}, u32[]{:S(2)}, u32[]{:S(2)}) collective-permute-start(f32[256,128]{1,0:T(8,128)S(1)} %get-tuple-element.146), channel_id=1, source_target_pairs={{0,2},{1,3},{2,0},{3,1},{4,6},{5,7},{6,4},{7,5},{8,10},{9,11},{10,... | collective-permute-start | bytes 393224 | tf_op jit(solution)/shard_map/ppermute | solution.py:53
  46.5 12.8 %collective-permute-start.12 = (f32[512,128]{1,0:T(8,128)S(1)}, f32[512,128]{1,0:T(8,128)S(1)}, u32[]{:S(2)}, u32[]{:S(2)}) collective-permute-start(f32[512,128]{1,0:T(8,128)S(1)} %pad_maximum_fusion.5), channel_id=1, source_target_pairs={{0,4},{1,5},{2,6},{3,7},{4,8},{5,9},{6,10},{7,11},{8,12},{9,13},{1... | collective-permute-start | bytes 786440 | tf_op jit(solution)/shard_map/ppermute | solution.py:53
  48.1 10.9 %collective-permute-start.11 = (f32[256,128]{1,0:T(8,128)S(1)}, f32[256,128]{1,0:T(8,128)S(1)}, u32[]{:S(2)}, u32[]{:S(2)}) collective-permute-start(f32[256,128]{1,0:T(8,128)S(1)} %collective-permute-done.7), channel_id=1, source_target_pairs={{0,4},{1,5},{2,6},{3,7},{4,8},{5,9},{6,10},{7,11},{8,12},{9,13},{1... | collective-permute-start | bytes 393224 | tf_op jit(solution)/shard_map/ppermute | solution.py:53
  50.0 24.0 %collective-permute-start.19 = (f32[512,128]{1,0:T(8,128)S(1)}, f32[512,128]{1,0:T(8,128)S(1)}, u32[]{:S(2)}, u32[]{:S(2)}) collective-permute-start(f32[512,128]{1,0:T(8,128)S(1)} %pad_maximum_fusion.6.refs_4_), channel_id=1, source_target_pairs={{0,2},{1,3},{2,0},{3,1},{4,6},{5,7},{6,4},{7,5},{8,10},{9,11},{10,... | collective-permute-start | bytes 786440 | tf_op jit(solution)/shard_map/ppermute | solution.py:53
  59.0 15.1 %collective-permute-start.20 = (f32[512,128]{1,0:T(8,128)S(1)}, f32[512,128]{1,0:T(8,128)S(1)}, u32[]{:S(2)}, u32[]{:S(2)}) collective-permute-start(f32[512,128]{1,0:T(8,128)S(1)} %pad_maximum_fusion.7.refs_6_), channel_id=1, source_target_pairs={{0,1},{1,0},{2,3},{3,2},{4,5},{5,4},{6,7},{7,6},{8,9},{9,8},{10,11... | collective-permute-start | bytes 786440 | tf_op jit(solution)/shard_map/ppermute | solution.py:53
  59.3 8.1 %collective-permute-start.15 = (f32[256,128]{1,0:T(8,128)S(1)}, f32[256,128]{1,0:T(8,128)S(1)}, u32[]{:S(2)}, u32[]{:S(2)}) collective-permute-start(f32[256,128]{1,0:T(8,128)S(1)} %get-tuple-element.145), channel_id=1, source_target_pairs={{0,1},{1,0},{2,3},{3,2},{4,5},{5,4},{6,7},{7,6},{8,9},{9,8},{10,11... | collective-permute-start | bytes 393224 | tf_op jit(solution)/shard_map/ppermute | solution.py:53
  61.1 6.3 %collective-permute-start.16 = (f32[256,128]{1,0:T(8,128)S(1)}, f32[256,128]{1,0:T(8,128)S(1)}, u32[]{:S(2)}, u32[]{:S(2)}) collective-permute-start(f32[256,128]{1,0:T(8,128)S(1)} %get-tuple-element.144), channel_id=1, source_target_pairs={{0,2},{1,3},{2,0},{3,1},{4,6},{5,7},{6,4},{7,5},{8,10},{9,11},{10,... | collective-permute-start | bytes 393224 | tf_op jit(solution)/shard_map/ppermute | solution.py:53
  67.4 9.6 %collective-permute-start.18 = (f32[512,128]{1,0:T(8,128)S(1)}, f32[512,128]{1,0:T(8,128)S(1)}, u32[]{:S(2)}, u32[]{:S(2)}) collective-permute-start(f32[512,128]{1,0:T(8,128)S(1)} %collective-permute-done.12), channel_id=1, source_target_pairs={{0,4},{1,5},{2,6},{3,7},{4,8},{5,9},{6,10},{7,11},{8,12},{9,13},{1... | collective-permute-start | bytes 786440 | tf_op jit(solution)/shard_map/ppermute | solution.py:53
  67.4 9.5 %collective-permute-start.17 = (f32[256,128]{1,0:T(8,128)S(1)}, f32[256,128]{1,0:T(8,128)S(1)}, u32[]{:S(2)}, u32[]{:S(2)}) collective-permute-start(f32[256,128]{1,0:T(8,128)S(1)} %collective-permute-done.11), channel_id=1, source_target_pairs={{0,4},{1,5},{2,6},{3,7},{4,8},{5,9},{6,10},{7,11},{8,12},{9,13},{1... | collective-permute-start | bytes 393224 | tf_op jit(solution)/shard_map/ppermute | solution.py:53
  77.0 8.5 %collective-permute-start.22 = (f32[512,128]{1,0:T(8,128)S(1)}, f32[512,128]{1,0:T(8,128)S(1)}, u32[]{:S(2)}, u32[]{:S(2)}) collective-permute-start(f32[512,128]{1,0:T(8,128)S(1)} %pad_maximum_fusion.12), channel_id=1, source_target_pairs={{0,1},{1,0},{2,3},{3,2},{4,5},{5,4},{6,7},{7,6},{8,9},{9,8},{10,11... | collective-permute-start | bytes 786440 | tf_op jit(solution)/shard_map/ppermute | solution.py:53
  77.4 10.3 %collective-permute-start.23 = (f32[512,128]{1,0:T(8,128)S(1)}, f32[512,128]{1,0:T(8,128)S(1)}, u32[]{:S(2)}, u32[]{:S(2)}) collective-permute-start(f32[512,128]{1,0:T(8,128)S(1)} %pad_maximum_fusion.13), channel_id=1, source_target_pairs={{0,2},{1,3},{2,0},{3,1},{4,6},{5,7},{6,4},{7,5},{8,10},{9,11},{10,... | collective-permute-start | bytes 786440 | tf_op jit(solution)/shard_map/ppermute | solution.py:53
  79.2 15.6 %collective-permute-start.25 = (f32[512,128]{1,0:T(8,128)S(1)}, f32[512,128]{1,0:T(8,128)S(1)}, u32[]{:S(2)}, u32[]{:S(2)}) collective-permute-start(f32[512,128]{1,0:T(8,128)S(1)} %pad_maximum_fusion.8.refs_8_), channel_id=1, source_target_pairs={{0,2},{1,3},{2,0},{3,1},{4,6},{5,7},{6,4},{7,5},{8,10},{9,11},{10,... | collective-permute-start | bytes 786440 | tf_op jit(solution)/shard_map/ppermute | solution.py:53
  79.6 15.2 %collective-permute-start.26 = (f32[512,128]{1,0:T(8,128)S(1)}, f32[512,128]{1,0:T(8,128)S(1)}, u32[]{:S(2)}, u32[]{:S(2)}) collective-permute-start(f32[512,128]{1,0:T(8,128)S(1)} %pad_maximum_fusion.9.refs_10_), channel_id=1, source_target_pairs={{0,1},{1,0},{2,3},{3,2},{4,5},{5,4},{6,7},{7,6},{8,9},{9,8},{10,11... | collective-permute-start | bytes 786440 | tf_op jit(solution)/shard_map/ppermute | solution.py:53
  81.4 13.5 %collective-permute-start.24 = (f32[512,128]{1,0:T(8,128)S(1)}, f32[512,128]{1,0:T(8,128)S(1)}, u32[]{:S(2)}, u32[]{:S(2)}) collective-permute-start(f32[512,128]{1,0:T(8,128)S(1)} %collective-permute-done.18), channel_id=1, source_target_pairs={{0,4},{1,5},{2,6},{3,7},{4,8},{5,9},{6,10},{7,11},{8,12},{9,13},{1... | collective-permute-start | bytes 786440 | tf_op jit(solution)/shard_map/ppermute | solution.py:53
  85.6 9.3 %collective-permute-start.27 = (f32[512,128]{1,0:T(8,128)S(1)}, f32[512,128]{1,0:T(8,128)S(1)}, u32[]{:S(2)}, u32[]{:S(2)}) collective-permute-start(f32[512,128]{1,0:T(8,128)S(1)} %pad_maximum_fusion.10.refs_12_), channel_id=1, source_target_pairs={{0,2},{1,3},{2,0},{3,1},{4,6},{5,7},{6,4},{7,5},{8,10},{9,11},{10,... | collective-permute-start | bytes 786440 | tf_op jit(solution)/shard_map/ppermute | solution.py:53
  87.7 9.2 %collective-permute-start.28 = (f32[512,128]{1,0:T(8,128)S(1)}, f32[512,128]{1,0:T(8,128)S(1)}, u32[]{:S(2)}, u32[]{:S(2)}) collective-permute-start(f32[512,128]{1,0:T(8,128)S(1)} %pad_maximum_fusion.11.refs_14_), channel_id=1, source_target_pairs={{0,1},{1,0},{2,3},{3,2},{4,5},{5,4},{6,7},{7,6},{8,9},{9,8},{10,11... | collective-permute-start | bytes 786440 | tf_op jit(solution)/shard_map/ppermute | solution.py:53
  97.0 15.2 %collective-permute-start.29 = (f32[1024,128]{1,0:T(8,128)S(1)}, f32[1024,128]{1,0:T(8,128)S(1)}, u32[]{:S(2)}, u32[]{:S(2)}) collective-permute-start(f32[1024,128]{1,0:T(8,128)S(1)} %pad_maximum_fusion), channel_id=1, source_target_pairs={{0,1},{1,0},{2,3},{3,2},{4,5},{5,4},{6,7},{7,6},{8,9},{9,8},{10,11... | collective-permute-start | bytes 1572872 | tf_op jit(solution)/shard_map/ppermute | solution.py:53
  97.5 14.8 %collective-permute-start.30 = (f32[1024,128]{1,0:T(8,128)S(1)}, f32[1024,128]{1,0:T(8,128)S(1)}, u32[]{:S(2)}, u32[]{:S(2)}) collective-permute-start(f32[1024,128]{1,0:T(8,128)S(1)} %pad_maximum_fusion.1), channel_id=1, source_target_pairs={{0,2},{1,3},{2,0},{3,1},{4,6},{5,7},{6,4},{7,5},{8,10},{9,11},{10,... | collective-permute-start | bytes 1572872 | tf_op jit(solution)/shard_map/ppermute | solution.py:53
  99.0 15.5 %collective-permute-start.31 = (f32[1024,128]{1,0:T(8,128)S(1)}, f32[1024,128]{1,0:T(8,128)S(1)}, u32[]{:S(2)}, u32[]{:S(2)}) collective-permute-start(f32[1024,128]{1,0:T(8,128)S(1)} %constant_dynamic-update-slice_fusion), channel_id=1, source_target_pairs={{0,2},{1,3},{2,0},{3,1},{4,6},{5,7},{6,4},{7,5},{8,10},{9,11},{10,... | collective-permute-start | bytes 1572872 | tf_op jit(solution)/shard_map/ppermute | solution.py:53
  99.6 15.6 %collective-permute-start.32 = (f32[1024,128]{1,0:T(8,128)S(1)}, f32[1024,128]{1,0:T(8,128)S(1)}, u32[]{:S(2)}, u32[]{:S(2)}) collective-permute-start(f32[1024,128]{1,0:T(8,128)S(1)} %constant_dynamic-update-slice_fusion.5), channel_id=1, source_target_pairs={{0,1},{1,0},{2,3},{3,2},{4,5},{5,4},{6,7},{7,6},{8,9},{9,8},{10,11... | collective-permute-start | bytes 1572872 | tf_op jit(solution)/shard_map/ppermute | solution.py:53
  115.3 4.2 %collective-permute-start.33 = (f32[4096,128]{1,0:T(8,128)S(1)}, f32[4096,128]{1,0:T(8,128)S(1)}, u32[]{:S(2)}, u32[]{:S(2)}) collective-permute-start(f32[4096,128]{1,0:T(8,128)S(1)} %constant_dynamic-update-slice_fusion.20.refs_0_), channel_id=1, source_target_pairs={{0,16},{16,0},{1,17},{17,1},{2,18},{18,2},{3,19},{19,3},{4,20},{20... | collective-permute-start | bytes 6291464 | tf_op jit(solution)/shard_map/ppermute | solution.py:404
  115.4 27.2 %collective-permute-start.34 = (f32[2048,128]{1,0:T(8,128)S(1)}, f32[2048,128]{1,0:T(8,128)S(1)}, u32[]{:S(2)}, u32[]{:S(2)}) collective-permute-start(f32[2048,128]{1,0:T(8,128)S(1)} %constant_dynamic-update-slice_fusion.10.refs_0_), channel_id=1, source_target_pairs={{0,2},{1,3},{2,0},{3,1},{4,6},{5,7},{6,4},{7,5},{8,10},{9,11},{10,... | collective-permute-start | bytes 3145736 | tf_op jit(solution)/shard_map/ppermute | solution.py:53
  116.8 25.7 %collective-permute-start.36 = (f32[2048,128]{1,0:T(8,128)S(1)}, f32[2048,128]{1,0:T(8,128)S(1)}, u32[]{:S(2)}, u32[]{:S(2)}) collective-permute-start(f32[2048,128]{1,0:T(8,128)S(1)} %constant_dynamic-update-slice_fusion.10.refs_0_), channel_id=1, source_target_pairs={{0,16},{16,0},{1,17},{17,1},{2,18},{18,2},{3,19},{19,3},{4,20},{20... | collective-permute-start | bytes 3145736 | tf_op jit(solution)/shard_map/ppermute | solution.py:404
  117.0 25.6 %collective-permute-start.35 = (f32[2048,128]{1,0:T(8,128)S(1)}, f32[2048,128]{1,0:T(8,128)S(1)}, u32[]{:S(2)}, u32[]{:S(2)}) collective-permute-start(f32[2048,128]{1,0:T(8,128)S(1)} %constant_dynamic-update-slice_fusion.15.refs_0_), channel_id=1, source_target_pairs={{0,1},{1,0},{2,3},{3,2},{4,5},{5,4},{6,7},{7,6},{8,9},{9,8},{10,11... | collective-permute-start | bytes 3145736 | tf_op jit(solution)/shard_map/ppermute | solution.py:53
  118.1 24.5 %collective-permute-start.37 = (f32[2048,128]{1,0:T(8,128)S(1)}, f32[2048,128]{1,0:T(8,128)S(1)}, u32[]{:S(2)}, u32[]{:S(2)}) collective-permute-start(f32[2048,128]{1,0:T(8,128)S(1)} %constant_dynamic-update-slice_fusion.15.refs_0_), channel_id=1, source_target_pairs={{0,16},{16,0},{1,17},{17,1},{2,18},{18,2},{3,19},{19,3},{4,20},{20... | collective-permute-start | bytes 3145736 | tf_op jit(solution)/shard_map/ppermute | solution.py:404
  125.8 16.8 %collective-permute-start.38 = (f32[512,512]{1,0:T(8,128)S(1)}, f32[512,512]{1,0:T(8,128)S(1)}, u32[]{:S(2)}, u32[]{:S(2)}) collective-permute-start(f32[512,512]{1,0:T(8,128)S(1)} %get-tuple-element.106), channel_id=1, source_target_pairs={{0,16},{16,0},{1,17},{17,1},{2,18},{18,2},{3,19},{19,3},{4,20},{20... | collective-permute-start | bytes 3145736 | tf_op jit(solution)/shard_map/ppermute | solution.py:404
  142.6 2.7 %collective-permute-start.39 = (f32[2048,128]{1,0:T(8,128)S(1)}, f32[2048,128]{1,0:T(8,128)S(1)}, u32[]{:S(2)}, u32[]{:S(2)}) collective-permute-start(f32[2048,128]{1,0:T(8,128)S(1)} %collective-permute-done.34.refs_2_), channel_id=1, source_target_pairs={{0,16},{16,0},{1,17},{17,1},{2,18},{18,2},{3,19},{19,3},{4,20},{20... | collective-permute-start | bytes 3145736 | tf_op jit(solution)/shard_map/ppermute | solution.py:404
  143.0 7.9 %collective-permute-start.40 = (f32[2048,128]{1,0:T(8,128)S(1)}, f32[2048,128]{1,0:T(8,128)S(1)}, u32[]{:S(2)}, u32[]{:S(2)}) collective-permute-start(f32[2048,128]{1,0:T(8,128)S(1)} %collective-permute-done.35.refs_2_), channel_id=1, source_target_pairs={{0,16},{16,0},{1,17},{17,1},{2,18},{18,2},{3,19},{19,3},{4,20},{20... | collective-permute-start | bytes 3145736 | tf_op jit(solution)/shard_map/ppermute | solution.py:404
  157.4 17.2 %collective-permute-start.41 = (f32[512,512]{1,0:T(8,128)}, f32[512,512]{1,0:T(8,128)}, u32[]{:S(2)}, u32[]{:S(2)}) collective-permute-start(f32[512,512]{1,0:T(8,128)} %get-tuple-element.119), channel_id=1, source_target_pairs={{0,16},{16,0},{1,17},{17,1},{2,18},{18,2},{3,19},{19,3},{4,20},{20... | collective-permute-start | bytes 3145736 | tf_op jit(solution)/shard_map/ppermute | solution.py:404

commit v4 on v3

--- a/solution.py
+++ b/solution.py
@@ -215,7 +215,7 @@
     return [spec] * len(operands)
 
 
-def solve(tiles, rhs, sizes, diagonal, name, chosen=None):
+def solve(tiles, rhs, sizes, diagonal, name, chosen=None, to_hbm=False):
     rows = rhs.shape[0]
     per_block = NB // 128
     half = NB // 2
@@ -237,14 +237,17 @@
 
     vmem = pl.BlockSpec(memory_space=pltpu.VMEM)
     f32 = jax.ShapeDtypeStruct((rows, half), F32)
-    b16 = pltpu.HBM((rows, NB), BF16)
-    whole = pl.BlockSpec((rows, NB), lambda i: (0, 0), pipeline_mode=pl.Buffered(1))
+    b16 = jax.ShapeDtypeStruct((rows, NB), BF16)
+    halves_spec = vmem
+    if to_hbm:
+        b16 = pltpu.HBM((rows, NB), BF16)
+        halves_spec = pl.BlockSpec((rows, NB), lambda i: (0, 0), pipeline_mode=pl.Buffered(1))
     return pl.pallas_call(
         kernel,
         out_shape=(f32, f32, b16, b16),
         grid=(1,),
         in_specs=[pl.BlockSpec(memory_space=pltpu.SMEM), vmem, *block_specs(operands, chosen)],
-        out_specs=(vmem, vmem, whole, whole),
+        out_specs=(vmem, vmem, halves_spec, halves_spec),
         scratch_shapes=[pltpu.VMEM((per_block, NB, 128), BF16)] * 2,
         compiler_params=pltpu.CompilerParams(vmem_limit_bytes=24 * MIB),
         cost_estimate=pl.CostEstimate(flops=6 * rows * NB * NB, transcendentals=0, bytes_accessed=8 * NB * NB),
@@ -267,22 +270,23 @@
             out_ref[to] = rhs_ref[to] - mul3(left, right, NN)
 
     vmem = pl.BlockSpec(memory_space=pltpu.VMEM)
-    whole = pl.BlockSpec((rows, NB), lambda i: (0, 0), pipeline_mode=pl.Buffered(1))
     return pl.pallas_call(
         kernel,
         out_shape=jax.ShapeDtypeStruct((rows, NB), F32),
         grid=(1,),
-        in_specs=[pl.BlockSpec(memory_space=pltpu.SMEM), vmem, whole, whole, *block_specs(operands, chosen)],
+        in_specs=[pl.BlockSpec(memory_space=pltpu.SMEM), vmem, vmem, vmem, *block_specs(operands, chosen)],
         out_specs=vmem,
         scratch_shapes=[pltpu.VMEM((per_block, NB, 128), BF16)] * 2,
         compiler_params=pltpu.CompilerParams(vmem_limit_bytes=22 * MIB),
         cost_estimate=pl.CostEstimate(flops=6 * rows * NB * NB, transcendentals=0, bytes_accessed=8 * NB * NB),
         name="couple",
-    )(tiles, rhs, *in_hbm(solved), *operands)
-
-
-def trail_specs(rows, wide):
+    )(tiles, rhs, *solved, *operands)
+
+
+def trail_specs(rows, wide, in_vmem):
     whole = pl.BlockSpec((rows, NB), lambda i: (0, 0), pipeline_mode=pl.Buffered(1))
+    if in_vmem:
+        whole = pl.BlockSpec(memory_space=pltpu.VMEM)
     part = pl.BlockSpec((NB // 2, wide), lambda i: (0, i))
     return [whole, whole, part, part, part, part]
 
@@ -324,13 +328,13 @@
         in_specs=[
             pl.BlockSpec((rows, group, width), lambda i: (0, i, 0)),
             pl.BlockSpec((rows, width), lambda i: (0, 0)),
-            *trail_specs(rows, wide),
+            *trail_specs(rows, wide, True),
         ],
         out_specs=pl.BlockSpec((rows, wide), lambda i: (0, i)),
         compiler_params=pltpu.CompilerParams(vmem_limit_bytes=24 * MIB),
         cost_estimate=trail_cost(rows, tiles),
         name="trail_first",
-    )(*in_hbm([sensitivity]), own_tile, *in_hbm([*solved, *halves]))
+    )(*in_hbm([sensitivity]), own_tile, *solved, *in_hbm(halves))
 
 
 def trail_second(partial, solved, halves, tiles):
@@ -351,7 +355,7 @@
         kernel,
         grid=(tiles // group,),
         out_shape=jax.ShapeDtypeStruct((rows, tiles, width), F32),
-        in_specs=[pl.BlockSpec((rows, wide), lambda i: (0, i)), *trail_specs(rows, wide)],
+        in_specs=[pl.BlockSpec((rows, wide), lambda i: (0, i)), *trail_specs(rows, wide, False)],
         out_specs=pl.BlockSpec((rows, group, width), lambda i: (0, i, 0)),
         compiler_params=pltpu.CompilerParams(vmem_limit_bytes=24 * MIB),
         cost_estimate=trail_cost(rows, tiles),
@@ -494,7 +498,7 @@
         second_rows,
     )
     rhs1 = couple(tiles, rhs1, sizes, y0, couple_group, None)
-    own_y1, other_y1, *y1 = solve(tiles, rhs1, sizes, second_group, "solve_second")
+    own_y1, other_y1, *y1 = solve(tiles, rhs1, sizes, second_group, "solve_second", to_hbm=True)
     updated = trail_second(partial, y1, (*own1, *other1), col_tiles)
 
     adjoint = place_unknowns(core.reshape(1).astype(jnp.int32), [own_y0, swapped_y0, own_y1, swap(other_y1)])

time: 179 us -> 177 us (0.989)
  Pallas kernels: 92.7 us -> 88.5 us
  waiting for transfers between devices: 42 us -> 45 us
    ppermute x33, waiting for transfers between devices: 33.2 us -> 36.1 us  [shift(): return lax.ppermute(value, 'pcol', pairs)]
    pallas_call x1, Pallas kernels: 16.6 us -> 14.8 us  [trail_first(): pl.pallas_call(kernel, grid=(tiles // group,), out_shape=pltpu.HBM((rows,...]
  transfers between devices with their start and end apart: 42 -> 42, of which waited for: 14 -> 16; matrix products, arithmetic and copies ran while one was open for 3% -> 3% of each run, Pallas kernels for 46% -> 44%
where the time goes in v4:
time: 177 us
  Pallas kernels  88.5 us (50%)
  waiting for transfers between devices  45 us (25%)
  starting transfers between devices  37.1 us (21%)
  local copies, waits for them, and re-layouts  4.85 us (3%)
    ppermute x33, waiting for transfers between devices, shift(): return lax.ppermute(value, 'pcol', pairs)  36.1 us
    ppermute x33, starting transfers between devices, shift(): return lax.ppermute(value, 'pcol', pairs)  32.7 us
    pallas_call x4, Pallas kernels, prepare(): pl.pallas_call(kernel, grid=(cycles,), out_shape=(out, out), in_specs=[pl...  26.2 us
    pallas_call x1, Pallas kernels, trail_second(): pl.pallas_call(kernel, grid=(tiles // group,), out_shape=jax.ShapeDtypeSt...  16.8 us
    pallas_call x1, Pallas kernels, trail_first(): pl.pallas_call(kernel, grid=(tiles // group,), out_shape=pltpu.HBM((rows,...  14.8 us
    pallas_call x2, Pallas kernels, solve(): pl.pallas_call(kernel, out_shape=(f32, f32, b16, b16), grid=(1,), in_spec...  11.3 us
    pallas_call x1, Pallas kernels, permute_columns(): pl.pallas_call(kernel, out_shape=[jax.ShapeDtypeStruct((rows, size), F32)...  11 us
    ppermute x1, waiting for transfers between devices, shards(): received = lax.ppermute(shared, 'pcol', partners)  5.3 us
  transfers between devices with their start and end apart: 42, of which 16 were waited for; matrix products, arithmetic and copies ran while one was open for 3% of the time, Pallas kernels for 44%

profile of v4, /device:TPU:0, one launch (start us, length us, event | category | flops | bytes accessed | tf_op | source)
XLA Modules:
  0.0 176.9 jit_solution(11957747200679923403)
XLA Ops:
  0.6 0.5 collective-permute-start.21
  1.1 1.7 slice.112
  2.9 2.6 %collective-permute-start = (f32[512,128]{1,0:T(8,128)S(1)}, f32[512,128]{1,0:T(8,128)S(1)}, u32[]{:S(2)}, u32[]{:S(2)}) collective-permute-start(f32[512,128]{1,0:T(8,128)S(1)} %bitcast.14), channel_id=1, source_target_pairs={{0,4},{1,5},{2,6},{3,7},{4,8},{5,9},{6,10},{7,11},{8,12},{9,13},{1... | collective-permute-start | bytes 786440 | tf_op jit(solution)/shard_map/ppermute | solution.py:53
  5.5 1.6 collective-permute-start.1
  7.1 1.5 collective-permute-start.2
  8.6 2.5 %fusion.11 = (f32[2,128,1,128]{3,2,1,0:T(1,128)S(1)}, f32[2,128,1,128]{3,2,1,0:T(1,128)S(1)}, f32[2,128,1,128]{3,2,1,0:T(1,128)S(1)}, f32[2,128,1,128]{3,2,1,0:T(1,128)S(1)}) fusion(f32[8,128,24,128]{3,2,1,0:T(8,128)} %param.3), kind=kLoop, calls=%fused_computation.74 | loop fusion | bytes 1048576 | tf_op jit(solution)/shard_map/slice | solution.py:428
  11.1 2.7 %collective-permute-start.3 = (f32[512,128]{1,0:T(8,128)S(1)}, f32[512,128]{1,0:T(8,128)S(1)}, u32[]{:S(2)}, u32[]{:S(2)}) collective-permute-start(f32[512,128]{1,0:T(8,128)S(1)} %pad_maximum_fusion.4), channel_id=1, source_target_pairs={{0,8},{1,9},{2,10},{3,11},{4,12},{5,13},{6,14},{7,15},{8,0},{9,1},... | collective-permute-start | bytes 786440 | tf_op jit(solution)/shard_map/ppermute | solution.py:418
  13.8 0.1 add_convert_fusion.keep_ref
  13.9 6.5 %prepare_own_first.1 = (bf16[512,3072]{1,0:T(8,128)(2,1)}, bf16[512,3072]{1,0:T(8,128)(2,1)}) custom-call(s32[2]{0:T(128)S(1)} %add_convert_fusion.keep_ref, f32[8,3072,128]{2,1,0:T(8,128)} %bitcast.12), custom_call_target="tpu_custom_call" | custom-call | bytes 18874368 | tf_op jit(solution)/shard_map/prepare_own_first/pallas_call | solution.py:170
  20.4 5.3 %collective-permute-done.3 = f32[512,128]{1,0:T(8,128)S(1)} collective-permute-done((f32[512,128]{1,0:T(8,128)S(1)}, f32[512,128]{1,0:T(8,128)S(1)}, u32[]{:S(2)}, u32[]{:S(2)}) %collective-permute-start.3) | collective-permute-done | bytes 262176 | tf_op jit(solution)/shard_map/ppermute | solution.py:418
  25.8 1.6 collective-permute-start.5
  27.4 1.5 collective-permute-start.6
  28.9 0.1 collective-permute-start.7
  29.0 6.5 %prepare_own_second.1 = (bf16[512,3072]{1,0:T(8,128)(2,1)}, bf16[512,3072]{1,0:T(8,128)(2,1)}) custom-call(s32[2]{0:T(128)S(1)} %add_convert_fusion.keep_ref, f32[8,3072,128]{2,1,0:T(8,128)} %bitcast.13), custom_call_target="tpu_custom_call" | custom-call | bytes 18874368 | tf_op jit(solution)/shard_map/prepare_own_second/pallas_call | solution.py:170
  35.6 0.5 collective-permute-start.13
  36.1 3.8 %collective-permute-done.7 = f32[256,128]{1,0:T(8,128)S(1)} collective-permute-done((f32[256,128]{1,0:T(8,128)S(1)}, f32[256,128]{1,0:T(8,128)S(1)}, u32[]{:S(2)}, u32[]{:S(2)}) %collective-permute-start.7) | collective-permute-done | bytes 131104 | tf_op jit(solution)/shard_map/ppermute | solution.py:53
  40.0 0.4 collective-permute-start.9
  40.4 0.1 dynamic_slice.3
  40.5 1.7 collective-permute-start.14
  42.2 0.9 collective-permute-done.13.refs_1_
  43.1 0.6 collective-permute-start.10
  43.8 2.7 %collective-permute-done.9 = f32[256,128]{1,0:T(8,128)S(1)} collective-permute-done((f32[256,128]{1,0:T(8,128)S(1)}, f32[256,128]{1,0:T(8,128)S(1)}, u32[]{:S(2)}, u32[]{:S(2)}) %collective-permute-start.9) | collective-permute-done | bytes 131104 | tf_op jit(solution)/shard_map/ppermute | solution.py:53
  46.5 1.6 collective-permute-done.10
  48.1 1.9 %collective-permute-start.11 = (f32[256,128]{1,0:T(8,128)S(1)}, f32[256,128]{1,0:T(8,128)S(1)}, u32[]{:S(2)}, u32[]{:S(2)}) collective-permute-start(f32[256,128]{1,0:T(8,128)S(1)} %collective-permute-done.7), channel_id=1, source_target_pairs={{0,4},{1,5},{2,6},{3,7},{4,8},{5,9},{6,10},{7,11},{8,12},{9,13},{1... | collective-permute-start | bytes 393224 | tf_op jit(solution)/shard_map/ppermute | solution.py:53
  50.0 1.4 collective-permute-start.19
  51.4 7.5 %collective-permute-done.11 = f32[256,128]{1,0:T(8,128)S(1)} collective-permute-done((f32[256,128]{1,0:T(8,128)S(1)}, f32[256,128]{1,0:T(8,128)S(1)}, u32[]{:S(2)}, u32[]{:S(2)}) %collective-permute-start.11) | collective-permute-done | bytes 131104 | tf_op jit(solution)/shard_map/ppermute | solution.py:53
  59.0 0.3 collective-permute-start.20
  59.3 1.8 collective-permute-start.15
  61.1 1.6 collective-permute-start.16
  62.7 4.7 %collective-permute-done.15 = f32[256,128]{1,0:T(8,128)S(1)} collective-permute-done((f32[256,128]{1,0:T(8,128)S(1)}, f32[256,128]{1,0:T(8,128)S(1)}, u32[]{:S(2)}, u32[]{:S(2)}) %collective-permute-start.15) | collective-permute-done | bytes 131104 | tf_op jit(solution)/shard_map/ppermute | solution.py:53
  67.6 6.5 %prepare_other_first.1 = (bf16[512,3072]{1,0:T(8,128)(2,1)}, bf16[512,3072]{1,0:T(8,128)(2,1)}) custom-call(s32[2]{0:T(128)S(1)} %add_convert_fusion.keep_ref, f32[8,3072,128]{2,1,0:T(8,128)} %bitcast.9.in_ref), custom_call_target="tpu_custom_call" | custom-call | bytes 18874368 | tf_op jit(solution)/shard_map/prepare_other_first/pallas_call | solution.py:170
  74.1 2.9 %collective-permute-done.17 = f32[256,128]{1,0:T(8,128)S(1)} collective-permute-done((f32[256,128]{1,0:T(8,128)S(1)}, f32[256,128]{1,0:T(8,128)S(1)}, u32[]{:S(2)}, u32[]{:S(2)}) %collective-permute-start.17) | collective-permute-done | bytes 131104 | tf_op jit(solution)/shard_map/ppermute | solution.py:53
  77.0 0.4 collective-permute-start.22
  77.4 1.8 %collective-permute-start.23 = (f32[512,128]{1,0:T(8,128)S(1)}, f32[512,128]{1,0:T(8,128)S(1)}, u32[]{:S(2)}, u32[]{:S(2)}) collective-permute-start(f32[512,128]{1,0:T(8,128)S(1)} %pad_maximum_fusion.13), channel_id=1, source_target_pairs={{0,2},{1,3},{2,0},{3,1},{4,6},{5,7},{6,4},{7,5},{8,10},{9,11},{10,... | collective-permute-start | bytes 786440 | tf_op jit(solution)/shard_map/ppermute | solution.py:53
  79.2 0.4 collective-permute-start.25
  79.6 1.7 collective-permute-start.26
  81.4 4.1 %collective-permute-done.22 = f32[512,128]{1,0:T(8,128)S(1)} collective-permute-done((f32[512,128]{1,0:T(8,128)S(1)}, f32[512,128]{1,0:T(8,128)S(1)}, u32[]{:S(2)}, u32[]{:S(2)}) %collective-permute-start.22) | collective-permute-done | bytes 262176 | tf_op jit(solution)/shard_map/ppermute | solution.py:53
  85.6 2.1 %collective-permute-start.27 = (f32[512,128]{1,0:T(8,128)S(1)}, f32[512,128]{1,0:T(8,128)S(1)}, u32[]{:S(2)}, u32[]{:S(2)}) collective-permute-start(f32[512,128]{1,0:T(8,128)S(1)} %pad_maximum_fusion.10.refs_12_), channel_id=1, source_target_pairs={{0,2},{1,3},{2,0},{3,1},{4,6},{5,7},{6,4},{7,5},{8,10},{9,11},{10,... | collective-permute-start | bytes 786440 | tf_op jit(solution)/shard_map/ppermute | solution.py:53
  87.7 0.4 collective-permute-start.28
  88.1 6.7 %prepare_other_second.1 = (bf16[512,3072]{1,0:T(8,128)(2,1)}, bf16[512,3072]{1,0:T(8,128)(2,1)}) custom-call(s32[2]{0:T(128)S(1)} %add_convert_fusion.keep_ref, f32[8,3072,128]{2,1,0:T(8,128)} %bitcast.9.in_ref), custom_call_target="tpu_custom_call" | custom-call | bytes 18874368 | tf_op jit(solution)/shard_map/prepare_other_second/pallas_call | solution.py:170
  94.9 2.1 %collective-permute-done.28.refs_15_ = f32[512,128]{1,0:T(8,128)S(1)} collective-permute-done((f32[512,128]{1,0:T(8,128)S(1)}, f32[512,128]{1,0:T(8,128)S(1)}, u32[]{:S(2)}, u32[]{:S(2)}) %collective-permute-start.28) | collective-permute-done | bytes 262176 | tf_op jit(solution)/shard_map/ppermute | solution.py:53
  97.0 0.4 collective-permute-start.29
  97.5 1.5 collective-permute-start.30
  99.0 0.6 collective-permute-start.31
  99.6 1.7 collective-permute-start.32
  101.3 11.0 %permute_columns.1 = (f32[512,1024]{1,0:T(8,128)S(1)}, f32[512,1024]{1,0:T(8,128)S(1)}, f32[512,128]{1,0:T(8,128)S(1)}) custom-call(s32[16]{0:T(128)S(1)} %fusion.2.tiles_ref, s32[1,2176]{1,0:T(1,128)S(1)} %reshape.25.wanted_ref, f32[512,128]{1,0:T(8,128)S(1)} %pad_maximum_fusion.2.refs_0_, f32[512,128]{1,0:T(8,128)S(1)} %collective-permute-done.13.refs_1_, ...), custom_call_target="tpu_custom_call" | custom-call | flops 9126805504 | bytes 8388608 | tf_op jit(solution)/shard_map/permute_columns/pallas_call | solution.py:138
  112.4 2.1 %collective-permute-done.31 = f32[1024,128]{1,0:T(8,128)S(1)} collective-permute-done((f32[1024,128]{1,0:T(8,128)S(1)}, f32[1024,128]{1,0:T(8,128)S(1)}, u32[]{:S(2)}, u32[]{:S(2)}) %collective-permute-start.31) | collective-permute-done | bytes 524320 | tf_op jit(solution)/shard_map/ppermute | solution.py:53
  114.5 0.6 collective-permute-done.32
  115.4 1.5 collective-permute-start.34
  116.8 0.2 collective-permute-start.36
  117.0 1.1 collective-permute-start.35
  118.2 1.4 collective-permute-done.33.refs_1_
  119.5 4.9 %solve_first.1 = (f32[512,512]{1,0:T(8,128)S(1)}, f32[512,512]{1,0:T(8,128)S(1)}, bf16[512,1024]{1,0:T(8,128)(2,1)S(1)}, bf16[512,1024]{1,0:T(8,128)(2,1)S(1)}) custom-call(s32[16]{0:T(128)S(1)} %fusion.2.tiles_ref, f32[512,1024]{1,0:T(8,128)S(1)} %get-tuple-element.94.rhs_ref, f32[4096,128]{1,0:T(8,128)S(1)} %constant_dynamic-update-slice_fusion.20.refs_0_, ...), custom_call_target="tpu_custom_call" | custom-call | flops 3221225472 | bytes 8388608 | tf_op jit(solution)/shard_map/solve_first/pallas_call | solution.py:245
  124.4 0.2 collective-permute-start.38
  124.6 14.8 %trail_first.1.in_ref = f32[512,3072]{1,0:T(8,128)} custom-call(f32[512,24,128]{2,1,0:T(8,128)} %sens_ref.1, f32[512,128]{1,0:T(8,128)S(1)} %get-tuple-element.107.own_ref, bf16[512,1024]{1,0:T(8,128)(2,1)S(1)} %get-tuple-element.108.refs_0_.yh_ref, bf16[512,1024]{1,0:T(8,128)(2,1)S(1)} %get-tuple-element.109.refs_1_.yl_ref, ...), custom_call_target="tpu_custom_call" | custom-call | flops 9663676416 | bytes 25165824 | tf_op jit(solution)/shard_map/trail_first/pallas_call | solution.py:324
  139.4 1.5 collective-permute-done.34.refs_2_
  141.0 1.5 collective-permute-done.35.refs_2_
  142.5 0.5 collective-permute-start.40
  143.0 2.1 %collective-permute-done.39.refs_3_ = f32[2048,128]{1,0:T(8,128)S(1)} collective-permute-done((f32[2048,128]{1,0:T(8,128)S(1)}, f32[2048,128]{1,0:T(8,128)S(1)}, u32[]{:S(2)}, u32[]{:S(2)}) %collective-permute-start.39) | collective-permute-done | bytes 1048608 | tf_op jit(solution)/shard_map/ppermute | solution.py:408
  145.2 4.6 %couple.1.rhs_ref = f32[512,1024]{1,0:T(8,128)S(1)} custom-call(s32[16]{0:T(128)S(1)} %fusion.2.tiles_ref, f32[512,1024]{1,0:T(8,128)S(1)} %get-tuple-element.110.rhs_ref, bf16[512,1024]{1,0:T(8,128)(2,1)S(1)} %get-tuple-element.108.refs_0_.yh_ref, bf16[512,1024]{1,0:T(8,128)(2,1)S(1)} %get-tuple-element.109.refs_1_.yl_ref, ...), custom_call_target="tpu_custom_call" | custom-call | flops 3221225472 | bytes 8388608 | tf_op jit(solution)/shard_map/couple/pallas_call | solution.py:273
  149.8 6.4 %solve_second.1 = (f32[512,512]{1,0:T(8,128)S(1)}, f32[512,512]{1,0:T(8,128)}, bf16[512,1024]{1,0:T(8,128)(2,1)}, bf16[512,1024]{1,0:T(8,128)(2,1)}) custom-call(s32[16]{0:T(128)S(1)} %fusion.2.tiles_ref, f32[512,1024]{1,0:T(8,128)S(1)} %couple.1.rhs_ref, f32[2048,128]{1,0:T(8,128)S(1)} %constant_dynamic-update-slice_fusion.15.refs_0_, ...), custom_call_target="tpu_custom_call" | custom-call | flops 3221225472 | bytes 8388608 | tf_op jit(solution)/shard_map/solve_second/pallas_call | solution.py:245
  156.2 0.1 collective-permute-start.41
  156.4 16.8 %trail_second.1 = f32[512,24,128]{2,1,0:T(8,128)} custom-call(f32[512,3072]{1,0:T(8,128)} %trail_first.1.in_ref, bf16[512,1024]{1,0:T(8,128)(2,1)} %get-tuple-element.120.refs_0_, bf16[512,1024]{1,0:T(8,128)(2,1)} %get-tuple-element.121.refs_1_, bf16[512,3072]{1,0:T(8,128)(2,1)} %get-tuple-element.68.refs_2_, bf16[512,3072]{1,0:T(8,128)(2,1)} %get-tuple-element.69.refs_3_, ...), custom_call_target="tpu_custom_call" | custom-call | flops 9663676416 | bytes 25165824 | tf_op jit(solution)/shard_map/trail_second/pallas_call | solution.py:354
  173.2 3.8 %place_unknowns.1 = f32[1024,8,128]{2,1,0:T(8,128)} custom-call(s32[1]{0:T(128)} %bitcast.core_ref, f32[512,512]{1,0:T(8,128)S(1)} %get-tuple-element.102.refs_0_, f32[512,512]{1,0:T(8,128)S(1)} %get-tuple-element.117.refs_1_, f32[512,512]{1,0:T(8,128)S(1)} %collective-permute-done.38.refs_2_, f32[512,512]{1,0:T(8,128)} %collective-permute-done.41.refs_3_), custom_call_target="tpu_custom_call" | custom-call | tf_op jit(solution)/shard_map/place_unknowns/pallas_call | solution.py:383
  (75 shorter events, 1.3 us)
Async XLA Ops:
  0.6 66.9 %collective-permute-start.21 = (f32[8,128,24,128]{3,2,1,0:T(8,128)}, f32[8,128,24,128]{3,2,1,0:T(8,128)}, u32[]{:S(2)}, u32[]{:S(2)}) collective-permute-start(f32[8,128,24,128]{3,2,1,0:T(8,128)} %param.3), channel_id=1, source_target_pairs={{0,16},{16,0},{1,17},{17,1},{2,18},{18,2},{3,19},{19,3},{4,20},{20... | collective-permute-start | bytes 37748744 | tf_op jit(solution)/shard_map/ppermute | solution.py:408
  2.9 22.9 %collective-permute-start = (f32[512,128]{1,0:T(8,128)S(1)}, f32[512,128]{1,0:T(8,128)S(1)}, u32[]{:S(2)}, u32[]{:S(2)}) collective-permute-start(f32[512,128]{1,0:T(8,128)S(1)} %bitcast.14), channel_id=1, source_target_pairs={{0,4},{1,5},{2,6},{3,7},{4,8},{5,9},{6,10},{7,11},{8,12},{9,13},{1... | collective-permute-start | bytes 786440 | tf_op jit(solution)/shard_map/ppermute | solution.py:53
  5.5 14.8 %collective-permute-start.1 = (f32[256,128]{1,0:T(8,128)S(1)}, f32[256,128]{1,0:T(8,128)S(1)}, u32[]{:S(2)}, u32[]{:S(2)}) collective-permute-start(f32[256,128]{1,0:T(8,128)S(1)} %get-tuple-element.152), channel_id=1, source_target_pairs={{0,1},{1,0},{2,3},{3,2},{4,5},{5,4},{6,7},{7,6},{8,9},{9,8},{10,11... | collective-permute-start | bytes 393224 | tf_op jit(solution)/shard_map/ppermute | solution.py:53
  7.1 13.3 %collective-permute-start.2 = (f32[256,128]{1,0:T(8,128)S(1)}, f32[256,128]{1,0:T(8,128)S(1)}, u32[]{:S(2)}, u32[]{:S(2)}) collective-permute-start(f32[256,128]{1,0:T(8,128)S(1)} %get-tuple-element.151), channel_id=1, source_target_pairs={{0,2},{1,3},{2,0},{3,1},{4,6},{5,7},{6,4},{7,5},{8,10},{9,11},{10,... | collective-permute-start | bytes 393224 | tf_op jit(solution)/shard_map/ppermute | solution.py:53
  11.1 14.6 %collective-permute-start.3 = (f32[512,128]{1,0:T(8,128)S(1)}, f32[512,128]{1,0:T(8,128)S(1)}, u32[]{:S(2)}, u32[]{:S(2)}) collective-permute-start(f32[512,128]{1,0:T(8,128)S(1)} %pad_maximum_fusion.4), channel_id=1, source_target_pairs={{0,8},{1,9},{2,10},{3,11},{4,12},{5,13},{6,14},{7,15},{8,0},{9,1},... | collective-permute-start | bytes 786440 | tf_op jit(solution)/shard_map/ppermute | solution.py:418
  25.8 9.7 %collective-permute-start.5 = (f32[256,128]{1,0:T(8,128)S(1)}, f32[256,128]{1,0:T(8,128)S(1)}, u32[]{:S(2)}, u32[]{:S(2)}) collective-permute-start(f32[256,128]{1,0:T(8,128)S(1)} %get-tuple-element.149), channel_id=1, source_target_pairs={{0,1},{1,0},{2,3},{3,2},{4,5},{5,4},{6,7},{7,6},{8,9},{9,8},{10,11... | collective-permute-start | bytes 393224 | tf_op jit(solution)/shard_map/ppermute | solution.py:53
  27.4 12.6 %collective-permute-start.4 = (f32[512,128]{1,0:T(8,128)S(1)}, f32[512,128]{1,0:T(8,128)S(1)}, u32[]{:S(2)}, u32[]{:S(2)}) collective-permute-start(f32[512,128]{1,0:T(8,128)S(1)} %collective-permute-done), channel_id=1, source_target_pairs={{0,4},{1,5},{2,6},{3,7},{4,8},{5,9},{6,10},{7,11},{8,12},{9,13},{1... | collective-permute-start | bytes 786440 | tf_op jit(solution)/shard_map/ppermute | solution.py:53
  27.4 13.0 %copy-start = (s32[2048]{0:T(1024)S(1)}, s32[2048]{0:T(1024)}, u32[]{:S(2)}) copy-start(s32[2048]{0:T(1024)} %param.5) | copy-start | bytes 24580
  27.4 8.7 %collective-permute-start.6 = (f32[256,128]{1,0:T(8,128)S(1)}, f32[256,128]{1,0:T(8,128)S(1)}, u32[]{:S(2)}, u32[]{:S(2)}) collective-permute-start(f32[256,128]{1,0:T(8,128)S(1)} %get-tuple-element.148), channel_id=1, source_target_pairs={{0,2},{1,3},{2,0},{3,1},{4,6},{5,7},{6,4},{7,5},{8,10},{9,11},{10,... | collective-permute-start | bytes 393224 | tf_op jit(solution)/shard_map/ppermute | solution.py:53
  28.9 11.0 %collective-permute-start.7 = (f32[256,128]{1,0:T(8,128)S(1)}, f32[256,128]{1,0:T(8,128)S(1)}, u32[]{:S(2)}, u32[]{:S(2)}) collective-permute-start(f32[256,128]{1,0:T(8,128)S(1)} %get-tuple-element.64), channel_id=1, source_target_pairs={{0,4},{1,5},{2,6},{3,7},{4,8},{5,9},{6,10},{7,11},{8,12},{9,13},{1... | collective-permute-start | bytes 393224 | tf_op jit(solution)/shard_map/ppermute | solution.py:53
  35.6 7.6 %collective-permute-start.13 = (f32[512,128]{1,0:T(8,128)S(1)}, f32[512,128]{1,0:T(8,128)S(1)}, u32[]{:S(2)}, u32[]{:S(2)}) collective-permute-start(f32[512,128]{1,0:T(8,128)S(1)} %pad_maximum_fusion.2.refs_0_), channel_id=1, source_target_pairs={{0,2},{1,3},{2,0},{3,1},{4,6},{5,7},{6,4},{7,5},{8,10},{9,11},{10,... | collective-permute-start | bytes 786440 | tf_op jit(solution)/shard_map/ppermute | solution.py:53
  40.0 6.5 %collective-permute-start.9 = (f32[256,128]{1,0:T(8,128)S(1)}, f32[256,128]{1,0:T(8,128)S(1)}, u32[]{:S(2)}, u32[]{:S(2)}) collective-permute-start(f32[256,128]{1,0:T(8,128)S(1)} %get-tuple-element.147), channel_id=1, source_target_pairs={{0,1},{1,0},{2,3},{3,2},{4,5},{5,4},{6,7},{7,6},{8,9},{9,8},{10,11... | collective-permute-start | bytes 393224 | tf_op jit(solution)/shard_map/ppermute | solution.py:53
  40.5 9.5 %collective-permute-start.14 = (f32[512,128]{1,0:T(8,128)S(1)}, f32[512,128]{1,0:T(8,128)S(1)}, u32[]{:S(2)}, u32[]{:S(2)}) collective-permute-start(f32[512,128]{1,0:T(8,128)S(1)} %pad_maximum_fusion.3.refs_2_), channel_id=1, source_target_pairs={{0,1},{1,0},{2,3},{3,2},{4,5},{5,4},{6,7},{7,6},{8,9},{9,8},{10,11... | collective-permute-start | bytes 786440 | tf_op jit(solution)/shard_map/ppermute | solution.py:53
  42.2 17.1 %collective-permute-start.8 = (f32[512,128]{1,0:T(8,128)S(1)}, f32[512,128]{1,0:T(8,128)S(1)}, u32[]{:S(2)}, u32[]{:S(2)}) collective-permute-start(f32[512,128]{1,0:T(8,128)S(1)} %collective-permute-done.4), channel_id=1, source_target_pairs={{0,4},{1,5},{2,6},{3,7},{4,8},{5,9},{6,10},{7,11},{8,12},{9,13},{1... | collective-permute-start | bytes 786440 | tf_op jit(solution)/shard_map/ppermute | solution.py:53
  43.1 5.0 %collective-permute-start.10 = (f32[256,128]{1,0:T(8,128)S(1)}, f32[256,128]{1,0:T(8,128)S(1)}, u32[]{:S(2)}, u32[]{:S(2)}) collective-permute-start(f32[256,128]{1,0:T(8,128)S(1)} %get-tuple-element.146), channel_id=1, source_target_pairs={{0,2},{1,3},{2,0},{3,1},{4,6},{5,7},{6,4},{7,5},{8,10},{9,11},{10,... | collective-permute-start | bytes 393224 | tf_op jit(solution)/shard_map/ppermute | solution.py:53
  46.5 12.8 %collective-permute-start.12 = (f32[512,128]{1,0:T(8,128)S(1)}, f32[512,128]{1,0:T(8,128)S(1)}, u32[]{:S(2)}, u32[]{:S(2)}) collective-permute-start(f32[512,128]{1,0:T(8,128)S(1)} %pad_maximum_fusion.5), channel_id=1, source_target_pairs={{0,4},{1,5},{2,6},{3,7},{4,8},{5,9},{6,10},{7,11},{8,12},{9,13},{1... | collective-permute-start | bytes 786440 | tf_op jit(solution)/shard_map/ppermute | solution.py:53
  48.1 10.9 %collective-permute-start.11 = (f32[256,128]{1,0:T(8,128)S(1)}, f32[256,128]{1,0:T(8,128)S(1)}, u32[]{:S(2)}, u32[]{:S(2)}) collective-permute-start(f32[256,128]{1,0:T(8,128)S(1)} %collective-permute-done.7), channel_id=1, source_target_pairs={{0,4},{1,5},{2,6},{3,7},{4,8},{5,9},{6,10},{7,11},{8,12},{9,13},{1... | collective-permute-start | bytes 393224 | tf_op jit(solution)/shard_map/ppermute | solution.py:53
  50.0 24.0 %collective-permute-start.19 = (f32[512,128]{1,0:T(8,128)S(1)}, f32[512,128]{1,0:T(8,128)S(1)}, u32[]{:S(2)}, u32[]{:S(2)}) collective-permute-start(f32[512,128]{1,0:T(8,128)S(1)} %pad_maximum_fusion.6.refs_4_), channel_id=1, source_target_pairs={{0,2},{1,3},{2,0},{3,1},{4,6},{5,7},{6,4},{7,5},{8,10},{9,11},{10,... | collective-permute-start | bytes 786440 | tf_op jit(solution)/shard_map/ppermute | solution.py:53
  59.0 15.1 %collective-permute-start.20 = (f32[512,128]{1,0:T(8,128)S(1)}, f32[512,128]{1,0:T(8,128)S(1)}, u32[]{:S(2)}, u32[]{:S(2)}) collective-permute-start(f32[512,128]{1,0:T(8,128)S(1)} %pad_maximum_fusion.7.refs_6_), channel_id=1, source_target_pairs={{0,1},{1,0},{2,3},{3,2},{4,5},{5,4},{6,7},{7,6},{8,9},{9,8},{10,11... | collective-permute-start | bytes 786440 | tf_op jit(solution)/shard_map/ppermute | solution.py:53
  59.3 8.1 %collective-permute-start.15 = (f32[256,128]{1,0:T(8,128)S(1)}, f32[256,128]{1,0:T(8,128)S(1)}, u32[]{:S(2)}, u32[]{:S(2)}) collective-permute-start(f32[256,128]{1,0:T(8,128)S(1)} %get-tuple-element.145), channel_id=1, source_target_pairs={{0,1},{1,0},{2,3},{3,2},{4,5},{5,4},{6,7},{7,6},{8,9},{9,8},{10,11... | collective-permute-start | bytes 393224 | tf_op jit(solution)/shard_map/ppermute | solution.py:53
  61.1 6.3 %collective-permute-start.16 = (f32[256,128]{1,0:T(8,128)S(1)}, f32[256,128]{1,0:T(8,128)S(1)}, u32[]{:S(2)}, u32[]{:S(2)}) collective-permute-start(f32[256,128]{1,0:T(8,128)S(1)} %get-tuple-element.144), channel_id=1, source_target_pairs={{0,2},{1,3},{2,0},{3,1},{4,6},{5,7},{6,4},{7,5},{8,10},{9,11},{10,... | collective-permute-start | bytes 393224 | tf_op jit(solution)/shard_map/ppermute | solution.py:53
  67.4 9.6 %collective-permute-start.18 = (f32[512,128]{1,0:T(8,128)S(1)}, f32[512,128]{1,0:T(8,128)S(1)}, u32[]{:S(2)}, u32[]{:S(2)}) collective-permute-start(f32[512,128]{1,0:T(8,128)S(1)} %collective-permute-done.12), channel_id=1, source_target_pairs={{0,4},{1,5},{2,6},{3,7},{4,8},{5,9},{6,10},{7,11},{8,12},{9,13},{1... | collective-permute-start | bytes 786440 | tf_op jit(solution)/shard_map/ppermute | solution.py:53
  67.4 9.5 %collective-permute-start.17 = (f32[256,128]{1,0:T(8,128)S(1)}, f32[256,128]{1,0:T(8,128)S(1)}, u32[]{:S(2)}, u32[]{:S(2)}) collective-permute-start(f32[256,128]{1,0:T(8,128)S(1)} %collective-permute-done.11), channel_id=1, source_target_pairs={{0,4},{1,5},{2,6},{3,7},{4,8},{5,9},{6,10},{7,11},{8,12},{9,13},{1... | collective-permute-start | bytes 393224 | tf_op jit(solution)/shard_map/ppermute | solution.py:53
  77.0 8.5 %collective-permute-start.22 = (f32[512,128]{1,0:T(8,128)S(1)}, f32[512,128]{1,0:T(8,128)S(1)}, u32[]{:S(2)}, u32[]{:S(2)}) collective-permute-start(f32[512,128]{1,0:T(8,128)S(1)} %pad_maximum_fusion.12), channel_id=1, source_target_pairs={{0,1},{1,0},{2,3},{3,2},{4,5},{5,4},{6,7},{7,6},{8,9},{9,8},{10,11... | collective-permute-start | bytes 786440 | tf_op jit(solution)/shard_map/ppermute | solution.py:53
  77.4 10.3 %collective-permute-start.23 = (f32[512,128]{1,0:T(8,128)S(1)}, f32[512,128]{1,0:T(8,128)S(1)}, u32[]{:S(2)}, u32[]{:S(2)}) collective-permute-start(f32[512,128]{1,0:T(8,128)S(1)} %pad_maximum_fusion.13), channel_id=1, source_target_pairs={{0,2},{1,3},{2,0},{3,1},{4,6},{5,7},{6,4},{7,5},{8,10},{9,11},{10,... | collective-permute-start | bytes 786440 | tf_op jit(solution)/shard_map/ppermute | solution.py:53
  79.2 15.6 %collective-permute-start.25 = (f32[512,128]{1,0:T(8,128)S(1)}, f32[512,128]{1,0:T(8,128)S(1)}, u32[]{:S(2)}, u32[]{:S(2)}) collective-permute-start(f32[512,128]{1,0:T(8,128)S(1)} %pad_maximum_fusion.8.refs_8_), channel_id=1, source_target_pairs={{0,2},{1,3},{2,0},{3,1},{4,6},{5,7},{6,4},{7,5},{8,10},{9,11},{10,... | collective-permute-start | bytes 786440 | tf_op jit(solution)/shard_map/ppermute | solution.py:53
  79.6 15.2 %collective-permute-start.26 = (f32[512,128]{1,0:T(8,128)S(1)}, f32[512,128]{1,0:T(8,128)S(1)}, u32[]{:S(2)}, u32[]{:S(2)}) collective-permute-start(f32[512,128]{1,0:T(8,128)S(1)} %pad_maximum_fusion.9.refs_10_), channel_id=1, source_target_pairs={{0,1},{1,0},{2,3},{3,2},{4,5},{5,4},{6,7},{7,6},{8,9},{9,8},{10,11... | collective-permute-start | bytes 786440 | tf_op jit(solution)/shard_map/ppermute | solution.py:53
  81.4 13.5 %collective-permute-start.24 = (f32[512,128]{1,0:T(8,128)S(1)}, f32[512,128]{1,0:T(8,128)S(1)}, u32[]{:S(2)}, u32[]{:S(2)}) collective-permute-start(f32[512,128]{1,0:T(8,128)S(1)} %collective-permute-done.18), channel_id=1, source_target_pairs={{0,4},{1,5},{2,6},{3,7},{4,8},{5,9},{6,10},{7,11},{8,12},{9,13},{1... | collective-permute-start | bytes 786440 | tf_op jit(solution)/shard_map/ppermute | solution.py:53
  85.6 9.3 %collective-permute-start.27 = (f32[512,128]{1,0:T(8,128)S(1)}, f32[512,128]{1,0:T(8,128)S(1)}, u32[]{:S(2)}, u32[]{:S(2)}) collective-permute-start(f32[512,128]{1,0:T(8,128)S(1)} %pad_maximum_fusion.10.refs_12_), channel_id=1, source_target_pairs={{0,2},{1,3},{2,0},{3,1},{4,6},{5,7},{6,4},{7,5},{8,10},{9,11},{10,... | collective-permute-start | bytes 786440 | tf_op jit(solution)/shard_map/ppermute | solution.py:53
  87.7 9.2 %collective-permute-start.28 = (f32[512,128]{1,0:T(8,128)S(1)}, f32[512,128]{1,0:T(8,128)S(1)}, u32[]{:S(2)}, u32[]{:S(2)}) collective-permute-start(f32[512,128]{1,0:T(8,128)S(1)} %pad_maximum_fusion.11.refs_14_), channel_id=1, source_target_pairs={{0,1},{1,0},{2,3},{3,2},{4,5},{5,4},{6,7},{7,6},{8,9},{9,8},{10,11... | collective-permute-start | bytes 786440 | tf_op jit(solution)/shard_map/ppermute | solution.py:53
  97.0 15.2 %collective-permute-start.29 = (f32[1024,128]{1,0:T(8,128)S(1)}, f32[1024,128]{1,0:T(8,128)S(1)}, u32[]{:S(2)}, u32[]{:S(2)}) collective-permute-start(f32[1024,128]{1,0:T(8,128)S(1)} %pad_maximum_fusion), channel_id=1, source_target_pairs={{0,1},{1,0},{2,3},{3,2},{4,5},{5,4},{6,7},{7,6},{8,9},{9,8},{10,11... | collective-permute-start | bytes 1572872 | tf_op jit(solution)/shard_map/ppermute | solution.py:53
  97.5 14.8 %collective-permute-start.30 = (f32[1024,128]{1,0:T(8,128)S(1)}, f32[1024,128]{1,0:T(8,128)S(1)}, u32[]{:S(2)}, u32[]{:S(2)}) collective-permute-start(f32[1024,128]{1,0:T(8,128)S(1)} %pad_maximum_fusion.1), channel_id=1, source_target_pairs={{0,2},{1,3},{2,0},{3,1},{4,6},{5,7},{6,4},{7,5},{8,10},{9,11},{10,... | collective-permute-start | bytes 1572872 | tf_op jit(solution)/shard_map/ppermute | solution.py:53
  99.0 15.5 %collective-permute-start.31 = (f32[1024,128]{1,0:T(8,128)S(1)}, f32[1024,128]{1,0:T(8,128)S(1)}, u32[]{:S(2)}, u32[]{:S(2)}) collective-permute-start(f32[1024,128]{1,0:T(8,128)S(1)} %constant_dynamic-update-slice_fusion), channel_id=1, source_target_pairs={{0,2},{1,3},{2,0},{3,1},{4,6},{5,7},{6,4},{7,5},{8,10},{9,11},{10,... | collective-permute-start | bytes 1572872 | tf_op jit(solution)/shard_map/ppermute | solution.py:53
  99.6 15.6 %collective-permute-start.32 = (f32[1024,128]{1,0:T(8,128)S(1)}, f32[1024,128]{1,0:T(8,128)S(1)}, u32[]{:S(2)}, u32[]{:S(2)}) collective-permute-start(f32[1024,128]{1,0:T(8,128)S(1)} %constant_dynamic-update-slice_fusion.5), channel_id=1, source_target_pairs={{0,1},{1,0},{2,3},{3,2},{4,5},{5,4},{6,7},{7,6},{8,9},{9,8},{10,11... | collective-permute-start | bytes 1572872 | tf_op jit(solution)/shard_map/ppermute | solution.py:53
  115.3 4.2 %collective-permute-start.33 = (f32[4096,128]{1,0:T(8,128)S(1)}, f32[4096,128]{1,0:T(8,128)S(1)}, u32[]{:S(2)}, u32[]{:S(2)}) collective-permute-start(f32[4096,128]{1,0:T(8,128)S(1)} %constant_dynamic-update-slice_fusion.20.refs_0_), channel_id=1, source_target_pairs={{0,16},{16,0},{1,17},{17,1},{2,18},{18,2},{3,19},{19,3},{4,20},{20... | collective-permute-start | bytes 6291464 | tf_op jit(solution)/shard_map/ppermute | solution.py:408
  115.4 25.6 %collective-permute-start.34 = (f32[2048,128]{1,0:T(8,128)S(1)}, f32[2048,128]{1,0:T(8,128)S(1)}, u32[]{:S(2)}, u32[]{:S(2)}) collective-permute-start(f32[2048,128]{1,0:T(8,128)S(1)} %constant_dynamic-update-slice_fusion.10.refs_0_), channel_id=1, source_target_pairs={{0,2},{1,3},{2,0},{3,1},{4,6},{5,7},{6,4},{7,5},{8,10},{9,11},{10,... | collective-permute-start | bytes 3145736 | tf_op jit(solution)/shard_map/ppermute | solution.py:53
  116.8 25.6 %collective-permute-start.36 = (f32[2048,128]{1,0:T(8,128)S(1)}, f32[2048,128]{1,0:T(8,128)S(1)}, u32[]{:S(2)}, u32[]{:S(2)}) collective-permute-start(f32[2048,128]{1,0:T(8,128)S(1)} %constant_dynamic-update-slice_fusion.10.refs_0_), channel_id=1, source_target_pairs={{0,16},{16,0},{1,17},{17,1},{2,18},{18,2},{3,19},{19,3},{4,20},{20... | collective-permute-start | bytes 3145736 | tf_op jit(solution)/shard_map/ppermute | solution.py:408
  117.0 25.4 %collective-permute-start.35 = (f32[2048,128]{1,0:T(8,128)S(1)}, f32[2048,128]{1,0:T(8,128)S(1)}, u32[]{:S(2)}, u32[]{:S(2)}) collective-permute-start(f32[2048,128]{1,0:T(8,128)S(1)} %constant_dynamic-update-slice_fusion.15.refs_0_), channel_id=1, source_target_pairs={{0,1},{1,0},{2,3},{3,2},{4,5},{5,4},{6,7},{7,6},{8,9},{9,8},{10,11... | collective-permute-start | bytes 3145736 | tf_op jit(solution)/shard_map/ppermute | solution.py:53
  118.1 24.3 %collective-permute-start.37 = (f32[2048,128]{1,0:T(8,128)S(1)}, f32[2048,128]{1,0:T(8,128)S(1)}, u32[]{:S(2)}, u32[]{:S(2)}) collective-permute-start(f32[2048,128]{1,0:T(8,128)S(1)} %constant_dynamic-update-slice_fusion.15.refs_0_), channel_id=1, source_target_pairs={{0,16},{16,0},{1,17},{17,1},{2,18},{18,2},{3,19},{19,3},{4,20},{20... | collective-permute-start | bytes 3145736 | tf_op jit(solution)/shard_map/ppermute | solution.py:408
  124.4 18.0 %collective-permute-start.38 = (f32[512,512]{1,0:T(8,128)S(1)}, f32[512,512]{1,0:T(8,128)S(1)}, u32[]{:S(2)}, u32[]{:S(2)}) collective-permute-start(f32[512,512]{1,0:T(8,128)S(1)} %get-tuple-element.106), channel_id=1, source_target_pairs={{0,16},{16,0},{1,17},{17,1},{2,18},{18,2},{3,19},{19,3},{4,20},{20... | collective-permute-start | bytes 3145736 | tf_op jit(solution)/shard_map/ppermute | solution.py:408
  142.4 2.7 %collective-permute-start.39 = (f32[2048,128]{1,0:T(8,128)S(1)}, f32[2048,128]{1,0:T(8,128)S(1)}, u32[]{:S(2)}, u32[]{:S(2)}) collective-permute-start(f32[2048,128]{1,0:T(8,128)S(1)} %collective-permute-done.34.refs_2_), channel_id=1, source_target_pairs={{0,16},{16,0},{1,17},{17,1},{2,18},{18,2},{3,19},{19,3},{4,20},{20... | collective-permute-start | bytes 3145736 | tf_op jit(solution)/shard_map/ppermute | solution.py:408
  142.5 7.3 %collective-permute-start.40 = (f32[2048,128]{1,0:T(8,128)S(1)}, f32[2048,128]{1,0:T(8,128)S(1)}, u32[]{:S(2)}, u32[]{:S(2)}) collective-permute-start(f32[2048,128]{1,0:T(8,128)S(1)} %collective-permute-done.35.refs_2_), channel_id=1, source_target_pairs={{0,16},{16,0},{1,17},{17,1},{2,18},{18,2},{3,19},{19,3},{4,20},{20... | collective-permute-start | bytes 3145736 | tf_op jit(solution)/shard_map/ppermute | solution.py:408
  156.2 16.9 %collective-permute-start.41 = (f32[512,512]{1,0:T(8,128)}, f32[512,512]{1,0:T(8,128)}, u32[]{:S(2)}, u32[]{:S(2)}) collective-permute-start(f32[512,512]{1,0:T(8,128)} %get-tuple-element.119), channel_id=1, source_target_pairs={{0,16},{16,0},{1,17},{17,1},{2,18},{18,2},{3,19},{19,3},{4,20},{20... | collective-permute-start | bytes 3145736 | tf_op jit(solution)/shard_map/ppermute | solution.py:408

commit v5 on v4

--- a/solution.py
+++ b/solution.py
@@ -430,7 +430,7 @@
             axis=0,
         )
     ]
-    stripe_layers[1], across, keep, diag0[0], late[0] = gate((stripe_layers[1], across, keep, diag0[0], late[0]), own0)
+    stripe_layers[1], across, keep = gate((stripe_layers[1], across, keep), own0)
 
     stripe_layers.append(step_z(stripe_layers[1]))
     arrays = [gather_along(across, sizes)]

time: 177 us -> 181 us (1.023)
  waiting for transfers between devices: 45 us -> 48.8 us
    ppermute x1, waiting for transfers between devices: 5.3 us -> 9.07 us  [shards(): received = lax.ppermute(shared, 'pcol', partners)]
  transfers between devices with their start and end apart: 42 -> 42, of which waited for: 16 -> 14; matrix products, arithmetic and copies ran while one was open for 3% -> 3% of each run, Pallas kernels for 44% -> 43%
where the time goes in v5:
time: 181 us; the launch traced here: 180 us
  Pallas kernels  88.6 us (49%)
  waiting for transfers between devices  48.8 us (27%)
  starting transfers between devices  36.5 us (20%)
  local copies, waits for them, and re-layouts  4.85 us (3%)
    ppermute x33, waiting for transfers between devices, shift(): return lax.ppermute(value, 'pcol', pairs)  36.1 us
    ppermute x33, starting transfers between devices, shift(): return lax.ppermute(value, 'pcol', pairs)  32.1 us
    pallas_call x4, Pallas kernels, prepare(): pl.pallas_call(kernel, grid=(cycles,), out_shape=(out, out), in_specs=[pl...  26.3 us
    pallas_call x1, Pallas kernels, trail_second(): pl.pallas_call(kernel, grid=(tiles // group,), out_shape=jax.ShapeDtypeSt...  16.8 us
    pallas_call x1, Pallas kernels, trail_first(): pl.pallas_call(kernel, grid=(tiles // group,), out_shape=pltpu.HBM((rows,...  14.8 us
    pallas_call x2, Pallas kernels, solve(): pl.pallas_call(kernel, out_shape=(f32, f32, b16, b16), grid=(1,), in_spec...  11.3 us
    pallas_call x1, Pallas kernels, permute_columns(): pl.pallas_call(kernel, out_shape=[jax.ShapeDtypeStruct((rows, size), F32)...  11 us
    ppermute x1, waiting for transfers between devices, shards(): received = lax.ppermute(shared, 'pcol', partners)  9.07 us
  transfers between devices with their start and end apart: 42, of which 14 were waited for; matrix products, arithmetic and copies ran while one was open for 3% of the time, Pallas kernels for 43%

profile of v5, /device:TPU:0, one launch (start us, length us, event | category | flops | bytes accessed | tf_op | source)
XLA Modules:
  0.0 180.1 jit_solution(5342604487167710323)
XLA Ops:
  0.6 0.5 collective-permute-start.21
  1.1 1.7 slice.120
  2.9 2.6 %collective-permute-start.1 = (f32[512,128]{1,0:T(8,128)S(1)}, f32[512,128]{1,0:T(8,128)S(1)}, u32[]{:S(2)}, u32[]{:S(2)}) collective-permute-start(f32[512,128]{1,0:T(8,128)S(1)} %bitcast.14), channel_id=1, source_target_pairs={{0,4},{1,5},{2,6},{3,7},{4,8},{5,9},{6,10},{7,11},{8,12},{9,13},{1... | collective-permute-start | bytes 786440 | tf_op jit(solution)/shard_map/ppermute | solution.py:53
  5.5 1.6 collective-permute-start.2
  7.1 1.5 collective-permute-start.3
  8.6 2.5 %fusion.11 = (f32[2,128,1,128]{3,2,1,0:T(1,128)S(1)}, f32[2,128,1,128]{3,2,1,0:T(1,128)S(1)}, f32[2,128,1,128]{3,2,1,0:T(1,128)S(1)}, f32[2,128,1,128]{3,2,1,0:T(1,128)S(1)}) fusion(f32[8,128,24,128]{3,2,1,0:T(8,128)} %param.3), kind=kLoop, calls=%fused_computation.74 | loop fusion | bytes 1048576 | tf_op jit(solution)/shard_map/slice | solution.py:428
  11.1 2.7 %collective-permute-start = (f32[512,128]{1,0:T(8,128)S(1)}, f32[512,128]{1,0:T(8,128)S(1)}, u32[]{:S(2)}, u32[]{:S(2)}) collective-permute-start(f32[512,128]{1,0:T(8,128)S(1)} %pad_maximum_fusion.2), channel_id=1, source_target_pairs={{0,8},{1,9},{2,10},{3,11},{4,12},{5,13},{6,14},{7,15},{8,0},{9,1},... | collective-permute-start | bytes 786440 | tf_op jit(solution)/shard_map/ppermute | solution.py:418
  13.8 0.1 add_convert_fusion.keep_ref
  13.9 6.5 %prepare_own_first.1 = (bf16[512,3072]{1,0:T(8,128)(2,1)}, bf16[512,3072]{1,0:T(8,128)(2,1)}) custom-call(s32[2]{0:T(128)S(1)} %add_convert_fusion.keep_ref, f32[8,3072,128]{2,1,0:T(8,128)} %bitcast.12), custom_call_target="tpu_custom_call" | custom-call | bytes 18874368 | tf_op jit(solution)/shard_map/prepare_own_first/pallas_call | solution.py:170
  20.5 0.3 collective-permute-start.4
  20.7 0.6 collective-permute-start.5
  21.3 0.9 collective-permute-start.6
  22.3 9.1 %collective-permute-done = f32[512,128]{1,0:T(8,128)S(1)} collective-permute-done((f32[512,128]{1,0:T(8,128)S(1)}, f32[512,128]{1,0:T(8,128)S(1)}, u32[]{:S(2)}, u32[]{:S(2)}) %collective-permute-start) | collective-permute-done | bytes 262176 | tf_op jit(solution)/shard_map/ppermute | solution.py:418
  31.5 6.6 %prepare_own_second.1 = (bf16[512,3072]{1,0:T(8,128)(2,1)}, bf16[512,3072]{1,0:T(8,128)(2,1)}) custom-call(s32[2]{0:T(128)S(1)} %add_convert_fusion.keep_ref, f32[8,3072,128]{2,1,0:T(8,128)} %bitcast.13), custom_call_target="tpu_custom_call" | custom-call | bytes 18874368 | tf_op jit(solution)/shard_map/prepare_own_second/pallas_call | solution.py:170
  38.1 1.5 collective-permute-start.13
  39.7 1.6 collective-permute-start.9
  41.2 0.1 dynamic_slice.3
  41.3 0.6 collective-permute-start.14
  41.9 0.1 collective-permute-start.8
  42.0 4.0 %collective-permute-done.13.refs_1_ = f32[512,128]{1,0:T(8,128)S(1)} collective-permute-done((f32[512,128]{1,0:T(8,128)S(1)}, f32[512,128]{1,0:T(8,128)S(1)}, u32[]{:S(2)}, u32[]{:S(2)}) %collective-permute-start.13) | collective-permute-done | bytes 262176 | tf_op jit(solution)/shard_map/ppermute | solution.py:53
  46.1 1.7 collective-permute-start.10
  47.8 3.2 %collective-permute-done.10 = f32[256,128]{1,0:T(8,128)S(1)} collective-permute-done((f32[256,128]{1,0:T(8,128)S(1)}, f32[256,128]{1,0:T(8,128)S(1)}, u32[]{:S(2)}, u32[]{:S(2)}) %collective-permute-start.10) | collective-permute-done | bytes 131104 | tf_op jit(solution)/shard_map/ppermute | solution.py:53
  51.1 1.8 %collective-permute-start.19 = (f32[512,128]{1,0:T(8,128)S(1)}, f32[512,128]{1,0:T(8,128)S(1)}, u32[]{:S(2)}, u32[]{:S(2)}) collective-permute-start(f32[512,128]{1,0:T(8,128)S(1)} %pad_maximum_fusion.5.refs_4_), channel_id=1, source_target_pairs={{0,2},{1,3},{2,0},{3,1},{4,6},{5,7},{6,4},{7,5},{8,10},{9,11},{10,... | collective-permute-start | bytes 786440 | tf_op jit(solution)/shard_map/ppermute | solution.py:53
  52.9 6.6 %collective-permute-done.11 = f32[256,128]{1,0:T(8,128)S(1)} collective-permute-done((f32[256,128]{1,0:T(8,128)S(1)}, f32[256,128]{1,0:T(8,128)S(1)}, u32[]{:S(2)}, u32[]{:S(2)}) %collective-permute-start.11) | collective-permute-done | bytes 131104 | tf_op jit(solution)/shard_map/ppermute | solution.py:53
  59.5 1.5 collective-permute-start.20
  61.1 0.6 collective-permute-start.15
  61.7 0.4 collective-permute-start.16
  62.1 6.5 %collective-permute-done.15 = f32[256,128]{1,0:T(8,128)S(1)} collective-permute-done((f32[256,128]{1,0:T(8,128)S(1)}, f32[256,128]{1,0:T(8,128)S(1)}, u32[]{:S(2)}, u32[]{:S(2)}) %collective-permute-start.15) | collective-permute-done | bytes 131104 | tf_op jit(solution)/shard_map/ppermute | solution.py:53
  68.6 0.4 collective-permute-start.17
  69.1 6.5 %prepare_other_first.1 = (bf16[512,3072]{1,0:T(8,128)(2,1)}, bf16[512,3072]{1,0:T(8,128)(2,1)}) custom-call(s32[2]{0:T(128)S(1)} %add_convert_fusion.keep_ref, f32[8,3072,128]{2,1,0:T(8,128)} %bitcast.9.in_ref), custom_call_target="tpu_custom_call" | custom-call | bytes 18874368 | tf_op jit(solution)/shard_map/prepare_other_first/pallas_call | solution.py:170
  75.6 2.8 %collective-permute-done.17 = f32[256,128]{1,0:T(8,128)S(1)} collective-permute-done((f32[256,128]{1,0:T(8,128)S(1)}, f32[256,128]{1,0:T(8,128)S(1)}, u32[]{:S(2)}, u32[]{:S(2)}) %collective-permute-start.17) | collective-permute-done | bytes 131104 | tf_op jit(solution)/shard_map/ppermute | solution.py:53
  78.5 1.6 collective-permute-start.22
  80.1 1.4 collective-permute-start.23
  81.5 0.8 collective-permute-start.25
  82.3 0.6 collective-permute-start.26
  82.9 4.4 %collective-permute-done.22 = f32[512,128]{1,0:T(8,128)S(1)} collective-permute-done((f32[512,128]{1,0:T(8,128)S(1)}, f32[512,128]{1,0:T(8,128)S(1)}, u32[]{:S(2)}, u32[]{:S(2)}) %collective-permute-start.22) | collective-permute-done | bytes 262176 | tf_op jit(solution)/shard_map/ppermute | solution.py:53
  87.3 2.0 %collective-permute-start.27 = (f32[512,128]{1,0:T(8,128)S(1)}, f32[512,128]{1,0:T(8,128)S(1)}, u32[]{:S(2)}, u32[]{:S(2)}) collective-permute-start(f32[512,128]{1,0:T(8,128)S(1)} %pad_maximum_fusion.10.refs_12_), channel_id=1, source_target_pairs={{0,2},{1,3},{2,0},{3,1},{4,6},{5,7},{6,4},{7,5},{8,10},{9,11},{10,... | collective-permute-start | bytes 786440 | tf_op jit(solution)/shard_map/ppermute | solution.py:53
  89.4 1.3 collective-permute-start.28
  90.7 6.7 %prepare_other_second.1 = (bf16[512,3072]{1,0:T(8,128)(2,1)}, bf16[512,3072]{1,0:T(8,128)(2,1)}) custom-call(s32[2]{0:T(128)S(1)} %add_convert_fusion.keep_ref, f32[8,3072,128]{2,1,0:T(8,128)} %bitcast.9.in_ref), custom_call_target="tpu_custom_call" | custom-call | bytes 18874368 | tf_op jit(solution)/shard_map/prepare_other_second/pallas_call | solution.py:170
  97.5 0.9 collective-permute-done.28.refs_15_
  98.4 1.3 collective-permute-start.29
  99.7 0.1 collective-permute-start.30
  99.9 2.0 %collective-permute-start.31 = (f32[1024,128]{1,0:T(8,128)S(1)}, f32[1024,128]{1,0:T(8,128)S(1)}, u32[]{:S(2)}, u32[]{:S(2)}) collective-permute-start(f32[1024,128]{1,0:T(8,128)S(1)} %constant_dynamic-update-slice_fusion), channel_id=1, source_target_pairs={{0,2},{1,3},{2,0},{3,1},{4,6},{5,7},{6,4},{7,5},{8,10},{9,11},{10,... | collective-permute-start | bytes 1572872 | tf_op jit(solution)/shard_map/ppermute | solution.py:53
  101.8 0.8 collective-permute-start.32
  102.6 11.0 %permute_columns.1 = (f32[512,1024]{1,0:T(8,128)S(1)}, f32[512,1024]{1,0:T(8,128)S(1)}, f32[512,128]{1,0:T(8,128)S(1)}) custom-call(s32[16]{0:T(128)S(1)} %fusion.2.tiles_ref, s32[1,2176]{1,0:T(1,128)S(1)} %reshape.25.wanted_ref, f32[512,128]{1,0:T(8,128)S(1)} %pad_maximum_fusion.3.refs_0_, f32[512,128]{1,0:T(8,128)S(1)} %collective-permute-done.13.refs_1_, ...), custom_call_target="tpu_custom_call" | custom-call | flops 9126805504 | bytes 8388608 | tf_op jit(solution)/shard_map/permute_columns/pallas_call | solution.py:138
  113.7 4.2 %collective-permute-done.31 = f32[1024,128]{1,0:T(8,128)S(1)} collective-permute-done((f32[1024,128]{1,0:T(8,128)S(1)}, f32[1024,128]{1,0:T(8,128)S(1)}, u32[]{:S(2)}, u32[]{:S(2)}) %collective-permute-start.31) | collective-permute-done | bytes 524320 | tf_op jit(solution)/shard_map/ppermute | solution.py:53
  118.0 0.3 collective-permute-done.32
  118.4 0.1 collective-permute-start.33
  118.5 1.5 collective-permute-start.34
  120.0 0.2 collective-permute-start.36
  120.2 0.9 collective-permute-start.35
  121.2 1.5 collective-permute-done.33.refs_1_
  122.6 4.9 %solve_first.1 = (f32[512,512]{1,0:T(8,128)S(1)}, f32[512,512]{1,0:T(8,128)S(1)}, bf16[512,1024]{1,0:T(8,128)(2,1)S(1)}, bf16[512,1024]{1,0:T(8,128)(2,1)S(1)}) custom-call(s32[16]{0:T(128)S(1)} %fusion.2.tiles_ref, f32[512,1024]{1,0:T(8,128)S(1)} %get-tuple-element.90.rhs_ref, f32[4096,128]{1,0:T(8,128)S(1)} %constant_dynamic-update-slice_fusion.20.refs_0_, ...), custom_call_target="tpu_custom_call" | custom-call | flops 3221225472 | bytes 8388608 | tf_op jit(solution)/shard_map/solve_first/pallas_call | solution.py:245
  127.5 0.2 collective-permute-start.38
  127.7 14.8 %trail_first.1.in_ref = f32[512,3072]{1,0:T(8,128)} custom-call(f32[512,24,128]{2,1,0:T(8,128)} %sens_ref.1, f32[512,128]{1,0:T(8,128)S(1)} %get-tuple-element.103.own_ref, bf16[512,1024]{1,0:T(8,128)(2,1)S(1)} %get-tuple-element.104.refs_0_.yh_ref, bf16[512,1024]{1,0:T(8,128)(2,1)S(1)} %get-tuple-element.105.refs_1_.yl_ref, ...), custom_call_target="tpu_custom_call" | custom-call | flops 9663676416 | bytes 25165824 | tf_op jit(solution)/shard_map/trail_first/pallas_call | solution.py:324
  142.6 1.5 collective-permute-done.34.refs_2_
  144.1 1.5 collective-permute-done.35.refs_2_
  145.7 0.5 collective-permute-start.40
  146.2 2.1 %collective-permute-done.39.refs_3_ = f32[2048,128]{1,0:T(8,128)S(1)} collective-permute-done((f32[2048,128]{1,0:T(8,128)S(1)}, f32[2048,128]{1,0:T(8,128)S(1)}, u32[]{:S(2)}, u32[]{:S(2)}) %collective-permute-start.39) | collective-permute-done | bytes 1048608 | tf_op jit(solution)/shard_map/ppermute | solution.py:408
  148.3 4.6 %couple.1.rhs_ref = f32[512,1024]{1,0:T(8,128)S(1)} custom-call(s32[16]{0:T(128)S(1)} %fusion.2.tiles_ref, f32[512,1024]{1,0:T(8,128)S(1)} %get-tuple-element.106.rhs_ref, bf16[512,1024]{1,0:T(8,128)(2,1)S(1)} %get-tuple-element.104.refs_0_.yh_ref, bf16[512,1024]{1,0:T(8,128)(2,1)S(1)} %get-tuple-element.105.refs_1_.yl_ref, ...), custom_call_target="tpu_custom_call" | custom-call | flops 3221225472 | bytes 8388608 | tf_op jit(solution)/shard_map/couple/pallas_call | solution.py:273
  153.0 6.4 %solve_second.1 = (f32[512,512]{1,0:T(8,128)S(1)}, f32[512,512]{1,0:T(8,128)}, bf16[512,1024]{1,0:T(8,128)(2,1)}, bf16[512,1024]{1,0:T(8,128)(2,1)}) custom-call(s32[16]{0:T(128)S(1)} %fusion.2.tiles_ref, f32[512,1024]{1,0:T(8,128)S(1)} %couple.1.rhs_ref, f32[2048,128]{1,0:T(8,128)S(1)} %constant_dynamic-update-slice_fusion.15.refs_0_, ...), custom_call_target="tpu_custom_call" | custom-call | flops 3221225472 | bytes 8388608 | tf_op jit(solution)/shard_map/solve_second/pallas_call | solution.py:245
  159.4 0.1 collective-permute-start.41
  159.5 16.8 %trail_second.1 = f32[512,24,128]{2,1,0:T(8,128)} custom-call(f32[512,3072]{1,0:T(8,128)} %trail_first.1.in_ref, bf16[512,1024]{1,0:T(8,128)(2,1)} %get-tuple-element.116.refs_0_, bf16[512,1024]{1,0:T(8,128)(2,1)} %get-tuple-element.117.refs_1_, bf16[512,3072]{1,0:T(8,128)(2,1)} %get-tuple-element.64.refs_2_, bf16[512,3072]{1,0:T(8,128)(2,1)} %get-tuple-element.65.refs_3_, ...), custom_call_target="tpu_custom_call" | custom-call | flops 9663676416 | bytes 25165824 | tf_op jit(solution)/shard_map/trail_second/pallas_call | solution.py:354
  176.3 3.8 %place_unknowns.1 = f32[1024,8,128]{2,1,0:T(8,128)} custom-call(s32[1]{0:T(128)} %bitcast.core_ref, f32[512,512]{1,0:T(8,128)S(1)} %get-tuple-element.98.refs_0_, f32[512,512]{1,0:T(8,128)S(1)} %get-tuple-element.113.refs_1_, f32[512,512]{1,0:T(8,128)S(1)} %collective-permute-done.38.refs_2_, f32[512,512]{1,0:T(8,128)} %collective-permute-done.41.refs_3_), custom_call_target="tpu_custom_call" | custom-call | tf_op jit(solution)/shard_map/place_unknowns/pallas_call | solution.py:383
  (75 shorter events, 1.3 us)
Async XLA Ops:
  0.6 68.4 %collective-permute-start.21 = (f32[8,128,24,128]{3,2,1,0:T(8,128)}, f32[8,128,24,128]{3,2,1,0:T(8,128)}, u32[]{:S(2)}, u32[]{:S(2)}) collective-permute-start(f32[8,128,24,128]{3,2,1,0:T(8,128)} %param.3), channel_id=1, source_target_pairs={{0,16},{16,0},{1,17},{17,1},{2,18},{18,2},{3,19},{19,3},{4,20},{20... | collective-permute-start | bytes 37748744 | tf_op jit(solution)/shard_map/ppermute | solution.py:408
  2.9 17.6 %collective-permute-start.1 = (f32[512,128]{1,0:T(8,128)S(1)}, f32[512,128]{1,0:T(8,128)S(1)}, u32[]{:S(2)}, u32[]{:S(2)}) collective-permute-start(f32[512,128]{1,0:T(8,128)S(1)} %bitcast.14), channel_id=1, source_target_pairs={{0,4},{1,5},{2,6},{3,7},{4,8},{5,9},{6,10},{7,11},{8,12},{9,13},{1... | collective-permute-start | bytes 786440 | tf_op jit(solution)/shard_map/ppermute | solution.py:53
  5.5 14.8 %collective-permute-start.2 = (f32[256,128]{1,0:T(8,128)S(1)}, f32[256,128]{1,0:T(8,128)S(1)}, u32[]{:S(2)}, u32[]{:S(2)}) collective-permute-start(f32[256,128]{1,0:T(8,128)S(1)} %get-tuple-element.148), channel_id=1, source_target_pairs={{0,1},{1,0},{2,3},{3,2},{4,5},{5,4},{6,7},{7,6},{8,9},{9,8},{10,11... | collective-permute-start | bytes 393224 | tf_op jit(solution)/shard_map/ppermute | solution.py:53
  7.1 13.3 %collective-permute-start.3 = (f32[256,128]{1,0:T(8,128)S(1)}, f32[256,128]{1,0:T(8,128)S(1)}, u32[]{:S(2)}, u32[]{:S(2)}) collective-permute-start(f32[256,128]{1,0:T(8,128)S(1)} %get-tuple-element.147), channel_id=1, source_target_pairs={{0,2},{1,3},{2,0},{3,1},{4,6},{5,7},{6,4},{7,5},{8,10},{9,11},{10,... | collective-permute-start | bytes 393224 | tf_op jit(solution)/shard_map/ppermute | solution.py:53
  11.1 20.2 %collective-permute-start = (f32[512,128]{1,0:T(8,128)S(1)}, f32[512,128]{1,0:T(8,128)S(1)}, u32[]{:S(2)}, u32[]{:S(2)}) collective-permute-start(f32[512,128]{1,0:T(8,128)S(1)} %pad_maximum_fusion.2), channel_id=1, source_target_pairs={{0,8},{1,9},{2,10},{3,11},{4,12},{5,13},{6,14},{7,15},{8,0},{9,1},... | collective-permute-start | bytes 786440 | tf_op jit(solution)/shard_map/ppermute | solution.py:418
  20.5 19.2 %collective-permute-start.4 = (f32[512,128]{1,0:T(8,128)S(1)}, f32[512,128]{1,0:T(8,128)S(1)}, u32[]{:S(2)}, u32[]{:S(2)}) collective-permute-start(f32[512,128]{1,0:T(8,128)S(1)} %collective-permute-done.1), channel_id=1, source_target_pairs={{0,4},{1,5},{2,6},{3,7},{4,8},{5,9},{6,10},{7,11},{8,12},{9,13},{1... | collective-permute-start | bytes 786440 | tf_op jit(solution)/shard_map/ppermute | solution.py:53
  20.7 17.3 %collective-permute-start.5 = (f32[256,128]{1,0:T(8,128)S(1)}, f32[256,128]{1,0:T(8,128)S(1)}, u32[]{:S(2)}, u32[]{:S(2)}) collective-permute-start(f32[256,128]{1,0:T(8,128)S(1)} %get-tuple-element.146), channel_id=1, source_target_pairs={{0,1},{1,0},{2,3},{3,2},{4,5},{5,4},{6,7},{7,6},{8,9},{9,8},{10,11... | collective-permute-start | bytes 393224 | tf_op jit(solution)/shard_map/ppermute | solution.py:53
  21.3 18.3 %collective-permute-start.6 = (f32[256,128]{1,0:T(8,128)S(1)}, f32[256,128]{1,0:T(8,128)S(1)}, u32[]{:S(2)}, u32[]{:S(2)}) collective-permute-start(f32[256,128]{1,0:T(8,128)S(1)} %get-tuple-element.145), channel_id=1, source_target_pairs={{0,2},{1,3},{2,0},{3,1},{4,6},{5,7},{6,4},{7,5},{8,10},{9,11},{10,... | collective-permute-start | bytes 393224 | tf_op jit(solution)/shard_map/ppermute | solution.py:53
  31.4 8.2 %collective-permute-start.7 = (f32[256,128]{1,0:T(8,128)S(1)}, f32[256,128]{1,0:T(8,128)S(1)}, u32[]{:S(2)}, u32[]{:S(2)}) collective-permute-start(f32[256,128]{1,0:T(8,128)S(1)} %get-tuple-element.123), channel_id=1, source_target_pairs={{0,4},{1,5},{2,6},{3,7},{4,8},{5,9},{6,10},{7,11},{8,12},{9,13},{1... | collective-permute-start | bytes 393224 | tf_op jit(solution)/shard_map/ppermute | solution.py:53
  31.5 9.8 %copy-start = (s32[2048]{0:T(1024)S(1)}, s32[2048]{0:T(1024)}, u32[]{:S(2)}) copy-start(s32[2048]{0:T(1024)} %param.5) | copy-start | bytes 24580
  38.1 8.0 %collective-permute-start.13 = (f32[512,128]{1,0:T(8,128)S(1)}, f32[512,128]{1,0:T(8,128)S(1)}, u32[]{:S(2)}, u32[]{:S(2)}) collective-permute-start(f32[512,128]{1,0:T(8,128)S(1)} %pad_maximum_fusion.3.refs_0_), channel_id=1, source_target_pairs={{0,2},{1,3},{2,0},{3,1},{4,6},{5,7},{6,4},{7,5},{8,10},{9,11},{10,... | collective-permute-start | bytes 786440 | tf_op jit(solution)/shard_map/ppermute | solution.py:53
  39.7 8.1 %collective-permute-start.9 = (f32[256,128]{1,0:T(8,128)S(1)}, f32[256,128]{1,0:T(8,128)S(1)}, u32[]{:S(2)}, u32[]{:S(2)}) collective-permute-start(f32[256,128]{1,0:T(8,128)S(1)} %get-tuple-element.143), channel_id=1, source_target_pairs={{0,1},{1,0},{2,3},{3,2},{4,5},{5,4},{6,7},{7,6},{8,9},{9,8},{10,11... | collective-permute-start | bytes 393224 | tf_op jit(solution)/shard_map/ppermute | solution.py:53
  41.3 9.8 %collective-permute-start.14 = (f32[512,128]{1,0:T(8,128)S(1)}, f32[512,128]{1,0:T(8,128)S(1)}, u32[]{:S(2)}, u32[]{:S(2)}) collective-permute-start(f32[512,128]{1,0:T(8,128)S(1)} %pad_maximum_fusion.4.refs_2_), channel_id=1, source_target_pairs={{0,1},{1,0},{2,3},{3,2},{4,5},{5,4},{6,7},{7,6},{8,9},{9,8},{10,11... | collective-permute-start | bytes 786440 | tf_op jit(solution)/shard_map/ppermute | solution.py:53
  41.9 19.1 %collective-permute-start.8 = (f32[512,128]{1,0:T(8,128)S(1)}, f32[512,128]{1,0:T(8,128)S(1)}, u32[]{:S(2)}, u32[]{:S(2)}) collective-permute-start(f32[512,128]{1,0:T(8,128)S(1)} %collective-permute-done.4), channel_id=1, source_target_pairs={{0,4},{1,5},{2,6},{3,7},{4,8},{5,9},{6,10},{7,11},{8,12},{9,13},{1... | collective-permute-start | bytes 786440 | tf_op jit(solution)/shard_map/ppermute | solution.py:53
  46.1 5.0 %collective-permute-start.10 = (f32[256,128]{1,0:T(8,128)S(1)}, f32[256,128]{1,0:T(8,128)S(1)}, u32[]{:S(2)}, u32[]{:S(2)}) collective-permute-start(f32[256,128]{1,0:T(8,128)S(1)} %get-tuple-element.142), channel_id=1, source_target_pairs={{0,2},{1,3},{2,0},{3,1},{4,6},{5,7},{6,4},{7,5},{8,10},{9,11},{10,... | collective-permute-start | bytes 393224 | tf_op jit(solution)/shard_map/ppermute | solution.py:53
  47.8 13.2 %collective-permute-start.12 = (f32[512,128]{1,0:T(8,128)S(1)}, f32[512,128]{1,0:T(8,128)S(1)}, u32[]{:S(2)}, u32[]{:S(2)}) collective-permute-start(f32[512,128]{1,0:T(8,128)S(1)} %pad_maximum_fusion.7), channel_id=1, source_target_pairs={{0,4},{1,5},{2,6},{3,7},{4,8},{5,9},{6,10},{7,11},{8,12},{9,13},{1... | collective-permute-start | bytes 786440 | tf_op jit(solution)/shard_map/ppermute | solution.py:53
  51.0 8.5 %collective-permute-start.11 = (f32[256,128]{1,0:T(8,128)S(1)}, f32[256,128]{1,0:T(8,128)S(1)}, u32[]{:S(2)}, u32[]{:S(2)}) collective-permute-start(f32[256,128]{1,0:T(8,128)S(1)} %collective-permute-done.7), channel_id=1, source_target_pairs={{0,4},{1,5},{2,6},{3,7},{4,8},{5,9},{6,10},{7,11},{8,12},{9,13},{1... | collective-permute-start | bytes 393224 | tf_op jit(solution)/shard_map/ppermute | solution.py:53
  51.1 24.5 %collective-permute-start.19 = (f32[512,128]{1,0:T(8,128)S(1)}, f32[512,128]{1,0:T(8,128)S(1)}, u32[]{:S(2)}, u32[]{:S(2)}) collective-permute-start(f32[512,128]{1,0:T(8,128)S(1)} %pad_maximum_fusion.5.refs_4_), channel_id=1, source_target_pairs={{0,2},{1,3},{2,0},{3,1},{4,6},{5,7},{6,4},{7,5},{8,10},{9,11},{10,... | collective-permute-start | bytes 786440 | tf_op jit(solution)/shard_map/ppermute | solution.py:53
  59.5 16.1 %collective-permute-start.20 = (f32[512,128]{1,0:T(8,128)S(1)}, f32[512,128]{1,0:T(8,128)S(1)}, u32[]{:S(2)}, u32[]{:S(2)}) collective-permute-start(f32[512,128]{1,0:T(8,128)S(1)} %pad_maximum_fusion.6.refs_6_), channel_id=1, source_target_pairs={{0,1},{1,0},{2,3},{3,2},{4,5},{5,4},{6,7},{7,6},{8,9},{9,8},{10,11... | collective-permute-start | bytes 786440 | tf_op jit(solution)/shard_map/ppermute | solution.py:53
  61.1 7.5 %collective-permute-start.15 = (f32[256,128]{1,0:T(8,128)S(1)}, f32[256,128]{1,0:T(8,128)S(1)}, u32[]{:S(2)}, u32[]{:S(2)}) collective-permute-start(f32[256,128]{1,0:T(8,128)S(1)} %get-tuple-element.141), channel_id=1, source_target_pairs={{0,1},{1,0},{2,3},{3,2},{4,5},{5,4},{6,7},{7,6},{8,9},{9,8},{10,11... | collective-permute-start | bytes 393224 | tf_op jit(solution)/shard_map/ppermute | solution.py:53
  61.7 6.9 %collective-permute-start.16 = (f32[256,128]{1,0:T(8,128)S(1)}, f32[256,128]{1,0:T(8,128)S(1)}, u32[]{:S(2)}, u32[]{:S(2)}) collective-permute-start(f32[256,128]{1,0:T(8,128)S(1)} %get-tuple-element.140), channel_id=1, source_target_pairs={{0,2},{1,3},{2,0},{3,1},{4,6},{5,7},{6,4},{7,5},{8,10},{9,11},{10,... | collective-permute-start | bytes 393224 | tf_op jit(solution)/shard_map/ppermute | solution.py:53
  68.6 9.9 %collective-permute-start.18 = (f32[512,128]{1,0:T(8,128)S(1)}, f32[512,128]{1,0:T(8,128)S(1)}, u32[]{:S(2)}, u32[]{:S(2)}) collective-permute-start(f32[512,128]{1,0:T(8,128)S(1)} %collective-permute-done.12), channel_id=1, source_target_pairs={{0,4},{1,5},{2,6},{3,7},{4,8},{5,9},{6,10},{7,11},{8,12},{9,13},{1... | collective-permute-start | bytes 786440 | tf_op jit(solution)/shard_map/ppermute | solution.py:53
  68.6 9.9 %collective-permute-start.17 = (f32[256,128]{1,0:T(8,128)S(1)}, f32[256,128]{1,0:T(8,128)S(1)}, u32[]{:S(2)}, u32[]{:S(2)}) collective-permute-start(f32[256,128]{1,0:T(8,128)S(1)} %collective-permute-done.11), channel_id=1, source_target_pairs={{0,4},{1,5},{2,6},{3,7},{4,8},{5,9},{6,10},{7,11},{8,12},{9,13},{1... | collective-permute-start | bytes 393224 | tf_op jit(solution)/shard_map/ppermute | solution.py:53
  78.5 8.8 %collective-permute-start.22 = (f32[512,128]{1,0:T(8,128)S(1)}, f32[512,128]{1,0:T(8,128)S(1)}, u32[]{:S(2)}, u32[]{:S(2)}) collective-permute-start(f32[512,128]{1,0:T(8,128)S(1)} %pad_maximum_fusion.12), channel_id=1, source_target_pairs={{0,1},{1,0},{2,3},{3,2},{4,5},{5,4},{6,7},{7,6},{8,9},{9,8},{10,11... | collective-permute-start | bytes 786440 | tf_op jit(solution)/shard_map/ppermute | solution.py:53
  80.1 9.3 %collective-permute-start.23 = (f32[512,128]{1,0:T(8,128)S(1)}, f32[512,128]{1,0:T(8,128)S(1)}, u32[]{:S(2)}, u32[]{:S(2)}) collective-permute-start(f32[512,128]{1,0:T(8,128)S(1)} %pad_maximum_fusion.13), channel_id=1, source_target_pairs={{0,2},{1,3},{2,0},{3,1},{4,6},{5,7},{6,4},{7,5},{8,10},{9,11},{10,... | collective-permute-start | bytes 786440 | tf_op jit(solution)/shard_map/ppermute | solution.py:53
  81.5 15.9 %collective-permute-start.25 = (f32[512,128]{1,0:T(8,128)S(1)}, f32[512,128]{1,0:T(8,128)S(1)}, u32[]{:S(2)}, u32[]{:S(2)}) collective-permute-start(f32[512,128]{1,0:T(8,128)S(1)} %pad_maximum_fusion.8.refs_8_), channel_id=1, source_target_pairs={{0,2},{1,3},{2,0},{3,1},{4,6},{5,7},{6,4},{7,5},{8,10},{9,11},{10,... | collective-permute-start | bytes 786440 | tf_op jit(solution)/shard_map/ppermute | solution.py:53
  82.3 15.1 %collective-permute-start.26 = (f32[512,128]{1,0:T(8,128)S(1)}, f32[512,128]{1,0:T(8,128)S(1)}, u32[]{:S(2)}, u32[]{:S(2)}) collective-permute-start(f32[512,128]{1,0:T(8,128)S(1)} %pad_maximum_fusion.9.refs_10_), channel_id=1, source_target_pairs={{0,1},{1,0},{2,3},{3,2},{4,5},{5,4},{6,7},{7,6},{8,9},{9,8},{10,11... | collective-permute-start | bytes 786440 | tf_op jit(solution)/shard_map/ppermute | solution.py:53
  82.9 14.6 %collective-permute-start.24 = (f32[512,128]{1,0:T(8,128)S(1)}, f32[512,128]{1,0:T(8,128)S(1)}, u32[]{:S(2)}, u32[]{:S(2)}) collective-permute-start(f32[512,128]{1,0:T(8,128)S(1)} %collective-permute-done.18), channel_id=1, source_target_pairs={{0,4},{1,5},{2,6},{3,7},{4,8},{5,9},{6,10},{7,11},{8,12},{9,13},{1... | collective-permute-start | bytes 786440 | tf_op jit(solution)/shard_map/ppermute | solution.py:53
  87.3 10.1 %collective-permute-start.27 = (f32[512,128]{1,0:T(8,128)S(1)}, f32[512,128]{1,0:T(8,128)S(1)}, u32[]{:S(2)}, u32[]{:S(2)}) collective-permute-start(f32[512,128]{1,0:T(8,128)S(1)} %pad_maximum_fusion.10.refs_12_), channel_id=1, source_target_pairs={{0,2},{1,3},{2,0},{3,1},{4,6},{5,7},{6,4},{7,5},{8,10},{9,11},{10,... | collective-permute-start | bytes 786440 | tf_op jit(solution)/shard_map/ppermute | solution.py:53
  89.4 8.9 %collective-permute-start.28 = (f32[512,128]{1,0:T(8,128)S(1)}, f32[512,128]{1,0:T(8,128)S(1)}, u32[]{:S(2)}, u32[]{:S(2)}) collective-permute-start(f32[512,128]{1,0:T(8,128)S(1)} %pad_maximum_fusion.11.refs_14_), channel_id=1, source_target_pairs={{0,1},{1,0},{2,3},{3,2},{4,5},{5,4},{6,7},{7,6},{8,9},{9,8},{10,11... | collective-permute-start | bytes 786440 | tf_op jit(solution)/shard_map/ppermute | solution.py:53
  98.4 15.2 %collective-permute-start.29 = (f32[1024,128]{1,0:T(8,128)S(1)}, f32[1024,128]{1,0:T(8,128)S(1)}, u32[]{:S(2)}, u32[]{:S(2)}) collective-permute-start(f32[1024,128]{1,0:T(8,128)S(1)} %pad_maximum_fusion), channel_id=1, source_target_pairs={{0,1},{1,0},{2,3},{3,2},{4,5},{5,4},{6,7},{7,6},{8,9},{9,8},{10,11... | collective-permute-start | bytes 1572872 | tf_op jit(solution)/shard_map/ppermute | solution.py:53
  99.7 14.0 %collective-permute-start.30 = (f32[1024,128]{1,0:T(8,128)S(1)}, f32[1024,128]{1,0:T(8,128)S(1)}, u32[]{:S(2)}, u32[]{:S(2)}) collective-permute-start(f32[1024,128]{1,0:T(8,128)S(1)} %pad_maximum_fusion.1), channel_id=1, source_target_pairs={{0,2},{1,3},{2,0},{3,1},{4,6},{5,7},{6,4},{7,5},{8,10},{9,11},{10,... | collective-permute-start | bytes 1572872 | tf_op jit(solution)/shard_map/ppermute | solution.py:53
  99.9 18.1 %collective-permute-start.31 = (f32[1024,128]{1,0:T(8,128)S(1)}, f32[1024,128]{1,0:T(8,128)S(1)}, u32[]{:S(2)}, u32[]{:S(2)}) collective-permute-start(f32[1024,128]{1,0:T(8,128)S(1)} %constant_dynamic-update-slice_fusion), channel_id=1, source_target_pairs={{0,2},{1,3},{2,0},{3,1},{4,6},{5,7},{6,4},{7,5},{8,10},{9,11},{10,... | collective-permute-start | bytes 1572872 | tf_op jit(solution)/shard_map/ppermute | solution.py:53
  101.8 16.4 %collective-permute-start.32 = (f32[1024,128]{1,0:T(8,128)S(1)}, f32[1024,128]{1,0:T(8,128)S(1)}, u32[]{:S(2)}, u32[]{:S(2)}) collective-permute-start(f32[1024,128]{1,0:T(8,128)S(1)} %constant_dynamic-update-slice_fusion.5), channel_id=1, source_target_pairs={{0,1},{1,0},{2,3},{3,2},{4,5},{5,4},{6,7},{7,6},{8,9},{9,8},{10,11... | collective-permute-start | bytes 1572872 | tf_op jit(solution)/shard_map/ppermute | solution.py:53
  118.4 4.2 %collective-permute-start.33 = (f32[4096,128]{1,0:T(8,128)S(1)}, f32[4096,128]{1,0:T(8,128)S(1)}, u32[]{:S(2)}, u32[]{:S(2)}) collective-permute-start(f32[4096,128]{1,0:T(8,128)S(1)} %constant_dynamic-update-slice_fusion.20.refs_0_), channel_id=1, source_target_pairs={{0,16},{16,0},{1,17},{17,1},{2,18},{18,2},{3,19},{19,3},{4,20},{20... | collective-permute-start | bytes 6291464 | tf_op jit(solution)/shard_map/ppermute | solution.py:408
  118.5 25.6 %collective-permute-start.34 = (f32[2048,128]{1,0:T(8,128)S(1)}, f32[2048,128]{1,0:T(8,128)S(1)}, u32[]{:S(2)}, u32[]{:S(2)}) collective-permute-start(f32[2048,128]{1,0:T(8,128)S(1)} %constant_dynamic-update-slice_fusion.10.refs_0_), channel_id=1, source_target_pairs={{0,2},{1,3},{2,0},{3,1},{4,6},{5,7},{6,4},{7,5},{8,10},{9,11},{10,... | collective-permute-start | bytes 3145736 | tf_op jit(solution)/shard_map/ppermute | solution.py:53
  120.0 25.6 %collective-permute-start.36 = (f32[2048,128]{1,0:T(8,128)S(1)}, f32[2048,128]{1,0:T(8,128)S(1)}, u32[]{:S(2)}, u32[]{:S(2)}) collective-permute-start(f32[2048,128]{1,0:T(8,128)S(1)} %constant_dynamic-update-slice_fusion.10.refs_0_), channel_id=1, source_target_pairs={{0,16},{16,0},{1,17},{17,1},{2,18},{18,2},{3,19},{19,3},{4,20},{20... | collective-permute-start | bytes 3145736 | tf_op jit(solution)/shard_map/ppermute | solution.py:408
  120.2 25.4 %collective-permute-start.35 = (f32[2048,128]{1,0:T(8,128)S(1)}, f32[2048,128]{1,0:T(8,128)S(1)}, u32[]{:S(2)}, u32[]{:S(2)}) collective-permute-start(f32[2048,128]{1,0:T(8,128)S(1)} %constant_dynamic-update-slice_fusion.15.refs_0_), channel_id=1, source_target_pairs={{0,1},{1,0},{2,3},{3,2},{4,5},{5,4},{6,7},{7,6},{8,9},{9,8},{10,11... | collective-permute-start | bytes 3145736 | tf_op jit(solution)/shard_map/ppermute | solution.py:53
  121.1 24.5 %collective-permute-start.37 = (f32[2048,128]{1,0:T(8,128)S(1)}, f32[2048,128]{1,0:T(8,128)S(1)}, u32[]{:S(2)}, u32[]{:S(2)}) collective-permute-start(f32[2048,128]{1,0:T(8,128)S(1)} %constant_dynamic-update-slice_fusion.15.refs_0_), channel_id=1, source_target_pairs={{0,16},{16,0},{1,17},{17,1},{2,18},{18,2},{3,19},{19,3},{4,20},{20... | collective-permute-start | bytes 3145736 | tf_op jit(solution)/shard_map/ppermute | solution.py:408
  127.5 18.1 %collective-permute-start.38 = (f32[512,512]{1,0:T(8,128)S(1)}, f32[512,512]{1,0:T(8,128)S(1)}, u32[]{:S(2)}, u32[]{:S(2)}) collective-permute-start(f32[512,512]{1,0:T(8,128)S(1)} %get-tuple-element.102), channel_id=1, source_target_pairs={{0,16},{16,0},{1,17},{17,1},{2,18},{18,2},{3,19},{19,3},{4,20},{20... | collective-permute-start | bytes 3145736 | tf_op jit(solution)/shard_map/ppermute | solution.py:408
  145.6 2.7 %collective-permute-start.39 = (f32[2048,128]{1,0:T(8,128)S(1)}, f32[2048,128]{1,0:T(8,128)S(1)}, u32[]{:S(2)}, u32[]{:S(2)}) collective-permute-start(f32[2048,128]{1,0:T(8,128)S(1)} %collective-permute-done.34.refs_2_), channel_id=1, source_target_pairs={{0,16},{16,0},{1,17},{17,1},{2,18},{18,2},{3,19},{19,3},{4,20},{20... | collective-permute-start | bytes 3145736 | tf_op jit(solution)/shard_map/ppermute | solution.py:408
  145.7 7.3 %collective-permute-start.40 = (f32[2048,128]{1,0:T(8,128)S(1)}, f32[2048,128]{1,0:T(8,128)S(1)}, u32[]{:S(2)}, u32[]{:S(2)}) collective-permute-start(f32[2048,128]{1,0:T(8,128)S(1)} %collective-permute-done.35.refs_2_), channel_id=1, source_target_pairs={{0,16},{16,0},{1,17},{17,1},{2,18},{18,2},{3,19},{19,3},{4,20},{20... | collective-permute-start | bytes 3145736 | tf_op jit(solution)/shard_map/ppermute | solution.py:408
  159.4 16.9 %collective-permute-start.41 = (f32[512,512]{1,0:T(8,128)}, f32[512,512]{1,0:T(8,128)}, u32[]{:S(2)}, u32[]{:S(2)}) collective-permute-start(f32[512,512]{1,0:T(8,128)} %get-tuple-element.115), channel_id=1, source_target_pairs={{0,16},{16,0},{1,17},{17,1},{2,18},{18,2},{3,19},{19,3},{4,20},{20... | collective-permute-start | bytes 3145736 | tf_op jit(solution)/shard_map/ppermute | solution.py:408
